TPU v7x, 128 devices: a whole 4x4x4 slice. The times are simulated.
128 devices in a mesh: row: 16 (over z_lo, y, core), col: 8 (over x, z_hi).
Axes of the slice: x: 4, y: 4, z: 4 (z_hi: 2, z_lo: 2; z = z_hi * 2 + z_lo), core: 2. Of those that a mesh axis runs over, the one named last changes fastest.
Arguments:
- queries: bfloat16 [8, 128, 4096], P(None, 'row', 'col'), may hold values from -13 to 13, as said below
- key_cache: bfloat16 [8, 65536, 1024], P(None, ('row', 'col')), may hold values from -13 to 13
- value_cache: bfloat16 [8, 65536, 1024], P(None, ('row', 'col')), may hold values from -6 to 6
- key_table: bfloat16 [1024, 1024], replicated, may hold values from -24 to 24
- value_table: bfloat16 [1024, 1024], replicated, may hold values from -6 to 6
- lengths: int32 [8], replicated, may hold values from 8192 to 65536
- token_ids: int32 [8, 128], P(None, 'row'), may hold values from 0 to 1023
Outputs:
- attended: bfloat16 [8, 128, 4096], P(None, 'row', 'col')
Inputs may be any that keep to these rules, and one draw needn't show every extreme that they name: `queries`: entries of the query array lie in the stated range.
All inputs are finite; a program needn't handle non-finite values.
Results may differ from a plain program's by a relative error of at most 0.006.
Values may be sent and summed in bfloat16 or wider, within the bound.
No kernel may reach another device: no remote copies, remote signals or barrier semaphores. Data moves between devices by JAX's collectives and lax.ppermute only.
A program may use at most 192 MiB of HBM per device.

v0:
```python
import jax
import jax.numpy as jnp
from jax import lax
from jax.sharding import PartitionSpec as P

HQ = 32
KH = 8
HD = 128


def laid_out(tiles, dim):
    lengths = list(tiles.shape[1:])
    lengths[dim] *= tiles.shape[0]
    return jnp.moveaxis(tiles, 0, dim).reshape(lengths)


def copy_for_each(array, axis):
    count = lax.axis_size(axis)
    return lax.all_to_all(
        jnp.broadcast_to(array[None], (count, *array.shape)), axis, 0, 0, tiled=True
    )


def gathered_copies(array, axis, dim):
    return laid_out(copy_for_each(array, axis), dim)


def cache_partials(whole, key_cache, value_cache, lengths, offset):
    users, beams, width = whole.shape
    positions = key_cache.shape[1]
    group = HQ // KH
    scale = HD ** (-0.5)

    def one_user(items):
        q_user, k_user, v_user, limit = items
        q_heads = q_user.reshape(beams, KH, group, HD)
        k_heads = k_user.reshape(positions, KH, HD)
        v_heads = v_user.reshape(positions, KH, HD)
        s = (
            jnp.einsum("wkgd,lkd->kwgl", q_heads, k_heads, preferred_element_type=jnp.float32)
            * scale
        )
        live = offset + jnp.arange(positions, dtype=jnp.int32) < limit
        s = jnp.where(live, s, -1e30)
        peak = jnp.max(s, axis=-1)
        weight = jnp.where(live, jnp.exp(s - peak[..., None]), 0.0)
        total = jnp.sum(weight, axis=-1)
        numer = jnp.einsum(
            "kwgl,lkd->wkgd",
            weight.astype(jnp.bfloat16),
            v_heads,
            preferred_element_type=jnp.float32,
        )
        peak = jnp.transpose(peak, (1, 0, 2)).reshape(beams, HQ)
        total = jnp.transpose(total, (1, 0, 2)).reshape(beams, HQ)
        return (numer.reshape(beams, width), peak, total)

    return lax.map(one_user, (whole, key_cache, value_cache, lengths))


def body(queries, key_cache, value_cache, key_table, value_table, lengths, token_ids):
    users, beam_part, width_part = queries.shape
    heads_part = width_part // HD
    scale = HD ** (-0.5)
    row_at = lax.axis_index("row")
    col_at = lax.axis_index("col")
    whole = gathered_copies(queries, "col", 2)
    whole = lax.all_gather(whole, "row", axis=1, tiled=True)
    offset = (row_at * lax.axis_size("col") + col_at) * key_cache.shape[1]
    numer_part, peak_part, total_part = cache_partials(
        whole, key_cache, value_cache, lengths, offset
    )
    peak_all = lax.pmax(peak_part, ("row", "col"))
    factor = jnp.exp(peak_part - peak_all)
    weighted = (numer_part.reshape(users, -1, HQ, HD) * factor[..., None]).reshape(
        users, -1, HQ * HD
    )
    mass = total_part * factor

    def local_part(array, per_head):
        picked = lax.dynamic_slice_in_dim(array, row_at * beam_part, beam_part, 1)
        return lax.dynamic_slice_in_dim(
            picked, col_at * heads_part * per_head, heads_part * per_head, 2
        )

    numer, total = lax.psum((weighted, mass), ("row", "col"))
    numer = local_part(numer, HD)
    total = local_part(total, 1)
    peak = local_part(peak_all, 1)
    codes = jnp.arange(key_table.shape[0], dtype=jnp.int32)
    onehot = (token_ids[..., None] == codes).astype(jnp.bfloat16)
    own_keys = jnp.einsum("uwv,vc->uwc", onehot, key_table, preferred_element_type=jnp.float32)
    own_values = jnp.einsum("uwv,vc->uwc", onehot, value_table, preferred_element_type=jnp.float32)
    group = HQ // KH
    own_keys = jnp.repeat(own_keys.reshape(users, beam_part, KH, HD), group, axis=2)
    own_values = jnp.repeat(own_values.reshape(users, beam_part, KH, HD), group, axis=2)
    own_keys = lax.dynamic_slice_in_dim(own_keys, col_at * heads_part, heads_part, 2)
    own_values = lax.dynamic_slice_in_dim(own_values, col_at * heads_part, heads_part, 2)
    q_local = queries.astype(jnp.float32).reshape(users, beam_part, heads_part, HD)
    own_score = jnp.sum(q_local * own_keys, axis=-1) * scale
    final_peak = jnp.maximum(peak, own_score)
    carried = jnp.exp(peak - final_peak)
    fresh = jnp.exp(own_score - final_peak)
    numer = (
        numer.reshape(users, beam_part, heads_part, HD) * carried[..., None]
        + fresh[..., None] * own_values
    )
    total = total * carried + fresh
    result = numer / total[..., None]
    return result.reshape(users, beam_part, width_part).astype(jnp.bfloat16)


def solution(mesh):
    return jax.shard_map(
        body,
        mesh=mesh,
        in_specs=(
            P(None, "row", "col"),
            P(None, ("row", "col"), None),
            P(None, ("row", "col"), None),
            P(),
            P(),
            P(),
            P(None, "row"),
        ),
        out_specs=P(None, "row", "col"),
        check_vma=False,
    )
```

profile of v0, /device:TPU:1, one launch (start us, length us, event | category | flops | bytes accessed | tf_op | source)
XLA Modules:
  0.0 743.7 jit_solution(7798961752427165654)
XLA Ops:
  7.6 17.5 %all_to_all.5 = bf16[8,8,8,512]{3,2,1,0:T(8,128)(2,1)S(1)} all-to-all(bf16[8,8,8,512]{3,2,1,0:T(8,128)(2,1)S(1)} %broadcast_in_dim.46), channel_id=1, replica_groups=mesh['row'=16,'col'=8] {'col'}, dimensions={0} | all-to-all | bytes 1048576 | tf_op jit(solution)/shard_map/all_to_all | solution.py:19
  26.6 52.4 %all-gather.2.cloned.1.call-done = bf16[8,128,4096]{2,0,1:T(8,128)(2,1)} async-done(((bf16[8,8,4096]{2,0,1:T(8,128)(2,1)}), bf16[8,128,4096]{2,0,1:T(8,128)(2,1)}) %all-gather.2.cloned.1.call-update) | async-done | bytes 8388624 | tf_op jit(solution)/shard_map/all_gather | solution.py:68
  79.0 12.5 %copy.35 = bf16[8,128,4096]{1,2,0:T(8,128)(2,1)} copy(bf16[8,128,4096]{2,0,1:T(8,128)(2,1)} %all-gather.2.cloned.1.call-done) | data formatting | bytes 16777216 | tf_op jit(solution)/shard_map/while | solution.py:58
  91.5 240.9 %while.14 = (s32[]{:T(128)}, f32[8,128,4096]{2,1,0:T(8,128)}, f32[8,128,32]{1,2,0:T(8,128)}, f32[8,128,32]{1,2,0:T(8,128)S(1)}, bf16[8,512,1024]{2,1,0:T(8,128)(...) while((s32[]{:T(128)}, f32[8,128,4096]{2,1,0:T(8,128)}, ...), condition=%wide.region_3.4_spmd, body=%wide.region_0.3_spmd.sunk | while | flops 1100997632 | bytes 82971808 | solution.py:58
  99.6 3.2 copy-done.1
  108.4 7.2 fusion.46
  129.7 3.2 copy-done.1
  138.5 7.2 fusion.46
  159.8 3.2 copy-done.1
  168.6 7.2 fusion.46
  189.9 3.2 copy-done.1
  198.7 7.2 fusion.46
  220.0 3.2 copy-done.1
  228.8 7.2 fusion.46
  258.9 7.2 fusion.46
  280.3 3.2 copy-done.1
  289.0 7.2 fusion.46
  310.4 3.2 copy-done.1
  319.2 7.2 fusion.46
  332.5 140.7 %all-reduce.4.cloned.1.call-done = f32[8,128,32]{1,2,0:T(8,128)} async-done(((f32[8,128,32]{1,2,0:T(8,128)}), f32[8,128,32]{1,2,0:T(8,128)}) %all-reduce.4.cloned.1.call-update) | async-done | bytes 131088 | tf_op jit(solution)/shard_map/pmax | solution.py:73
  475.0 8.4 %mul.66 = f32[8,128,32,128]{3,2,1,0:T(8,128)} broadcast(f32[8,128,32]{2,1,0:T(8,128)S(1)} %copy.37), dimensions={0,1,2} | broadcast | bytes 16908288 | tf_op jit(solution)/shard_map/mul | solution.py:75
  483.4 18.2 %mul.67 = f32[8,128,4096]{2,1,0:T(8,128)} reshape(f32[8,128,32,128]{3,2,1,0:T(8,128)} %mul.66) | data formatting | bytes 33554432 | tf_op jit(solution)/shard_map/mul | solution.py:75
  501.6 17.8 %mul.68 = f32[8,128,4096]{2,1,0:T(8,128)} multiply(f32[8,128,4096]{2,1,0:T(8,128)} %get-tuple-element.54, f32[8,128,4096]{2,1,0:T(8,128)} %mul.67) | non-fusion elementwise | flops 4194304 | bytes 50331648 | tf_op jit(solution)/shard_map/mul | solution.py:75
  523.0 211.3 %all-reduce.6.cloned.1.call-done = (f32[8,128,32]{1,2,0:T(8,128)}, f32[8,128,4096]{2,1,0:T(8,128)}) async-done(((f32[8,128,32]{1,2,0:T(8,128)}, f32[8,128,4096]{2,1,0:T(8,128)}), (f32[8,128,32]{1,2,0:T(8,128)}, f32[8,128,4096]{2,1,0:T(8,128)})) %all-reduce.6.cloned.1.call-update) | async-done | bytes 16908304 | tf_op jit(solution)/shard_map/psum | solution.py:86
  (134 shorter events, 171.3 us)
Async XLA Ops:
  6.5 512.9 %copy-start = (bf16[1024,1024]{1,0:T(8,128)(2,1)S(1)}, bf16[1024,1024]{1,0:T(8,128)(2,1)}, u32[]{:S(2)}) copy-start(bf16[1024,1024]{1,0:T(8,128)(2,1)} %param.12) | copy-start | bytes 6291460
  6.5 72.5 %all-gather.2.cloned.1.call-start = ((), (), s32[]{:S(2)}) async-start(), calls=%async_computation.1 | async-start | bytes 8912896 | tf_op jit(solution)/shard_map/all_gather | solution.py:68
  26.5 446.7 %all-reduce.4.cloned.1.call-start = ((), (), s32[]{:S(2)}) async-start(), calls=%async_computation.2 | async-start | bytes 262144 | tf_op jit(solution)/shard_map/pmax | solution.py:73
  26.6 64.9 %copy-start.4 = (s32[8]{0:T(128)S(1)}, s32[8]{0:T(128)}, u32[]{:S(2)}) copy-start(s32[8]{0:T(128)} %param.14) | copy-start | bytes 100
  99.6 3.2 copy-start.1
  129.7 3.2 copy-start.1
  159.8 3.2 copy-start.1
  189.9 3.2 copy-start.1
  220.0 3.2 copy-start.1
  250.1 3.2 copy-start.1
  280.2 3.2 copy-start.1
  310.4 3.2 copy-start.1
  332.4 401.9 %all-reduce.6.cloned.1.call-start = ((), (), s32[]{:S(2)}) async-start(), calls=%async_computation.3 | async-start | bytes 33816576 | tf_op jit(solution)/shard_map/psum | solution.py:86
  519.4 0.7 copy-start.3
  519.4 1.3 copy-start.2
Sparse Core Ops, SparseCore 0:
  26.6 52.3 all-gather.1
  332.5 140.5 all-reduce.3
  519.6 214.6 all-reduce.5
where the time goes:
time: 747 us; the launch traced here: 744 us
  waiting for transfers between devices  404 us (54%)
  local copies, waits for them, and re-layouts  179 us (24%)
  matrix products  82.9 us (11%)
  other arithmetic  46.2 us (6%)
  blocking collectives  17.5 us (2%)
  between operations  13.2 us (2%)
    psum x1, waiting for transfers between devices, body(): numer, total = lax.psum((weighted, mass), ('row', 'col'))  211 us
    pmax x1, waiting for transfers between devices, body(): peak_all = lax.pmax(peak_part, ('row', 'col'))  141 us
    dynamic_slice x48, local copies, waits for them, and re-layouts, cache_partials(): return lax.map(one_user, (whole, key_cache, value_cache, lengths))  57.7 us
    dot_general x8, matrix products, one_user(): jnp.einsum('kwgl,lkd->wkgd', weight.astype(jnp.bfloat16), v_heads, prefer...  57.5 us
    dynamic_update_slice x24, local copies, waits for them, and re-layouts, cache_partials(): return lax.map(one_user, (whole, key_cache, value_cache, lengths))  53.1 us
    all_gather x1, waiting for transfers between devices, body(): whole = lax.all_gather(whole, 'row', axis=1, tiled=True)  52.4 us
    mul x2, local copies, waits for them, and re-layouts, body(): numer_part.reshape(users, -1, HQ, HD) * factor[..., None]  26.6 us
    while x16, local copies, waits for them, and re-layouts  25.8 us
  transfers between devices with their start and end apart: 3, of which 3 were waited for; matrix products, arithmetic and copies ran while one was open for 0% of the time, Pallas kernels for 0%

commit v1 on v0

v1 whole, which is shorter than its diff:
```python
import functools

import jax
import jax.numpy as jnp
import numpy as np
from jax import lax
from jax.experimental import pallas as pl
from jax.experimental.pallas import tpu as pltpu
from jax.sharding import Mesh
from jax.sharding import PartitionSpec as P

KH = 8
GROUP = 4
HD = 128
LOG2E = 1.4426950408889634
SCALE = HD**-0.5
FINE = ("zl", "y", "c", "x", "zh")
SIZES = (2, 4, 2, 4, 2)
CHIPS = ("zl", "y", "x", "zh")
DEAD = -(2.0**100)


def partial_kernel(info, q_ref, k0_ref, k1_ref, v0_ref, v1_ref, o_ref):
    users = pl.num_programs(1)
    u = pl.program_id(1)
    length = k0_ref.shape[1]
    rows = GROUP * 16
    at = lax.broadcasted_iota(jnp.int32, (1, length), 1)
    bias0 = jnp.where(at < info[1 + u], 0.0, DEAD)
    bias1 = jnp.where(at < info[1 + users + u], 0.0, DEAD)
    k0 = k0_ref[0]
    k1 = k1_ref[0]
    v0 = v0_ref[0]
    v1 = v1_ref[0]
    lane = lax.broadcasted_iota(jnp.int32, (16, HD), 1)
    per = 2
    dims = (((1,), (1,)), ((), ()))

    @pl.when(u == 0)
    def _():
        o_ref[:, 0, users * rows :, :] = jnp.zeros((o_ref.shape[0], 16, HD), jnp.bfloat16)

    for i in range(0, q_ref.shape[0], per):
        q = q_ref[i : i + per, 0].reshape(per * rows, HD)
        s0 = lax.dot_general(q, k0, dims, preferred_element_type=jnp.float32)
        s1 = lax.dot_general(q, k1, dims, preferred_element_type=jnp.float32)
        s0 = s0 * (SCALE * LOG2E) + bias0
        s1 = s1 * (SCALE * LOG2E) + bias1
        peak = jnp.maximum(
            jnp.max(s0, axis=1, keepdims=True), jnp.max(s1, axis=1, keepdims=True)
        )
        peak = peak.astype(jnp.bfloat16).astype(jnp.float32)
        w0 = jnp.exp2(s0 - peak)
        w1 = jnp.exp2(s1 - peak)
        total = jnp.sum(w0, axis=1, keepdims=True) + jnp.sum(w1, axis=1, keepdims=True)
        numer = jnp.dot(
            w0.astype(jnp.bfloat16), v0, preferred_element_type=jnp.float32
        ) + jnp.dot(w1.astype(jnp.bfloat16), v1, preferred_element_type=jnp.float32)
        numer = (numer * (1.0 / total)).astype(jnp.bfloat16)
        o_ref[i : i + per, 0, pl.ds(pl.multiple_of(u * rows, rows), rows), :] = (
            numer.reshape(per, rows, HD)
        )
        high = total.astype(jnp.bfloat16).astype(jnp.float32)
        low = total - high
        for d in range(per):
            held = o_ref[i + d, 0, users * rows :, :].astype(jnp.float32)
            for g in range(GROUP):
                part = slice(d * rows + g * 16, d * rows + g * 16 + 16)
                base = u * 16 + g
                held = jnp.where(lane == base, peak[part], held)
                held = jnp.where(lane == base + 4, high[part], held)
                held = jnp.where(lane == base + 8, low[part], held)
            o_ref[i + d, 0, users * rows :, :] = held.astype(jnp.bfloat16)


def partials(info, q, k0, k1, v0, v1):
    lead, heads, qrows, _ = q.shape
    rows = GROUP * 16
    users = qrows // rows
    length = k0.shape[1]

    def mine(j, u, info):
        return (info[0] + u, 0, j)

    def other(j, u, info):
        return (u, 0, j)

    cache = (1, length, HD)
    return pl.pallas_call(
        partial_kernel,
        grid_spec=pltpu.PrefetchScalarGridSpec(
            num_scalar_prefetch=1,
            grid=(heads, users),
            in_specs=[
                pl.BlockSpec((lead, 1, rows, HD), lambda j, u, info: (0, j, u, 0)),
                pl.BlockSpec(cache, mine),
                pl.BlockSpec(cache, other),
                pl.BlockSpec(cache, mine),
                pl.BlockSpec(cache, other),
            ],
            out_specs=pl.BlockSpec(
                (lead, 1, qrows + 16, HD), lambda j, u, info: (0, j, 0, 0)
            ),
        ),
        out_shape=jax.ShapeDtypeStruct((lead, heads, qrows + 16, HD), jnp.bfloat16),
        compiler_params=pltpu.CompilerParams(
            dimension_semantics=("arbitrary", "arbitrary"),
            vmem_limit_bytes=40 << 20,
        ),
        cost_estimate=pl.CostEstimate(
            flops=8 * heads * lead * qrows * HD * length,
            bytes_accessed=8 * users * length * heads * HD + 4 * q.size,
            transcendentals=2 * heads * lead * qrows * length,
        ),
    )(info, q, k0, k1, v0, v1)


def combine_kernel(x_ref, own_ref, value_ref, o_ref, w_ref):
    chips = x_ref.shape[0]
    users = value_ref.shape[0]
    rows = GROUP * 16
    base = users * rows
    own = own_ref[...]

    def top(i, peak):
        return jnp.maximum(peak, x_ref[i, base:, :].astype(jnp.float32))

    peak = lax.fori_loop(0, chips, top, own, unroll=8)

    def weigh(i, total):
        held = x_ref[i, base:, :].astype(jnp.float32)
        mass = pltpu.roll(held, HD - 4, 1) + pltpu.roll(held, HD - 8, 1)
        weight = mass * jnp.exp2(held - peak)
        w_ref[i] = weight
        return total + weight

    fresh = jnp.exp2(own - peak)
    total = lax.fori_loop(0, chips, weigh, fresh, unroll=8)
    inverse = 1.0 / total
    fresh = fresh * inverse
    for u in range(users):
        acc = [
            fresh[:, u * 16 + g : u * 16 + g + 1] * value_ref[u] for g in range(GROUP)
        ]

        def add(i, acc):
            weight = w_ref[i] * inverse
            return [
                acc[g]
                + weight[:, u * 16 + g : u * 16 + g + 1]
                * x_ref[i, u * rows + g * 16 : u * rows + g * 16 + 16, :].astype(jnp.float32)
                for g in range(GROUP)
            ]

        acc = lax.fori_loop(0, chips, add, acc, unroll=4)
        for g in range(GROUP):
            o_ref[u, g] = acc[g].astype(jnp.bfloat16)


def combined(x, own, value):
    users = value.shape[0]
    return pl.pallas_call(
        combine_kernel,
        out_shape=jax.ShapeDtypeStruct((users, GROUP, 16, HD), jnp.bfloat16),
        scratch_shapes=[pltpu.VMEM((x.shape[0], 16, HD), jnp.float32)],
        compiler_params=pltpu.CompilerParams(vmem_limit_bytes=40 << 20),
        cost_estimate=pl.CostEstimate(
            flops=2 * x.size, bytes_accessed=2 * x.size, transcendentals=0
        ),
    )(x, own, value)


def body(queries, key_cache, value_cache, key_table, value_table, lengths, token_ids):
    users, beams, _ = queries.shape
    half = users // 2
    length = key_cache.shape[1]
    c = lax.axis_index("c")
    row = (lax.axis_index("zl") * SIZES[1] + lax.axis_index("y")) * 2 + c
    col = lax.axis_index("x") * SIZES[4] + lax.axis_index("zh")
    swap = functools.partial(lax.ppermute, axis_name="c", perm=[(0, 1), (1, 0)])

    def halves(array):
        return (
            lax.dynamic_slice_in_dim(array, c * half, half, 0),
            lax.dynamic_slice_in_dim(array, (1 - c) * half, half, 0),
        )

    q = queries.reshape(users, beams, GROUP, HD).transpose(0, 2, 1, 3)
    q_mine, q_give = halves(q)
    q_chip = jnp.concatenate([q_mine, swap(q_give)], axis=2)
    t_mine, t_give = halves(token_ids)
    tokens = jnp.concatenate([t_mine, swap(t_give)], axis=1)
    k_other = swap(halves(key_cache)[1])
    v_other = swap(halves(value_cache)[1])

    chips = SIZES[0] * SIZES[1] * SIZES[3] * SIZES[4]
    packed = q_chip.reshape(1, half * GROUP * 2 * beams, HD)
    everyone = lax.all_to_all(
        jnp.broadcast_to(packed, (chips, *packed.shape[1:])), CHIPS, 0, 0, tiled=True
    )
    everyone = everyone.reshape(chips // KH, KH, *packed.shape[1:])

    limits = lax.dynamic_slice_in_dim(lengths, c * half, half, 0)
    offset = (row * KH + col) * length
    other = ((row + 1 - 2 * c) * KH + col) * length
    info = jnp.concatenate([(c * half)[None], limits - offset, limits - other]).astype(jnp.int32)
    sent = partials(info, everyone, key_cache, k_other, value_cache, v_other)
    sent = sent.reshape(chips, *sent.shape[2:])
    arrived = lax.all_to_all(sent, CHIPS, 0, 0, tiled=True)

    codes = jnp.arange(key_table.shape[0], dtype=jnp.int32)
    onehot = (tokens[..., None] == codes).astype(jnp.bfloat16)
    keys = lax.dynamic_slice_in_dim(key_table, col * HD, HD, 1)
    values = lax.dynamic_slice_in_dim(value_table, col * HD, HD, 1)
    own_keys = jnp.einsum("uwv,vc->uwc", onehot, keys, preferred_element_type=jnp.float32)
    own_values = jnp.einsum("uwv,vc->uwc", onehot, values, preferred_element_type=jnp.float32)
    own = jnp.sum(q_chip.astype(jnp.float32) * own_keys[:, None], axis=-1) * (SCALE * LOG2E)
    own = jnp.pad(own.transpose(2, 0, 1), ((0, 0), (0, 0), (0, 16 - GROUP)))
    own = jnp.pad(own.reshape(2 * beams, half * 16), ((0, 0), (0, HD - half * 16)))

    result = combined(arrived, own, own_values)
    keep, give = result[:, :, :beams], result[:, :, beams:]
    got = swap(give)
    whole = jnp.where(
        c == 0, jnp.concatenate([keep, got]), jnp.concatenate([got, keep])
    )
    return whole.transpose(0, 2, 1, 3).reshape(users, beams, GROUP * HD)


def solution(mesh):
    fine = Mesh(np.asarray(mesh.devices).reshape(SIZES), FINE)
    row, col = ("zl", "y", "c"), ("x", "zh")
    return jax.shard_map(
        body,
        mesh=fine,
        in_specs=(
            P(None, row, col),
            P(None, row + col, None),
            P(None, row + col, None),
            P(),
            P(),
            P(),
            P(None, row),
        ),
        out_specs=P(None, row, col),
        check_vma=False,
    )
```

time: 747 us -> 217 us (0.29)
  waiting for transfers between devices: 404 us -> 103 us
  local copies, waits for them, and re-layouts: 179 us -> 11.6 us
  matrix products: 82.9 us -> 1.43 us
  Pallas kernels: 0 us -> 68.2 us
  other arithmetic: 46.2 us -> 1.01 us
  starting transfers between devices: 0.09 us -> 29 us
  blocking collectives: 17.5 us -> 0 us
  between operations: 13.2 us -> 0.12 us
    psum x1 -> x0, waiting for transfers between devices: 211 us -> none  [body(): numer, total = lax.psum((weighted, mass), ('row', 'col'))]
    pmax x1 -> x0, waiting for transfers between devices: 141 us -> none  [body(): peak_all = lax.pmax(peak_part, ('row', 'col'))]
    all_to_all x0 -> x2, waiting for transfers between devices: none -> 101 us  [the longest x1 54.4 us: body(): lax.all_to_all(jnp.broadcast_to(packed, (chips, *packed.shape[1:])), CHIP...]
    dot_general x18 -> x2, matrix products: 82.9 us -> 1.43 us  [the longest x1 1.19 us: body(): jnp.einsum('uwv,vc->uwc', onehot, keys, preferred_element_type=jnp.float32)]
    pallas_call x0 -> x2, Pallas kernels: none -> 68.2 us  [the longest x1 57.2 us: partials(): pl.pallas_call(partial_kernel, grid_spec=pltpu.PrefetchScalarGridSpec(num...]
    dynamic_update_slice x24 -> x0, local copies, waits for them, and re-layouts: 53.1 us -> none  [cache_partials(): return lax.map(one_user, (whole, key_cache, value_cache, lengths))]
    all_gather x1 -> x0, waiting for transfers between devices: 52.4 us -> none  [body(): whole = lax.all_gather(whole, 'row', axis=1, tiled=True)]
    dynamic_slice x48 -> x4, local copies, waits for them, and re-layouts: 57.7 us -> 8.49 us  [the longest x2 7.55 us: halves(): lax.dynamic_slice_in_dim(array, (1 - c) * half, half, 0)]
  transfers between devices with their start and end apart: 3 -> 7, of which waited for: 3 -> 4; matrix products, arithmetic and copies ran while one was open for 0% -> 6% of each run, Pallas kernels for 0% -> 0%
where the time goes in v1:
time: 217 us; the launch traced here: 215 us
  waiting for transfers between devices  103 us (47%)
  Pallas kernels  68.2 us (31%)
  starting transfers between devices  29 us (13%)
  local copies, waits for them, and re-layouts  11.6 us (5%)
    pallas_call x1, Pallas kernels, partials(): pl.pallas_call(partial_kernel, grid_spec=pltpu.PrefetchScalarGridSpec(num...  57.2 us
    all_to_all x1, waiting for transfers between devices, body(): lax.all_to_all(jnp.broadcast_to(packed, (chips, *packed.shape[1:])), CHIP...  54.4 us
    all_to_all x1, waiting for transfers between devices, body(): arrived = lax.all_to_all(sent, CHIPS, 0, 0, tiled=True)  47 us
    all_to_all x1, starting transfers between devices, body(): lax.all_to_all(jnp.broadcast_to(packed, (chips, *packed.shape[1:])), CHIP...  11.6 us
    pallas_call x1, Pallas kernels, combined(): pl.pallas_call(combine_kernel, out_shape=jax.ShapeDtypeStruct((users, GRO...  11 us
    all_to_all x1, starting transfers between devices, body(): arrived = lax.all_to_all(sent, CHIPS, 0, 0, tiled=True)  9.68 us
    dynamic_slice x2, local copies, waits for them, and re-layouts, halves(): lax.dynamic_slice_in_dim(array, (1 - c) * half, half, 0)  7.55 us
  transfers between devices with their start and end apart: 7, of which 4 were waited for; matrix products, arithmetic and copies ran while one was open for 6% of the time, Pallas kernels for 0%

profile of v1, /device:TPU:1, one launch (start us, length us, event | category | flops | bytes accessed | tf_op | source)
XLA Modules:
  0.0 214.5 jit_solution(11138826898552458050)
XLA Ops:
  0.0 0.9 dynamic-slice_bitcast_fusion.1
  0.9 1.5 collective-permute-start
  2.4 5.2 %constant_dynamic-slice_fusion.2 = bf16[4,512,1024]{2,1,0:T(8,128)(2,1)} fusion(bf16[8,512,1024]{2,1,0:T(8,128)(2,1)} %v0_ref.1, s32[]{:T(128)S(6)} %select_n.25), kind=kLoop, calls=%fused_computation.21 | loop fusion | bytes 8388612 | tf_op jit(solution)/shard_map/dynamic_slice | solution.py:185
  7.6 2.4 %constant_dynamic-slice_fusion.3 = bf16[4,512,1024]{2,1,0:T(8,128)(2,1)} fusion(bf16[8,512,1024]{2,1,0:T(8,128)(2,1)S(1)} %copy-done.1, s32[]{:T(128)S(6)} %select_n.25), kind=kLoop, calls=%fused_computation.22 | loop fusion | bytes 8388612 | tf_op jit(solution)/shard_map/dynamic_slice | solution.py:185
  10.0 0.9 collective-permute-start.1
  10.9 3.0 %broadcast_in_dim.15 = bf16[64,256,128]{2,1,0:T(8,128)(2,1)} broadcast(bf16[256,128]{1,0:T(8,128)(2,1)S(1)} %bitcast.23), dimensions={1,2} | broadcast | bytes 4259840 | tf_op jit(solution)/shard_map/broadcast_in_dim | solution.py:199
  13.9 11.6 %all-to-all-start = ((bf16[64,256,128]{2,1,0:T(8,128)(2,1)}), bf16[64,256,128]{2,1,0:T(8,128)(2,1)}, u32[]{:S(2)}, u32[]{:S(2)}) async-start(bf16[64,256,128]{2,1,0:T(8,128)(2,1)} %broadcast_in_dim.15), calls=%async_computation | async-start | bytes 8388608 | tf_op jit(solution)/shard_map/all_to_all | solution.py:198
  25.6 0.1 broadcast_subtract_fusion.1
  25.6 0.1 pad_add_fusion.1.info
  25.7 54.4 %all-to-all-done = bf16[64,256,128]{2,1,0:T(8,128)(2,1)} async-done(((bf16[64,256,128]{2,1,0:T(8,128)(2,1)}), bf16[64,256,128]{2,1,0:T(8,128)(2,1)}, u32[]{:S(2)}, u32[]{:S(2)}) %all-to-all-start) | async-done | bytes 4194336 | tf_op jit(solution)/shard_map/all_to_all | solution.py:198
  80.1 57.2 %shard_map.73 = bf16[8,8,272,128]{3,2,1,0:T(8,128)(2,1)} custom-call(s32[9]{0:T(128)S(1)} %pad_add_fusion.1.info, bf16[8,8,256,128]{3,2,1,0:T(8,128)(2,1)} %bitcast.5.q_ref, bf16[8,512,1024]{2,1,0:T(8,128)(2,1)} %k0_ref.1, bf16[4,512,1024]{2,1,0:T(8,128)(2,1)} %collective-permute-done.1.k1_ref, bf16[8,512,1024]{2,1,0:T(8,128)(2,1)} %v0_ref.1, ...), custom_call_target="tpu_custom_call" | custom-call | flops 8589934592 | bytes 25165824 | tf_op jit(solution)/shard_map/pallas_call | solution.py:89
  137.3 9.7 %all-to-all-start.1 = ((bf16[64,272,128]{2,1,0:T(8,128)(2,1)}), bf16[64,272,128]{2,1,0:T(8,128)(2,1)}, u32[]{:S(2)}, u32[]{:S(2)}) async-start(bf16[64,272,128]{2,1,0:T(8,128)(2,1)} %bitcast.22), calls=%async_computation.1 | async-start | bytes 8912896 | tf_op jit(solution)/shard_map/all_to_all | solution.py:209
  147.0 1.8 collective-permute-start.3
  148.8 0.8 collective-permute-done.3
  149.6 0.1 pad_add_fusion
  149.7 0.2 fusion.value_ref
  150.0 1.2 fusion.2
  151.1 0.1 multiply_reduce_fusion
  151.3 0.1 copy.9
  151.4 47.0 %all-to-all-done.1.x_ref = bf16[64,272,128]{2,1,0:T(8,128)(2,1)} async-done(((bf16[64,272,128]{2,1,0:T(8,128)(2,1)}), bf16[64,272,128]{2,1,0:T(8,128)(2,1)}, u32[]{:S(2)}, u32[]{:S(2)}) %all-to-all-start.1) | async-done | bytes 4456480 | tf_op jit(solution)/shard_map/all_to_all | solution.py:209
  198.4 11.0 %shard_map.74 = bf16[4,4,16,128]{3,2,1,0:T(8,128)(2,1)S(1)} custom-call(bf16[64,272,128]{2,1,0:T(8,128)(2,1)} %all-to-all-done.1.x_ref, f32[16,128]{1,0:T(8,128)S(1)} %pad.9.own_ref, f32[4,16,128]{2,1,0:T(8,128)S(1)} %fusion.value_ref), custom_call_target="tpu_custom_call" | custom-call | flops 4456448 | bytes 4456448 | tf_op jit(solution)/shard_map/pallas_call | solution.py:162
  209.5 3.5 %collective-permute-start.4 = (bf16[4,4,8,128]{3,2,1,0:T(8,128)(2,1)S(1)}, bf16[4,4,8,128]{3,2,1,0:T(8,128)(2,1)S(1)}, u32[]{:S(2)}, u32[]{:S(2)}) collective-permute-start(bf16[4,4,8,128]{3,2,1,0:T(8,128)(2,1)S(1)} %get-tuple-element.6), channel_id=1, source_target_pairs={{0,8},{8,0},{1,9},{9,1},{2,10},{10,2},{3,11},{11,3},{4,12},{12,4},... | collective-permute-start | bytes 98312 | tf_op jit(solution)/shard_map/ppermute | solution.py:223
  213.0 0.9 collective-permute-done.4
  213.9 0.6 fusion.8
  (18 shorter events, 0.1 us)
Async XLA Ops:
  0.0 149.7 %copy-start = (bf16[1024,1024]{1,0:T(8,128)(2,1)S(1)}, bf16[1024,1024]{1,0:T(8,128)(2,1)}, u32[]{:S(2)}) copy-start(bf16[1024,1024]{1,0:T(8,128)(2,1)} %param.11) | copy-start | bytes 6291460
  0.9 6.7 %copy-start.1 = (bf16[8,512,1024]{2,1,0:T(8,128)(2,1)S(1)}, bf16[8,512,1024]{2,1,0:T(8,128)(2,1)}, u32[]{:S(2)}) copy-start(bf16[8,512,1024]{2,1,0:T(8,128)(2,1)} %k0_ref.1) | copy-start | bytes 25165828
  0.9 10.0 %collective-permute-start = (bf16[4,4,8,128]{3,2,1,0:T(8,128)(2,1)S(1)}, bf16[4,4,8,128]{3,2,1,0:T(8,128)(2,1)S(1)}, u32[]{:S(2)}, u32[]{:S(2)}) collective-permute-start(bf16[4,4,8,128]{3,2,1,0:T(8,128)(2,1)S(1)} %get-tuple-element.8), channel_id=1, source_target_pairs={{0,8},{8,0},{1,9},{9,1},{2,10},{10,2},{3,11},{11,3},{4,12},{12,4},... | collective-permute-start | bytes 98312 | tf_op jit(solution)/shard_map/ppermute | solution.py:190
  7.6 72.5 %collective-permute-start.2 = (bf16[4,512,1024]{2,1,0:T(8,128)(2,1)}, bf16[4,512,1024]{2,1,0:T(8,128)(2,1)}, u32[]{:S(2)}, u32[]{:S(2)}) collective-permute-start(bf16[4,512,1024]{2,1,0:T(8,128)(2,1)} %constant_dynamic-slice_fusion.2), channel_id=1, source_target_pairs={{0,8},{8,0},{1,9},{9,1},{2,10},{10,2},{3,11},{11,3},{4,12},{12,4},... | collective-permute-start | bytes 12582920 | tf_op jit(solution)/shard_map/ppermute | solution.py:194
  10.0 70.2 %collective-permute-start.1 = (bf16[4,512,1024]{2,1,0:T(8,128)(2,1)}, bf16[4,512,1024]{2,1,0:T(8,128)(2,1)}, u32[]{:S(2)}, u32[]{:S(2)}) collective-permute-start(bf16[4,512,1024]{2,1,0:T(8,128)(2,1)} %constant_dynamic-slice_fusion.3), channel_id=1, source_target_pairs={{0,8},{8,0},{1,9},{9,1},{2,10},{10,2},{3,11},{11,3},{4,12},{12,4},... | collective-permute-start | bytes 12582920 | tf_op jit(solution)/shard_map/ppermute | solution.py:193
  13.9 11.6 %copy-start.3 = (s32[8]{0:T(128)S(1)}, s32[8]{0:T(128)}, u32[]{:S(2)}) copy-start(s32[8]{0:T(128)} %param.12) | copy-start | bytes 100
  13.9 66.2 %all-to-all-start = ((bf16[64,256,128]{2,1,0:T(8,128)(2,1)}), bf16[64,256,128]{2,1,0:T(8,128)(2,1)}, u32[]{:S(2)}, u32[]{:S(2)}) async-start(bf16[64,256,128]{2,1,0:T(8,128)(2,1)} %broadcast_in_dim.15), calls=%async_computation | async-start | bytes 8388608 | tf_op jit(solution)/shard_map/all_to_all | solution.py:198
  137.3 9.7 %copy-start.2 = (s32[8,8]{1,0:T(8,128)S(1)}, s32[8,8]{1,0:T(8,128)}, u32[]{:S(2)}) copy-start(s32[8,8]{1,0:T(8,128)} %param.13) | copy-start | bytes 772
  137.3 61.1 %all-to-all-start.1 = ((bf16[64,272,128]{2,1,0:T(8,128)(2,1)}), bf16[64,272,128]{2,1,0:T(8,128)(2,1)}, u32[]{:S(2)}, u32[]{:S(2)}) async-start(bf16[64,272,128]{2,1,0:T(8,128)(2,1)} %bitcast.22), calls=%async_computation.1 | async-start | bytes 8912896 | tf_op jit(solution)/shard_map/all_to_all | solution.py:209
  147.0 2.6 %collective-permute-start.3 = (s32[4,8]{1,0:T(4,128)S(1)}, s32[4,8]{1,0:T(4,128)S(1)}, u32[]{:S(2)}, u32[]{:S(2)}) collective-permute-start(s32[4,8]{1,0:T(4,128)S(1)} %get-tuple-element.10), channel_id=1, source_target_pairs={{0,8},{8,0},{1,9},{9,1},{2,10},{10,2},{3,11},{11,3},{4,12},{12,4},... | collective-permute-start | bytes 392 | tf_op jit(solution)/shard_map/ppermute | solution.py:192
  209.5 4.4 %collective-permute-start.4 = (bf16[4,4,8,128]{3,2,1,0:T(8,128)(2,1)S(1)}, bf16[4,4,8,128]{3,2,1,0:T(8,128)(2,1)S(1)}, u32[]{:S(2)}, u32[]{:S(2)}) collective-permute-start(bf16[4,4,8,128]{3,2,1,0:T(8,128)(2,1)S(1)} %get-tuple-element.6), channel_id=1, source_target_pairs={{0,8},{8,0},{1,9},{9,1},{2,10},{10,2},{3,11},{11,3},{4,12},{12,4},... | collective-permute-start | bytes 98312 | tf_op jit(solution)/shard_map/ppermute | solution.py:223

commit v2 on v1

v2 whole, which is shorter than its diff:
```python
import functools

import jax
import jax.numpy as jnp
import numpy as np
from jax import lax
from jax.experimental import pallas as pl
from jax.experimental.pallas import tpu as pltpu
from jax.sharding import Mesh
from jax.sharding import PartitionSpec as P

KH = 8
GROUP = 4
HD = 128
HALF = HD // 2
SCALE2 = HD**-0.5 * 1.4426950408889634
FINE = ("zl", "y", "c", "x", "zh")
SIZES = (2, 4, 2, 4, 2)
CHIPS = ("zl", "y", "x", "zh")
DEAD = -(2.0**100)
ROWS = 64
META = 8
CHUNKS = 2
PARTS = 2


def packed_tiles(first, second):
    low = lax.broadcasted_iota(jnp.int32, (first.shape[0], HD), 1) < ROWS
    out = []
    for k in range(first.shape[1] // HD):
        a = first[:, k * HD : (k + 1) * HD]
        b = second[:, k * HD : (k + 1) * HD]
        crossed = pltpu.roll(jnp.where(low, b, a), ROWS, 1)
        out.append(jnp.where(low, a, crossed))
        out.append(jnp.where(low, crossed, b))
    return out


def partial_kernel(info, q_ref, k0_ref, k1_ref, v0_ref, v1_ref, o_ref, m_ref):
    users = pl.num_programs(0)
    u = pl.program_id(0)
    part = pl.program_id(1)
    length = k0_ref.shape[1]
    leads, heads = q_ref.shape[:2]
    width = leads * ROWS
    limit0 = info[1 + u]
    limit1 = info[1 + users + u]
    rows_dims = (((1,), (1,)), ((), ()))
    first_dims = (((0,), (0,)), ((), ()))

    def run(masked):
        for j in range(heads):
            cols = slice(j * HD, (j + 1) * HD)
            q = q_ref[:, j].reshape(width, HD)
            s0 = lax.dot_general(
                k0_ref[0, :, cols], q, rows_dims, preferred_element_type=jnp.float32
            )
            s1 = lax.dot_general(
                k1_ref[0, :, cols], q, rows_dims, preferred_element_type=jnp.float32
            )
            s0 = s0 * SCALE2
            s1 = s1 * SCALE2
            if masked:
                at = lax.broadcasted_iota(jnp.int32, (length, width), 0)
                s0 = jnp.where(at < limit0, s0, DEAD)
                s1 = jnp.where(at < limit1, s1, DEAD)
            peak = jnp.maximum(
                jnp.max(s0, axis=0, keepdims=True), jnp.max(s1, axis=0, keepdims=True)
            )
            peak = peak.astype(jnp.bfloat16).astype(jnp.float32)
            w0 = jnp.exp2(s0 - peak)
            w1 = jnp.exp2(s1 - peak)
            total = jnp.sum(w0, axis=0, keepdims=True) + jnp.sum(w1, axis=0, keepdims=True)
            numer = lax.dot_general(
                v0_ref[0, :, cols],
                w0.astype(jnp.bfloat16),
                first_dims,
                preferred_element_type=jnp.float32,
            ) + lax.dot_general(
                v1_ref[0, :, cols],
                w1.astype(jnp.bfloat16),
                first_dims,
                preferred_element_type=jnp.float32,
            )
            numer = numer * (1.0 / total)
            spot = pl.ds(pl.multiple_of(u * ROWS, ROWS), ROWS)
            for d, tile in enumerate(packed_tiles(numer[:HALF], numer[HALF:])):
                o_ref[d, part * heads + j, spot, :] = tile.astype(jnp.bfloat16)
            high = total.astype(jnp.bfloat16).astype(jnp.float32)
            low = total - high
            head = part * heads + j
            m_ref[0, head, pl.ds(2 * u, 1), :] = peak
            m_ref[1, head, pl.ds(2 * u, 1), :] = high
            m_ref[0, head, pl.ds(2 * u + 1, 1), :] = low
            m_ref[1, head, pl.ds(2 * u + 1, 1), :] = low

    @pl.when((u == 0) & (part == 0))
    def _():
        m_ref[...] = jnp.zeros_like(m_ref)

    live = (limit0 >= length) & (limit1 >= length)
    pl.when(live)(lambda: run(False))
    pl.when(jnp.logical_not(live))(lambda: run(True))

    @pl.when((u == users - 1) & (part == pl.num_programs(1) - 1))
    def _():
        for j in range(o_ref.shape[1]):
            for d, tile in enumerate(packed_tiles(m_ref[0, j], m_ref[1, j])):
                o_ref[d, j, users * ROWS :, :] = tile.astype(jnp.bfloat16)


def partials(info, q, k0, k1, v0, v1, base):
    lead, heads, qrows, _ = q.shape
    users = qrows // ROWS
    length = k0.shape[1]
    share = heads // PARTS

    def mine(u, p, info):
        return (info[0] + u, 0, p)

    def other(u, p, info):
        return (base + u if base else u, 0, p)

    cache = (1, length, share * HD)
    out = (lead, heads, qrows + META, HD)
    return pl.pallas_call(
        partial_kernel,
        grid_spec=pltpu.PrefetchScalarGridSpec(
            num_scalar_prefetch=1,
            grid=(users, PARTS),
            in_specs=[
                pl.BlockSpec((lead, share, ROWS, HD), lambda u, p, info: (0, p, u, 0)),
                pl.BlockSpec(cache, mine),
                pl.BlockSpec(cache, other),
                pl.BlockSpec(cache, mine),
                pl.BlockSpec(cache, other),
            ],
            out_specs=pl.BlockSpec(out, lambda u, p, info: (0, 0, 0, 0)),
            scratch_shapes=[pltpu.VMEM((2, heads, META, lead * ROWS), jnp.float32)],
        ),
        out_shape=jax.ShapeDtypeStruct(out, jnp.bfloat16),
        compiler_params=pltpu.CompilerParams(
            dimension_semantics=("arbitrary", "arbitrary"),
            vmem_limit_bytes=40 << 20,
        ),
        cost_estimate=pl.CostEstimate(
            flops=8 * heads * lead * qrows * HD * length,
            bytes_accessed=8 * users * length * heads * HD + 4 * q.size,
            transcendentals=2 * heads * lead * qrows * length,
        ),
    )(info, q, k0, k1, v0, v1)


def combine_kernel(x_ref, own_ref, value_ref, o_ref, w_ref):
    chips = x_ref.shape[0]
    users = value_ref.shape[0]
    low = lax.broadcasted_iota(jnp.int32, (1, HD), 1) < ROWS
    for u in range(users):
        own = own_ref[u]

        def stats(i):
            both = x_ref[i, users * ROWS :, :].astype(jnp.float32)
            line = both[2 * u : 2 * u + 1]
            turned = pltpu.roll(line, ROWS, 1)
            return (
                jnp.where(low, line, turned),
                jnp.where(low, turned, line) + both[2 * u + 1 : 2 * u + 2],
            )

        peak = own
        for i in range(chips):
            peak = jnp.maximum(peak, stats(i)[0])
        fresh = jnp.exp2(own - peak)
        total = fresh
        for i in range(chips):
            top, mass = stats(i)
            weight = mass * jnp.exp2(top - peak)
            w_ref[i : i + 1, :] = weight
            total = total + weight
        inverse = 1.0 / total
        acc = value_ref[u] * fresh
        for i in range(chips):
            acc = acc + x_ref[i, u * ROWS : (u + 1) * ROWS, :].astype(jnp.float32) * w_ref[
                i : i + 1, :
            ]
        turned = (acc * inverse).T
        o_ref[u] = jnp.concatenate([turned[:ROWS], turned[ROWS:]], axis=1).astype(
            jnp.bfloat16
        )


def combined(x, own, value):
    users = value.shape[0]
    return pl.pallas_call(
        combine_kernel,
        out_shape=jax.ShapeDtypeStruct((users, ROWS, HD), jnp.bfloat16),
        scratch_shapes=[pltpu.VMEM((x.shape[0], HD), jnp.float32)],
        compiler_params=pltpu.CompilerParams(vmem_limit_bytes=24 << 20),
        cost_estimate=pl.CostEstimate(
            flops=2 * x.size, bytes_accessed=2 * x.size, transcendentals=0
        ),
    )(x, own, value)


def body(queries, key_cache, value_cache, key_table, value_table, lengths, token_ids):
    users, beams, _ = queries.shape
    half = users // 2
    each = half // CHUNKS
    length = key_cache.shape[1]
    c = lax.axis_index("c")
    row = (lax.axis_index("zl") * SIZES[1] + lax.axis_index("y")) * 2 + c
    col = lax.axis_index("x") * SIZES[4] + lax.axis_index("zh")
    swap = functools.partial(lax.ppermute, axis_name="c", perm=[(0, 1), (1, 0)])

    def halves(array):
        return (
            lax.dynamic_slice_in_dim(array, c * half, half, 0),
            lax.dynamic_slice_in_dim(array, (1 - c) * half, half, 0),
        )

    q = queries.reshape(users, beams, GROUP, HD).transpose(0, 2, 1, 3)
    q_mine, q_give = halves(q)
    q_chip = jnp.concatenate([q_mine, swap(q_give)], axis=2)
    chips = SIZES[0] * SIZES[1] * SIZES[3] * SIZES[4]

    everyone = []
    for n in range(CHUNKS):
        packed = q_chip[n * each : (n + 1) * each].reshape(1, each * ROWS, HD)
        got = lax.all_to_all(
            jnp.broadcast_to(packed, (chips, *packed.shape[1:])), CHIPS, 0, 0, tiled=True
        )
        everyone.append(got.reshape(chips // KH, KH, *packed.shape[1:]))

    k_other = swap(halves(key_cache)[1])
    v_other = swap(halves(value_cache)[1])

    limits = lax.dynamic_slice_in_dim(lengths, c * half, half, 0)
    offset = (row * KH + col) * length
    other = ((row + 1 - 2 * c) * KH + col) * length
    arrived = []
    for n in range(CHUNKS):
        part = limits[n * each : (n + 1) * each]
        info = jnp.concatenate(
            [(c * half + n * each)[None], part - offset, part - other]
        ).astype(jnp.int32)
        sent = partials(info, everyone[n], key_cache, k_other, value_cache, v_other, n * each)
        sent = sent.reshape(chips, *sent.shape[2:])
        arrived.append(lax.all_to_all(sent, CHIPS, 0, 0, tiled=True))

    t_mine, t_give = halves(token_ids)
    tokens = jnp.concatenate([t_mine, swap(t_give)], axis=1)
    codes = jnp.arange(key_table.shape[0], dtype=jnp.int32)
    onehot = (tokens[..., None] == codes).astype(jnp.bfloat16)
    keys = lax.dynamic_slice_in_dim(key_table, col * HD, HD, 1)
    values = lax.dynamic_slice_in_dim(value_table, col * HD, HD, 1)
    own_keys = jnp.einsum("uwv,vc->uwc", onehot, keys, preferred_element_type=jnp.float32)
    own_values = jnp.einsum("uwv,vc->uwc", onehot, values, preferred_element_type=jnp.float32)
    own = jnp.sum(q_chip.astype(jnp.float32) * own_keys[:, None], axis=-1) * SCALE2
    own = jnp.tile(own.reshape(half, 1, ROWS), (1, 1, 2))
    own_values = own_values.reshape(half, 2 * beams, 2, HALF).transpose(0, 3, 2, 1)
    own_values = jnp.broadcast_to(
        own_values[:, :, :, None], (half, HALF, 2, GROUP, 2 * beams)
    ).reshape(half, HALF, HD)

    kept, received = [], []
    for n in range(CHUNKS):
        mine = slice(n * each, (n + 1) * each)
        result = combined(arrived[n], own[mine], own_values[mine])
        result = result.reshape(each, GROUP, 2 * beams, HD)
        kept.append(result[:, :, :beams])
        received.append(swap(result[:, :, beams:]))
    whole = jnp.where(
        c == 0, jnp.concatenate(kept + received), jnp.concatenate(received + kept)
    )
    return whole.transpose(0, 2, 1, 3).reshape(users, beams, GROUP * HD)


def solution(mesh):
    fine = Mesh(np.asarray(mesh.devices).reshape(SIZES), FINE)
    row, col = ("zl", "y", "c"), ("x", "zh")
    return jax.shard_map(
        body,
        mesh=fine,
        in_specs=(
            P(None, row, col),
            P(None, row + col, None),
            P(None, row + col, None),
            P(),
            P(),
            P(),
            P(None, row),
        ),
        out_specs=P(None, row, col),
        check_vma=False,
    )
```

time: 217 us -> 166 us (0.76); the launches traced: 215 us -> 166 us
  waiting for transfers between devices: 103 us -> 35.9 us
  blocking collectives: 0 us -> 38.8 us
  Pallas kernels: 68.2 us -> 40.6 us
  starting transfers between devices: 29 us -> 32.9 us
  local copies, waits for them, and re-layouts: 11.6 us -> 14.7 us
    all_to_all x1, waiting for transfers between devices: 54.4 us -> 4.64 us  [body(): lax.all_to_all(jnp.broadcast_to(packed, (chips, *packed.shape[1:])), CHIP...]
    all_to_all x0 -> x1, blocking collectives: none -> 38.8 us  [body(): lax.all_to_all(jnp.broadcast_to(packed, (chips, *packed.shape[1:])), CHIP...]
    pallas_call x1 -> x2, Pallas kernels: 57.2 us -> 35.4 us  [partials(): pl.pallas_call(partial_kernel, grid_spec=pltpu.PrefetchScalarGridSpec(num...]
    all_to_all x1 -> x2, waiting for transfers between devices: 47 us -> 26.6 us  [body(): arrived.append(lax.all_to_all(sent, CHIPS, 0, 0, tiled=True))]
    all_to_all x1 -> x2, starting transfers between devices: 9.68 us -> 16.6 us  [body(): arrived.append(lax.all_to_all(sent, CHIPS, 0, 0, tiled=True))]
    pallas_call x1 -> x2, Pallas kernels: 11 us -> 5.24 us  [combined(): pl.pallas_call(combine_kernel, out_shape=jax.ShapeDtypeStruct((users, ROW...]
    all_to_all x1, starting transfers between devices: 11.6 us -> 6.69 us  [body(): lax.all_to_all(jnp.broadcast_to(packed, (chips, *packed.shape[1:])), CHIP...]
    unnamed x8 -> x16, local copies, waits for them, and re-layouts: 0.02 us -> 4.4 us
  transfers between devices with their start and end apart: 7 -> 9, of which waited for: 4 -> 6; matrix products, arithmetic and copies ran while one was open for 6% -> 4% of each run, Pallas kernels for 0% -> 25%
where the time goes in v2:
time: 166 us
  Pallas kernels  40.6 us (24%)
  blocking collectives  38.8 us (23%)
  waiting for transfers between devices  35.9 us (22%)
  starting transfers between devices  32.9 us (20%)
  local copies, waits for them, and re-layouts  14.7 us (9%)
    all_to_all x1, blocking collectives, body(): lax.all_to_all(jnp.broadcast_to(packed, (chips, *packed.shape[1:])), CHIP...  38.8 us
    pallas_call x2, Pallas kernels, partials(): pl.pallas_call(partial_kernel, grid_spec=pltpu.PrefetchScalarGridSpec(num...  35.4 us
    all_to_all x2, waiting for transfers between devices, body(): arrived.append(lax.all_to_all(sent, CHIPS, 0, 0, tiled=True))  26.6 us
    all_to_all x2, starting transfers between devices, body(): arrived.append(lax.all_to_all(sent, CHIPS, 0, 0, tiled=True))  16.6 us
    dynamic_slice x3, local copies, waits for them, and re-layouts, halves(): lax.dynamic_slice_in_dim(array, (1 - c) * half, half, 0)  7.33 us
    all_to_all x1, starting transfers between devices, body(): lax.all_to_all(jnp.broadcast_to(packed, (chips, *packed.shape[1:])), CHIP...  6.69 us
    pallas_call x2, Pallas kernels, combined(): pl.pallas_call(combine_kernel, out_shape=jax.ShapeDtypeStruct((users, ROW...  5.24 us
    all_to_all x1, waiting for transfers between devices, body(): lax.all_to_all(jnp.broadcast_to(packed, (chips, *packed.shape[1:])), CHIP...  4.64 us
  transfers between devices with their start and end apart: 9, of which 6 were waited for; matrix products, arithmetic and copies ran while one was open for 4% of the time, Pallas kernels for 25%

profile of v2, /device:TPU:1, one launch (start us, length us, event | category | flops | bytes accessed | tf_op | source)
XLA Modules:
  0.0 165.7 jit_solution(18057133074301518711)
XLA Ops:
  0.0 4.9 %constant_dynamic-slice_fusion.3 = bf16[4,512,1024]{2,1,0:T(8,128)(2,1)} fusion(bf16[8,512,1024]{2,1,0:T(8,128)(2,1)} %k0_ref.3, s32[]{:T(128)S(6)} %select_n.25), kind=kLoop, calls=%fused_computation.28 | loop fusion | bytes 8388612 | tf_op jit(solution)/shard_map/dynamic_slice | solution.py:218
  5.0 1.4 collective-permute-start.1
  6.4 2.4 %constant_dynamic-slice_fusion.2 = bf16[4,512,1024]{2,1,0:T(8,128)(2,1)} fusion(bf16[8,512,1024]{2,1,0:T(8,128)(2,1)S(1)} %copy-done.4, s32[]{:T(128)S(6)} %select_n.25), kind=kLoop, calls=%fused_computation.27 | loop fusion | bytes 8388612 | tf_op jit(solution)/shard_map/dynamic_slice | solution.py:218
  8.8 1.4 collective-permute-start.2
  10.2 3.0 %collective-permute-done = bf16[4,4,8,128]{3,2,1,0:T(8,128)(2,1)S(1)} collective-permute-done((bf16[4,4,8,128]{3,2,1,0:T(8,128)(2,1)S(1)}, bf16[4,4,8,128]{3,2,1,0:T(8,128)(2,1)S(1)}, u32[]{:S(2)}, u32[]{:S(2)}) %collective-permute-start) | collective-permute-done | bytes 32800 | tf_op jit(solution)/shard_map/ppermute | solution.py:223
  13.8 38.8 %all_to_all.20 = bf16[64,128,128]{2,1,0:T(8,128)(2,1)} all-to-all(bf16[64,128,128]{2,1,0:T(8,128)(2,1)S(1)} %broadcast_in_dim.33), channel_id=1, replica_groups=mesh['zl'=2,'y'=4,'c'=2,'x'=4,'zh'=2] {'zl','y','x','zh'}, dimensions={0} | all-to-all | bytes 4194304 | tf_op jit(solution)/shard_map/all_to_all | solution.py:229
  52.5 1.8 %broadcast_in_dim.37 = bf16[64,128,128]{2,1,0:T(8,128)(2,1)} broadcast(bf16[128,128]{1,0:T(8,128)(2,1)S(1)} %bitcast.40), dimensions={1,2} | broadcast | bytes 2129920 | tf_op jit(solution)/shard_map/broadcast_in_dim | solution.py:230
  54.4 6.7 %all-to-all-start.2 = ((bf16[64,128,128]{2,1,0:T(8,128)(2,1)}), bf16[64,128,128]{2,1,0:T(8,128)(2,1)}, u32[]{:S(2)}, u32[]{:S(2)}) async-start(bf16[64,128,128]{2,1,0:T(8,128)(2,1)} %broadcast_in_dim.37), calls=%async_computation.2 | async-start | bytes 4194304 | tf_op jit(solution)/shard_map/all_to_all | solution.py:229
  61.3 1.6 copy-done.3
  62.9 17.6 %shard_map.73 = bf16[8,8,136,128]{3,2,1,0:T(8,128)(2,1)S(1)} custom-call(s32[5]{0:T(128)S(1)} %pad_add_fusion.1.info, bf16[8,8,128,128]{3,2,1,0:T(8,128)(2,1)S(1)} %bitcast.34, bf16[8,512,1024]{2,1,0:T(8,128)(2,1)} %k0_ref.3, bf16[4,512,1024]{2,1,0:T(8,128)(2,1)} %collective-permute-done.1.k1_ref, bf16[8,512,1024]{2,1,0:T(8,128)(2,1)} %v0_ref.3, ...), custom_call_target="tpu_custom_call" | custom-call | flops 4294967296 | bytes 12582912 | tf_op jit(solution)/shard_map/pallas_call | solution.py:126
  80.6 1.4 copy-done.2
  82.0 4.6 %all-to-all-done.2 = bf16[64,128,128]{2,1,0:T(8,128)(2,1)} async-done(((bf16[64,128,128]{2,1,0:T(8,128)(2,1)}), bf16[64,128,128]{2,1,0:T(8,128)(2,1)}, u32[]{:S(2)}, u32[]{:S(2)}) %all-to-all-start.2) | async-done | bytes 2097184 | tf_op jit(solution)/shard_map/all_to_all | solution.py:229
  86.6 8.4 %all-to-all-start.1 = ((bf16[64,136,128]{2,1,0:T(8,128)(2,1)}), bf16[64,136,128]{2,1,0:T(8,128)(2,1)}, u32[]{:S(2)}, u32[]{:S(2)}) async-start(bf16[64,136,128]{2,1,0:T(8,128)(2,1)} %bitcast.33), calls=%async_computation.1 | async-start | bytes 4456448 | tf_op jit(solution)/shard_map/all_to_all | solution.py:248
  95.1 17.7 %shard_map.75 = bf16[8,8,136,128]{3,2,1,0:T(8,128)(2,1)S(1)} custom-call(s32[5]{0:T(128)S(1)} %pad_add_fusion.2.info, bf16[8,8,128,128]{3,2,1,0:T(8,128)(2,1)} %bitcast.15.q_ref, bf16[8,512,1024]{2,1,0:T(8,128)(2,1)} %k0_ref.3, bf16[4,512,1024]{2,1,0:T(8,128)(2,1)} %collective-permute-done.1.k1_ref, bf16[8,512,1024]{2,1,0:T(8,128)(2,1)} %v0_ref.3, ...), custom_call_target="tpu_custom_call" | custom-call | flops 4294967296 | bytes 12582912 | tf_op jit(solution)/shard_map/pallas_call | solution.py:126
  112.8 1.4 copy-done.1
  114.2 7.9 %all-to-all-done.1.x_ref = bf16[64,136,128]{2,1,0:T(8,128)(2,1)} async-done(((bf16[64,136,128]{2,1,0:T(8,128)(2,1)}), bf16[64,136,128]{2,1,0:T(8,128)(2,1)}, u32[]{:S(2)}, u32[]{:S(2)}) %all-to-all-start.1) | async-done | bytes 2228256 | tf_op jit(solution)/shard_map/all_to_all | solution.py:248
  122.2 8.2 %all-to-all-start.3 = ((bf16[64,136,128]{2,1,0:T(8,128)(2,1)}), bf16[64,136,128]{2,1,0:T(8,128)(2,1)}, u32[]{:S(2)}, u32[]{:S(2)}) async-start(bf16[64,136,128]{2,1,0:T(8,128)(2,1)} %bitcast.32), calls=%async_computation.3 | async-start | bytes 4456448 | tf_op jit(solution)/shard_map/all_to_all | solution.py:248
  130.4 2.2 %collective-permute-start.3 = (s32[4,8]{1,0:T(4,128)S(1)}, s32[4,8]{1,0:T(4,128)S(1)}, u32[]{:S(2)}, u32[]{:S(2)}) collective-permute-start(s32[4,8]{1,0:T(4,128)S(1)} %get-tuple-element.16), channel_id=1, source_target_pairs={{0,8},{8,0},{1,9},{9,1},{2,10},{10,2},{3,11},{11,3},{4,12},{12,4},... | collective-permute-start | bytes 392 | tf_op jit(solution)/shard_map/ppermute | solution.py:251
  134.1 1.2 fusion.2
  135.7 2.6 %shard_map.74 = bf16[2,64,128]{2,1,0:T(8,128)(2,1)S(1)} custom-call(bf16[64,136,128]{2,1,0:T(8,128)(2,1)} %all-to-all-done.1.x_ref, f32[2,1,128]{2,1,0:T(1,128)S(1)} %tile.13.own_ref, f32[2,64,128]{2,1,0:T(8,128)S(1)} %copy.11.value_ref), custom_call_target="tpu_custom_call" | custom-call | flops 2228224 | bytes 2228224 | tf_op jit(solution)/shard_map/pallas_call | solution.py:194
  138.8 18.7 %all-to-all-done.3.x_ref = bf16[64,136,128]{2,1,0:T(8,128)(2,1)} async-done(((bf16[64,136,128]{2,1,0:T(8,128)(2,1)}), bf16[64,136,128]{2,1,0:T(8,128)(2,1)}, u32[]{:S(2)}, u32[]{:S(2)}) %all-to-all-start.3) | async-done | bytes 2228256 | tf_op jit(solution)/shard_map/all_to_all | solution.py:248
  157.5 2.6 %shard_map.76 = bf16[2,64,128]{2,1,0:T(8,128)(2,1)S(1)} custom-call(bf16[64,136,128]{2,1,0:T(8,128)(2,1)} %all-to-all-done.3.x_ref, f32[2,1,128]{2,1,0:T(1,128)S(1)} %tile.15.own_ref, f32[2,64,128]{2,1,0:T(8,128)S(1)} %copy.13.value_ref), custom_call_target="tpu_custom_call" | custom-call | flops 2228224 | bytes 2228224 | tf_op jit(solution)/shard_map/pallas_call | solution.py:194
  160.1 4.1 %collective-permute-start.5 = (bf16[2,4,8,128]{3,2,1,0:T(8,128)(2,1)S(1)}, bf16[2,4,8,128]{3,2,1,0:T(8,128)(2,1)S(1)}, u32[]{:S(2)}, u32[]{:S(2)}) collective-permute-start(bf16[2,4,8,128]{3,2,1,0:T(8,128)(2,1)S(1)} %get-tuple-element.14), channel_id=1, source_target_pairs={{0,8},{8,0},{1,9},{9,1},{2,10},{10,2},{3,11},{11,3},{4,12},{12,4},... | collective-permute-start | bytes 49160 | tf_op jit(solution)/shard_map/ppermute | solution.py:271
  164.2 0.8 collective-permute-done.5
  (48 shorter events, 3.8 us)
Async XLA Ops:
  0.0 133.5 %copy-start = (bf16[1024,1024]{1,0:T(8,128)(2,1)S(1)}, bf16[1024,1024]{1,0:T(8,128)(2,1)}, u32[]{:S(2)}) copy-start(bf16[1024,1024]{1,0:T(8,128)(2,1)} %param.11) | copy-start | bytes 6291460
  0.0 6.4 %copy-start.4 = (bf16[8,512,1024]{2,1,0:T(8,128)(2,1)S(1)}, bf16[8,512,1024]{2,1,0:T(8,128)(2,1)}, u32[]{:S(2)}) copy-start(bf16[8,512,1024]{2,1,0:T(8,128)(2,1)} %v0_ref.3) | copy-start | bytes 25165828
  5.0 5.2 %copy-start.5 = (bf16[8,8,512]{2,1,0:T(8,128)(2,1)S(1)}, bf16[8,8,512]{2,1,0:T(8,128)(2,1)}, u32[]{:S(2)}) copy-start(bf16[8,8,512]{2,1,0:T(8,128)(2,1)} %param.7) | copy-start | bytes 196612
  5.0 56.4 %collective-permute-start.1 = (bf16[4,512,1024]{2,1,0:T(8,128)(2,1)}, bf16[4,512,1024]{2,1,0:T(8,128)(2,1)}, u32[]{:S(2)}, u32[]{:S(2)}) collective-permute-start(bf16[4,512,1024]{2,1,0:T(8,128)(2,1)} %constant_dynamic-slice_fusion.3), channel_id=1, source_target_pairs={{0,8},{8,0},{1,9},{9,1},{2,10},{10,2},{3,11},{11,3},{4,12},{12,4},... | collective-permute-start | bytes 12582920 | tf_op jit(solution)/shard_map/ppermute | solution.py:234
  8.8 52.6 %collective-permute-start.2 = (bf16[4,512,1024]{2,1,0:T(8,128)(2,1)}, bf16[4,512,1024]{2,1,0:T(8,128)(2,1)}, u32[]{:S(2)}, u32[]{:S(2)}) collective-permute-start(bf16[4,512,1024]{2,1,0:T(8,128)(2,1)} %constant_dynamic-slice_fusion.2), channel_id=1, source_target_pairs={{0,8},{8,0},{1,9},{9,1},{2,10},{10,2},{3,11},{11,3},{4,12},{12,4},... | collective-permute-start | bytes 12582920 | tf_op jit(solution)/shard_map/ppermute | solution.py:235
  10.1 3.1 %collective-permute-start = (bf16[4,4,8,128]{3,2,1,0:T(8,128)(2,1)S(1)}, bf16[4,4,8,128]{3,2,1,0:T(8,128)(2,1)S(1)}, u32[]{:S(2)}, u32[]{:S(2)}) collective-permute-start(bf16[4,4,8,128]{3,2,1,0:T(8,128)(2,1)S(1)} %get-tuple-element.9), channel_id=1, source_target_pairs={{0,8},{8,0},{1,9},{9,1},{2,10},{10,2},{3,11},{11,3},{4,12},{12,4},... | collective-permute-start | bytes 98312 | tf_op jit(solution)/shard_map/ppermute | solution.py:223
  54.4 6.7 %copy-start.7 = (s32[8]{0:T(128)S(1)}, s32[8]{0:T(128)}, u32[]{:S(2)}) copy-start(s32[8]{0:T(128)} %param.12) | copy-start | bytes 100
  54.4 32.3 %all-to-all-start.2 = ((bf16[64,128,128]{2,1,0:T(8,128)(2,1)}), bf16[64,128,128]{2,1,0:T(8,128)(2,1)}, u32[]{:S(2)}, u32[]{:S(2)}) async-start(bf16[64,128,128]{2,1,0:T(8,128)(2,1)} %broadcast_in_dim.37), calls=%async_computation.2 | async-start | bytes 4194304 | tf_op jit(solution)/shard_map/all_to_all | solution.py:229
  61.3 1.6 copy-start.3
  80.6 1.4 copy-start.2
  86.6 35.5 %all-to-all-start.1 = ((bf16[64,136,128]{2,1,0:T(8,128)(2,1)}), bf16[64,136,128]{2,1,0:T(8,128)(2,1)}, u32[]{:S(2)}, u32[]{:S(2)}) async-start(bf16[64,136,128]{2,1,0:T(8,128)(2,1)} %bitcast.33), calls=%async_computation.1 | async-start | bytes 4456448 | tf_op jit(solution)/shard_map/all_to_all | solution.py:248
  112.8 1.4 copy-start.1
  122.1 8.2 %copy-start.6 = (s32[8,8]{1,0:T(8,128)S(1)}, s32[8,8]{1,0:T(8,128)}, u32[]{:S(2)}) copy-start(s32[8,8]{1,0:T(8,128)} %param.13) | copy-start | bytes 772
  122.2 35.3 %all-to-all-start.3 = ((bf16[64,136,128]{2,1,0:T(8,128)(2,1)}), bf16[64,136,128]{2,1,0:T(8,128)(2,1)}, u32[]{:S(2)}, u32[]{:S(2)}) async-start(bf16[64,136,128]{2,1,0:T(8,128)(2,1)} %bitcast.32), calls=%async_computation.3 | async-start | bytes 4456448 | tf_op jit(solution)/shard_map/all_to_all | solution.py:248
  130.4 3.1 %collective-permute-start.3 = (s32[4,8]{1,0:T(4,128)S(1)}, s32[4,8]{1,0:T(4,128)S(1)}, u32[]{:S(2)}, u32[]{:S(2)}) collective-permute-start(s32[4,8]{1,0:T(4,128)S(1)} %get-tuple-element.16), channel_id=1, source_target_pairs={{0,8},{8,0},{1,9},{9,1},{2,10},{10,2},{3,11},{11,3},{4,12},{12,4},... | collective-permute-start | bytes 392 | tf_op jit(solution)/shard_map/ppermute | solution.py:251
  138.4 25.9 %collective-permute-start.4 = (bf16[2,4,8,128]{3,2,1,0:T(8,128)(2,1)S(1)}, bf16[2,4,8,128]{3,2,1,0:T(8,128)(2,1)S(1)}, u32[]{:S(2)}, u32[]{:S(2)}) collective-permute-start(bf16[2,4,8,128]{3,2,1,0:T(8,128)(2,1)S(1)} %get-tuple-element.12), channel_id=1, source_target_pairs={{0,8},{8,0},{1,9},{9,1},{2,10},{10,2},{3,11},{11,3},{4,12},{12,4},... | collective-permute-start | bytes 49160 | tf_op jit(solution)/shard_map/ppermute | solution.py:271
  160.1 5.0 %collective-permute-start.5 = (bf16[2,4,8,128]{3,2,1,0:T(8,128)(2,1)S(1)}, bf16[2,4,8,128]{3,2,1,0:T(8,128)(2,1)S(1)}, u32[]{:S(2)}, u32[]{:S(2)}) collective-permute-start(bf16[2,4,8,128]{3,2,1,0:T(8,128)(2,1)S(1)} %get-tuple-element.14), channel_id=1, source_target_pairs={{0,8},{8,0},{1,9},{9,1},{2,10},{10,2},{3,11},{11,3},{4,12},{12,4},... | collective-permute-start | bytes 49160 | tf_op jit(solution)/shard_map/ppermute | solution.py:271

commit v3 on v2

v3 whole, which is shorter than its diff:
```python
import functools

import jax
import jax.numpy as jnp
import numpy as np
from jax import lax
from jax.experimental import pallas as pl
from jax.experimental.pallas import tpu as pltpu
from jax.sharding import Mesh
from jax.sharding import PartitionSpec as P

KH = 8
GROUP = 4
HD = 128
HALF = HD // 2
SCALE2 = HD**-0.5 * 1.4426950408889634
FINE = ("zl", "y", "c", "x", "zh")
SIZES = (2, 4, 2, 4, 2)
CHIPS = ("zl", "y", "x", "zh")
DEAD = -(2.0**100)
ROWS = 64
META = 8
PARTS = 2


def packed_tiles(first, second):
    low = lax.broadcasted_iota(jnp.int32, (first.shape[0], HD), 1) < ROWS
    out = []
    for k in range(first.shape[1] // HD):
        a = first[:, k * HD : (k + 1) * HD]
        b = second[:, k * HD : (k + 1) * HD]
        crossed = pltpu.roll(jnp.where(low, b, a), ROWS, 1)
        out.append(jnp.where(low, a, crossed))
        out.append(jnp.where(low, crossed, b))
    return out


def spread_kernel(holders, q_ref, o_ref):
    for t, w in enumerate(holders):
        o_ref[t] = q_ref[w]


def partial_kernel(
    info, lengths, qa_ref, qb_ref, k0_ref, k1_ref, v0_ref, v1_ref, oa_ref, ob_ref
):
    length = k0_ref.shape[1]
    leads, heads = qa_ref.shape[:2]
    width = 2 * leads * ROWS
    limit0 = lengths[info[0]] - info[2]
    limit1 = lengths[info[0]] - info[3]
    rows_dims = (((1,), (1,)), ((), ()))
    first_dims = (((0,), (0,)), ((), ()))

    def run(masked):
        def head(j):
            if isinstance(j, int):
                cols = slice(j * HD, (j + 1) * HD)
            else:
                cols = pl.ds(pl.multiple_of(j * HD, HD), HD)
            q = jnp.concatenate(
                [
                    qa_ref[:, j].reshape(width // 2, HD),
                    qb_ref[:, j].reshape(width // 2, HD),
                ]
            )
            s0 = lax.dot_general(
                k0_ref[0, :, cols], q, rows_dims, preferred_element_type=jnp.float32
            )
            s1 = lax.dot_general(
                k1_ref[0, :, cols], q, rows_dims, preferred_element_type=jnp.float32
            )
            s0 = s0 * SCALE2
            s1 = s1 * SCALE2
            if masked:
                at = lax.broadcasted_iota(jnp.int32, (length, width), 0)
                s0 = jnp.where(at < limit0, s0, DEAD)
                s1 = jnp.where(at < limit1, s1, DEAD)
            peak = jnp.maximum(
                jnp.max(s0, axis=0, keepdims=True), jnp.max(s1, axis=0, keepdims=True)
            )
            peak = peak.astype(jnp.bfloat16).astype(jnp.float32)
            w0 = jnp.exp2(s0 - peak)
            w1 = jnp.exp2(s1 - peak)
            total = jnp.sum(w0, axis=0, keepdims=True) + jnp.sum(w1, axis=0, keepdims=True)
            numer = lax.dot_general(
                v0_ref[0, :, cols],
                w0.astype(jnp.bfloat16),
                first_dims,
                preferred_element_type=jnp.float32,
            ) + lax.dot_general(
                v1_ref[0, :, cols],
                w1.astype(jnp.bfloat16),
                first_dims,
                preferred_element_type=jnp.float32,
            )
            numer = numer * (1.0 / total)
            high = total.astype(jnp.bfloat16).astype(jnp.float32)
            low = total - high
            top = lax.broadcasted_iota(jnp.int32, (META, width), 0) == 0
            tiles = packed_tiles(numer[:HALF], numer[HALF:])
            notes = packed_tiles(jnp.where(top, peak, low), jnp.where(top, high, low))
            for d in range(2 * leads):
                o_ref = oa_ref if d < leads else ob_ref
                o_ref[d % leads, j, :ROWS, :] = tiles[d].astype(jnp.bfloat16)
                o_ref[d % leads, j, ROWS:, :] = notes[d].astype(jnp.bfloat16)

        if masked:
            pl.loop(0, heads)(head)
        else:
            for j in range(heads):
                head(j)

    live = (limit0 >= length) & (limit1 >= length)
    pl.when(live)(lambda: run(False))
    pl.when(jnp.logical_not(live))(lambda: run(True))


def partials(info, lengths, qa, qb, k0, k1, v0, v1):
    same = qa is qb
    lead, heads = qa.shape[0] // (2 if same else 1), qa.shape[1]
    length = k0.shape[1]
    share = heads // PARTS
    cache = (1, length, share * HD)

    def mine(p, info, lengths):
        return (info[0], 0, p)

    def other(p, info, lengths):
        return (info[1], 0, p)

    def first(p, info, lengths):
        return (0, p, 0, 0)

    def second(p, info, lengths):
        return (1 if same else 0, p, 0, 0)

    out = jax.ShapeDtypeStruct((lead, heads, ROWS + META, HD), jnp.bfloat16)
    block = pl.BlockSpec((lead, share, ROWS + META, HD), first)
    return pl.pallas_call(
        partial_kernel,
        grid_spec=pltpu.PrefetchScalarGridSpec(
            num_scalar_prefetch=2,
            grid=(PARTS,),
            in_specs=[
                pl.BlockSpec((lead, share, ROWS, HD), first),
                pl.BlockSpec((lead, share, ROWS, HD), second),
                pl.BlockSpec(cache, mine),
                pl.BlockSpec(cache, other),
                pl.BlockSpec(cache, mine),
                pl.BlockSpec(cache, other),
            ],
            out_specs=[block, block],
        ),
        out_shape=[out, out],
        compiler_params=pltpu.CompilerParams(
            dimension_semantics=("arbitrary",),
            vmem_limit_bytes=40 << 20,
        ),
        cost_estimate=pl.CostEstimate(
            flops=16 * heads * lead * ROWS * HD * length,
            bytes_accessed=8 * length * heads * HD + 8 * lead * heads * ROWS * HD,
            transcendentals=4 * heads * lead * ROWS * length,
        ),
    )(info, lengths, qa, qb, k0, k1, v0, v1)


def stats_of(notes, low):
    line = notes[:1]
    turned = pltpu.roll(line, ROWS, 1)
    return jnp.where(low, line, turned), jnp.where(low, turned, line) + notes[1:2]


def merge_kernel(*refs):
    o_ref = refs[-1]
    low = lax.broadcasted_iota(jnp.int32, (1, HD), 1) < ROWS
    first = lax.broadcasted_iota(jnp.int32, (META, HD), 0) == 0

    def join(parts):
        def one(t, _):
            pairs = [stats_of(r[t, ROWS:, :].astype(jnp.float32), low) for r in parts]
            peak = functools.reduce(jnp.maximum, [p for p, _ in pairs])
            weights = [m * jnp.exp2(p - peak) for p, m in pairs]
            total = functools.reduce(jnp.add, weights)
            inverse = 1.0 / total
            acc = None
            for r, w in zip(parts, weights):
                term = r[t, :ROWS, :].astype(jnp.float32) * (w * inverse)
                acc = term if acc is None else acc + term
            o_ref[t, :ROWS, :] = acc.astype(jnp.bfloat16)
            high = total.astype(jnp.bfloat16).astype(jnp.float32)
            rest = total - high
            line = jnp.where(low, peak, high)
            o_ref[t, ROWS:, :] = jnp.where(first, line, rest).astype(jnp.bfloat16)
            return 0

        lax.fori_loop(0, parts[0].shape[0], one, 0, unroll=4)

    per = (len(refs) - 1) // 2
    half = pl.num_programs(0) // 2
    pl.when(pl.program_id(0) < half)(lambda: join(refs[:per]))
    pl.when(pl.program_id(0) >= half)(lambda: join(refs[per : 2 * per]))


def merged(left, right):
    count, rows, _ = left[0].shape
    steps = 2
    size = count // steps
    block = (size, rows, HD)
    ahead = pl.BlockSpec(block, lambda i: (jnp.minimum(i, steps - 1), 0, 0))
    behind = pl.BlockSpec(block, lambda i: (jnp.maximum(i - steps, 0), 0, 0))
    return pl.pallas_call(
        merge_kernel,
        grid=(2 * steps,),
        in_specs=[ahead] * len(left) + [behind] * len(right),
        out_specs=pl.BlockSpec(block, lambda i: (i, 0, 0)),
        out_shape=jax.ShapeDtypeStruct((2 * count, rows, HD), jnp.bfloat16),
        compiler_params=pltpu.CompilerParams(
            dimension_semantics=("arbitrary",), vmem_limit_bytes=40 << 20
        ),
        cost_estimate=pl.CostEstimate(
            flops=16 * left[0].size, bytes_accessed=20 * left[0].size, transcendentals=0
        ),
    )(*left, *right)


def combine_kernel(holders, x_ref, own_ref, value_ref, o_ref, w_ref):
    users = value_ref.shape[0]
    low = lax.broadcasted_iota(jnp.int32, (1, HD), 1) < ROWS
    for u in range(users):
        own = own_ref[u]
        senders = [i for i, w in enumerate(holders) if w == u]
        pairs = [stats_of(x_ref[i, ROWS:, :].astype(jnp.float32), low) for i in senders]
        peak = own
        for top, _ in pairs:
            peak = jnp.maximum(peak, top)
        fresh = jnp.exp2(own - peak)
        total = fresh
        for i, (top, mass) in zip(senders, pairs):
            weight = mass * jnp.exp2(top - peak)
            w_ref[i : i + 1, :] = weight
            total = total + weight
        inverse = 1.0 / total
        acc = value_ref[u] * fresh
        for i in senders:
            acc = acc + x_ref[i, :ROWS, :].astype(jnp.float32) * w_ref[i : i + 1, :]
        turned = (acc * inverse).T
        o_ref[u] = jnp.concatenate([turned[:ROWS], turned[ROWS:]], axis=1).astype(
            jnp.bfloat16
        )


def combined(holders, x, own, value):
    users = value.shape[0]
    return pl.pallas_call(
        functools.partial(combine_kernel, holders),
        out_shape=jax.ShapeDtypeStruct((users, ROWS, HD), jnp.bfloat16),
        scratch_shapes=[pltpu.VMEM((x.shape[0], HD), jnp.float32)],
        compiler_params=pltpu.CompilerParams(vmem_limit_bytes=24 << 20),
        cost_estimate=pl.CostEstimate(
            flops=2 * x.size, bytes_accessed=2 * x.size, transcendentals=0
        ),
    )(x, own, value)


def moved(array, axis, step):
    count = SIZES[FINE.index(axis)]
    return lax.ppermute(array, axis, [(i, (i + step) % count) for i in range(count)])


def body(queries, key_cache, value_cache, key_table, value_table, lengths, token_ids):
    users, beams, _ = queries.shape
    half = users // 2
    length = key_cache.shape[1]
    x, y, zl, zh, c = (lax.axis_index(n) for n in ("x", "y", "zl", "zh", "c"))
    row = (zl * SIZES[1] + y) * 2 + c
    col = x * SIZES[4] + zh
    swap = functools.partial(lax.ppermute, axis_name="c", perm=[(0, 1), (1, 0)])

    def halves(array):
        return (
            lax.dynamic_slice_in_dim(array, c * half, half, 0),
            lax.dynamic_slice_in_dim(array, (1 - c) * half, half, 0),
        )

    q = queries.reshape(users, beams, GROUP, HD).transpose(0, 2, 1, 3)
    q_mine, q_give = halves(q)
    q_chip = jnp.concatenate([q_mine, swap(q_give)], axis=2).reshape(half, ROWS, HD)

    holders = [
        (a + b + 2 * h + l) % half
        for l in range(SIZES[0])
        for b in range(SIZES[1])
        for a in range(SIZES[3])
        for h in range(SIZES[4])
    ]
    chips = len(holders)
    held = (x + y + 2 * zh + zl) % half
    operand = pl.pallas_call(
        functools.partial(spread_kernel, holders),
        out_shape=jax.ShapeDtypeStruct((chips, ROWS, HD), jnp.bfloat16),
    )(q_chip)
    got = lax.all_to_all(operand, CHIPS, 0, 0, tiled=True)
    got = got.reshape(chips // KH, KH, ROWS, HD)
    lead = chips // KH // 2
    got_a, got_b = got[:lead], got[lead:]

    k_other = swap(halves(key_cache)[1])
    v_other = swap(halves(value_cache)[1])

    offset = (row * KH + col) * length
    other = ((row + 1 - 2 * c) * KH + col) * length

    def computed(step, qa, qb):
        user = (held - step) % half
        info = jnp.stack([c * half + user, user, offset, other]).astype(jnp.int32)
        return partials(info, lengths, qa, qb, key_cache, k_other, value_cache, v_other)

    left, right = [], []
    for step in (0, 1, -1, 2):
        if step:
            parts = computed(step, moved(got_a, "x", step), moved(got_b, "y", step))
        else:
            parts = computed(0, got, got)
        one, two = (p.reshape(-1, ROWS + META, HD) for p in parts)
        left.append(moved(one, "x", -step) if step else one)
        right.append(moved(two, "y", -step) if step else two)
    arrived = lax.all_to_all(merged(left, right), CHIPS, 0, 0, tiled=True)

    t_mine, t_give = halves(token_ids)
    tokens = jnp.concatenate([t_mine, swap(t_give)], axis=1)
    codes = jnp.arange(key_table.shape[0], dtype=jnp.int32)
    onehot = (tokens[..., None] == codes).astype(jnp.bfloat16)
    keys = lax.dynamic_slice_in_dim(key_table, col * HD, HD, 1)
    values = lax.dynamic_slice_in_dim(value_table, col * HD, HD, 1)
    own_keys = jnp.einsum("uwv,vc->uwc", onehot, keys, preferred_element_type=jnp.float32)
    own_values = jnp.einsum("uwv,vc->uwc", onehot, values, preferred_element_type=jnp.float32)
    q_rows = q_chip.reshape(half, GROUP, 2 * beams, HD).astype(jnp.float32)
    own = jnp.sum(q_rows * own_keys[:, None], axis=-1) * SCALE2
    own = jnp.tile(own.reshape(half, 1, ROWS), (1, 1, 2))
    own_values = own_values.reshape(half, 2 * beams, 2, HALF).transpose(0, 3, 2, 1)
    own_values = jnp.broadcast_to(
        own_values[:, :, :, None], (half, HALF, 2, GROUP, 2 * beams)
    ).reshape(half, HALF, HD)

    result = combined(holders, arrived, own, own_values)
    result = result.reshape(half, GROUP, 2 * beams, HD)
    kept = result[:, :, :beams]
    received = swap(result[:, :, beams:])
    whole = jnp.where(
        c == 0, jnp.concatenate([kept, received]), jnp.concatenate([received, kept])
    )
    return whole.transpose(0, 2, 1, 3).reshape(users, beams, GROUP * HD)


def solution(mesh):
    fine = Mesh(np.asarray(mesh.devices).reshape(SIZES), FINE)
    row, col = ("zl", "y", "c"), ("x", "zh")
    return jax.shard_map(
        body,
        mesh=fine,
        in_specs=(
            P(None, row, col),
            P(None, row + col, None),
            P(None, row + col, None),
            P(),
            P(),
            P(),
            P(None, row),
        ),
        out_specs=P(None, row, col),
        check_vma=False,
    )
```

time: 166 us -> 160 us (0.964)
  waiting for transfers between devices: 35.9 us -> 20.8 us
  starting transfers between devices: 32.9 us -> 45.5 us
  blocking collectives: 38.8 us -> 28.2 us
  Pallas kernels: 40.6 us -> 49.2 us
  local copies, waits for them, and re-layouts: 14.7 us -> 12.3 us
    all_to_all x3 -> x1, waiting for transfers between devices: 31.2 us -> 0.83 us  [body(): arrived = lax.all_to_all(merged(left, right), CHIPS, 0, 0, tiled=True)]
    ppermute x3 -> x14, starting transfers between devices: 4.64 us -> 25.5 us  [the longest x12 16 us: moved(): lax.ppermute(array, axis, [(i, (i + step) % count) for i in range(count)])]
    ppermute x3 -> x14, waiting for transfers between devices: 3.88 us -> 19.1 us  [the longest x12 15.2 us: moved(): lax.ppermute(array, axis, [(i, (i + step) % count) for i in range(count)])]
    all_to_all x3 -> x1, starting transfers between devices: 23.3 us -> 8.9 us  [body(): arrived = lax.all_to_all(merged(left, right), CHIPS, 0, 0, tiled=True)]
    all_to_all x1, blocking collectives: 38.8 us -> 28.2 us  [body(): got = lax.all_to_all(operand, CHIPS, 0, 0, tiled=True)]
    pallas_call x2 -> x4, Pallas kernels: 35.4 us -> 42.2 us  [partials(): pl.pallas_call(partial_kernel, grid_spec=pltpu.PrefetchScalarGridSpec(num...]
    ppermute x1, starting transfers between devices: 2.24 us -> 8.37 us  [body(): tokens = jnp.concatenate([t_mine, swap(t_give)], axis=1)]
    unnamed x16, local copies, waits for them, and re-layouts: 4.4 us -> 1.84 us
  transfers between devices with their start and end apart: 9 -> 18, of which waited for: 6 -> 7; matrix products, arithmetic and copies ran while one was open for 4% -> 5% of each run, Pallas kernels for 25% -> 28%
where the time goes in v3:
time: 160 us; the launch traced here: 159 us
  Pallas kernels  49.2 us (31%)
  starting transfers between devices  45.5 us (28%)
  blocking collectives  28.2 us (18%)
  waiting for transfers between devices  20.8 us (13%)
  local copies, waits for them, and re-layouts  12.3 us (8%)
  other arithmetic  1.78 us (1%)
    pallas_call x4, Pallas kernels, partials(): pl.pallas_call(partial_kernel, grid_spec=pltpu.PrefetchScalarGridSpec(num...  42.2 us
    all_to_all x1, blocking collectives, body(): got = lax.all_to_all(operand, CHIPS, 0, 0, tiled=True)  28.2 us
    ppermute x12, starting transfers between devices, moved(): lax.ppermute(array, axis, [(i, (i + step) % count) for i in range(count)])  16 us
    ppermute x12, waiting for transfers between devices, moved(): lax.ppermute(array, axis, [(i, (i + step) % count) for i in range(count)])  15.2 us
    ppermute x1, starting transfers between devices, body(): received = swap(result[:, :, beams:])  9.41 us
    all_to_all x1, starting transfers between devices, body(): arrived = lax.all_to_all(merged(left, right), CHIPS, 0, 0, tiled=True)  8.9 us
    ppermute x1, starting transfers between devices, body(): tokens = jnp.concatenate([t_mine, swap(t_give)], axis=1)  8.37 us
    dynamic_slice x2, local copies, waits for them, and re-layouts, halves(): lax.dynamic_slice_in_dim(array, (1 - c) * half, half, 0)  7.33 us
  transfers between devices with their start and end apart: 18, of which 7 were waited for; matrix products, arithmetic and copies ran while one was open for 5% of the time, Pallas kernels for 28%

profile of v3, /device:TPU:1, one launch (start us, length us, event | category | flops | bytes accessed | tf_op | source)
XLA Modules:
  0.0 159.5 jit_solution(5319047497914199155)
XLA Ops:
  0.0 4.9 %constant_dynamic-slice_fusion.3 = bf16[4,512,1024]{2,1,0:T(8,128)(2,1)} fusion(bf16[8,512,1024]{2,1,0:T(8,128)(2,1)} %k0_ref.7, s32[]{:T(128)S(6)} %select_n.49), kind=kLoop, calls=%fused_computation.22 | loop fusion | bytes 8388612 | tf_op jit(solution)/shard_map/dynamic_slice | solution.py:282
  5.0 1.4 collective-permute-start.1
  6.4 2.4 %constant_dynamic-slice_fusion.2 = bf16[4,512,1024]{2,1,0:T(8,128)(2,1)} fusion(bf16[8,512,1024]{2,1,0:T(8,128)(2,1)S(1)} %copy-done.5, s32[]{:T(128)S(6)} %select_n.49), kind=kLoop, calls=%fused_computation.21 | loop fusion | bytes 8388612 | tf_op jit(solution)/shard_map/dynamic_slice | solution.py:282
  8.8 1.4 collective-permute-start.2
  10.2 3.0 %collective-permute-done = bf16[4,4,8,128]{3,2,1,0:T(8,128)(2,1)S(1)} collective-permute-done((bf16[4,4,8,128]{3,2,1,0:T(8,128)(2,1)S(1)}, bf16[4,4,8,128]{3,2,1,0:T(8,128)(2,1)S(1)}, u32[]{:S(2)}, u32[]{:S(2)}) %collective-permute-start) | collective-permute-done | bytes 32800 | tf_op jit(solution)/shard_map/ppermute | solution.py:287
  13.9 2.0 %shard_map.73 = bf16[64,64,128]{2,1,0:T(8,128)(2,1)} custom-call(bf16[4,64,128]{2,1,0:T(8,128)(2,1)} %bitcast.47), custom_call_target="tpu_custom_call" | custom-call | tf_op jit(solution)/shard_map/pallas_call | solution.py:298
  15.8 28.2 %all_to_all.10 = bf16[64,64,128]{2,1,0:T(8,128)(2,1)S(1)} all-to-all(bf16[64,64,128]{2,1,0:T(8,128)(2,1)} %shard_map.73), channel_id=1, replica_groups=mesh['zl'=2,'y'=4,'c'=2,'x'=4,'zh'=2] {'zl','y','x','zh'}, dimensions={0} | all-to-all | bytes 2097152 | tf_op jit(solution)/shard_map/all_to_all | solution.py:302
  46.3 2.2 %collective-permute-start.6 = (bf16[4,8,64,128]{3,2,1,0:T(8,128)(2,1)}, bf16[4,8,64,128]{3,2,1,0:T(8,128)(2,1)S(1)}, u32[]{:S(2)}, u32[]{:S(2)}) collective-permute-start(bf16[4,8,64,128]{3,2,1,0:T(8,128)(2,1)} %bitcast.12), channel_id=1, source_target_pairs={{0,6},{2,0},{4,2},{6,4},{1,7},{3,1},{5,3},{7,5},{8,14},{10,8},{12,... | collective-permute-start | bytes 1572872 | tf_op jit(solution)/shard_map/ppermute | solution.py:267
  48.6 9.1 %collective-permute-done.3.qa_ref = bf16[4,8,64,128]{3,2,1,0:T(8,128)(2,1)} collective-permute-done((bf16[4,8,64,128]{3,2,1,0:T(8,128)(2,1)}, bf16[4,8,64,128]{3,2,1,0:T(8,128)(2,1)}, u32[]{:S(2)}, u32[]{:S(2)}) %collective-permute-start.3) | collective-permute-done | bytes 524320 | tf_op jit(solution)/shard_map/ppermute | solution.py:267
  57.7 1.3 collective-permute-start.7
  59.1 2.3 %collective-permute-start.9 = (bf16[4,8,64,128]{3,2,1,0:T(8,128)(2,1)}, bf16[4,8,64,128]{3,2,1,0:T(8,128)(2,1)S(1)}, u32[]{:S(2)}, u32[]{:S(2)}) collective-permute-start(bf16[4,8,64,128]{3,2,1,0:T(8,128)(2,1)} %bitcast.12), channel_id=1, source_target_pairs={{0,4},{2,6},{4,0},{6,2},{1,5},{3,7},{5,1},{7,3},{8,12},{10,14},{12... | collective-permute-start | bytes 1572872 | tf_op jit(solution)/shard_map/ppermute | solution.py:267
  61.4 10.8 %shard_map.75 = (bf16[4,8,72,128]{3,2,1,0:T(8,128)(2,1)S(1)}, bf16[4,8,72,128]{3,2,1,0:T(8,128)(2,1)}) custom-call(s32[4]{0:T(128)S(1)} %add_add_fusion.1.info, s32[8]{0:T(128)S(1)} %copy-done.4, bf16[4,8,64,128]{3,2,1,0:T(8,128)(2,1)} %collective-permute-done.3.qa_ref, bf16[4,8,64,128]{3,2,1,0:T(8,128)(2,1)} %collective-permute-done.4.qb_ref, ...), custom_call_target="tpu_custom_call" | custom-call | flops 2147483648 | bytes 6291456 | tf_op jit(solution)/shard_map/pallas_call | solution.py:139
  73.3 10.7 %shard_map.76 = (bf16[4,8,72,128]{3,2,1,0:T(8,128)(2,1)}, bf16[4,8,72,128]{3,2,1,0:T(8,128)(2,1)}) custom-call(s32[4]{0:T(128)S(1)} %add_add_fusion.2.info, s32[8]{0:T(128)S(1)} %copy-done.4, bf16[4,8,64,128]{3,2,1,0:T(8,128)(2,1)S(1)} %collective-permute-done.6.qa_ref, bf16[4,8,64,128]{3,2,1,0:T(8,128)(2,1)S(1)} %collective-permute-done.7.qb_ref, ...), custom_call_target="tpu_custom_call" | custom-call | flops 2147483648 | bytes 6291456 | tf_op jit(solution)/shard_map/pallas_call | solution.py:139
  84.6 10.7 %shard_map.77 = (bf16[4,8,72,128]{3,2,1,0:T(8,128)(2,1)}, bf16[4,8,72,128]{3,2,1,0:T(8,128)(2,1)}) custom-call(s32[4]{0:T(128)S(1)} %add_add_fusion.3.info, s32[8]{0:T(128)S(1)} %copy-done.4, bf16[4,8,64,128]{3,2,1,0:T(8,128)(2,1)S(1)} %collective-permute-done.9.qa_ref, bf16[4,8,64,128]{3,2,1,0:T(8,128)(2,1)S(1)} %collective-permute-done.10.qb_ref, ...), custom_call_target="tpu_custom_call" | custom-call | flops 2147483648 | bytes 6291456 | tf_op jit(solution)/shard_map/pallas_call | solution.py:139
  95.3 2.3 %collective-permute-start.11 = (bf16[32,72,128]{2,1,0:T(8,128)(2,1)}, bf16[32,72,128]{2,1,0:T(8,128)(2,1)}, u32[]{:S(2)}, u32[]{:S(2)}) collective-permute-start(bf16[32,72,128]{2,1,0:T(8,128)(2,1)} %bitcast.20), channel_id=1, source_target_pairs={{0,4},{2,6},{4,0},{6,2},{1,5},{3,7},{5,1},{7,3},{8,12},{10,14},{12... | collective-permute-start | bytes 1769480 | tf_op jit(solution)/shard_map/ppermute | solution.py:267
  97.7 3.9 %collective-permute-start.12 = (bf16[32,72,128]{2,1,0:T(8,128)(2,1)}, bf16[32,72,128]{2,1,0:T(8,128)(2,1)}, u32[]{:S(2)}, u32[]{:S(2)}) collective-permute-start(bf16[32,72,128]{2,1,0:T(8,128)(2,1)} %bitcast.22), channel_id=1, source_target_pairs={{0,48},{16,0},{32,16},{48,32},{1,49},{17,1},{33,17},{49,33},{2,50}... | collective-permute-start | bytes 1769480 | tf_op jit(solution)/shard_map/ppermute | solution.py:267
  103.7 10.0 %shard_map.74 = (bf16[4,8,72,128]{3,2,1,0:T(8,128)(2,1)S(1)}, bf16[4,8,72,128]{3,2,1,0:T(8,128)(2,1)S(1)}) custom-call(s32[4]{0:T(128)S(1)} %add_add_fusion.info, s32[8]{0:T(128)S(1)} %copy-done.4, bf16[8,8,64,128]{3,2,1,0:T(8,128)(2,1)S(1)} %bitcast.40, bf16[8,8,64,128]{3,2,1,0:T(8,128)(2,1)S(1)} %bitcast.41, bf16[8,512,1024]{2,1,0:T(8,128)(2,1)} %k0_ref.7, ...), custom_call_target="tpu_custom_call" | custom-call | flops 2147483648 | bytes 6291456 | tf_op jit(solution)/shard_map/pallas_call | solution.py:139
  113.7 3.7 %collective-permute-done.12.refs_5_ = bf16[32,72,128]{2,1,0:T(8,128)(2,1)} collective-permute-done((bf16[32,72,128]{2,1,0:T(8,128)(2,1)}, bf16[32,72,128]{2,1,0:T(8,128)(2,1)}, u32[]{:S(2)}, u32[]{:S(2)}) %collective-permute-start.12) | collective-permute-done | bytes 589856 | tf_op jit(solution)/shard_map/ppermute | solution.py:267
  117.4 2.4 %collective-permute-done.13.refs_6_ = bf16[32,72,128]{2,1,0:T(8,128)(2,1)} collective-permute-done((bf16[32,72,128]{2,1,0:T(8,128)(2,1)}, bf16[32,72,128]{2,1,0:T(8,128)(2,1)}, u32[]{:S(2)}, u32[]{:S(2)}) %collective-permute-start.13) | collective-permute-done | bytes 589856 | tf_op jit(solution)/shard_map/ppermute | solution.py:267
  119.8 4.5 %shard_map.78 = bf16[64,72,128]{2,1,0:T(8,128)(2,1)S(1)} custom-call(bf16[32,72,128]{2,1,0:T(8,128)(2,1)S(1)} %bitcast.42, bf16[32,72,128]{2,1,0:T(8,128)(2,1)S(1)} %copy-done.3, bf16[32,72,128]{2,1,0:T(8,128)(2,1)} %collective-permute-done.8.refs_2_, bf16[32,72,128]{2,1,0:T(8,128)(2,1)} %collective-permute-done.11.refs_3_, ...), custom_call_target="tpu_custom_call" | custom-call | flops 4718592 | bytes 5898240 | tf_op jit(solution)/shard_map/pallas_call | solution.py:211
  125.3 8.9 %all-to-all-start.1 = ((bf16[64,72,128]{2,1,0:T(8,128)(2,1)}), bf16[64,72,128]{2,1,0:T(8,128)(2,1)S(1)}, u32[]{:S(2)}, u32[]{:S(2)}) async-start(bf16[64,72,128]{2,1,0:T(8,128)(2,1)} %copy-done.1), calls=%async_computation.1 | async-start | bytes 2359296 | tf_op jit(solution)/shard_map/all_to_all | solution.py:327
  134.2 8.4 %collective-permute-start.15 = (s32[4,8]{1,0:T(4,128)S(1)}, s32[4,8]{1,0:T(4,128)S(1)}, u32[]{:S(2)}, u32[]{:S(2)}) collective-permute-start(s32[4,8]{1,0:T(4,128)S(1)} %get-tuple-element.28), channel_id=1, source_target_pairs={{0,8},{8,0},{1,9},{9,1},{2,10},{10,2},{3,11},{11,3},{4,12},{12,4},... | collective-permute-start | bytes 392 | tf_op jit(solution)/shard_map/ppermute | solution.py:330
  145.7 1.2 fusion.2
  148.6 9.4 %collective-permute-start.16 = (bf16[4,4,8,128]{3,2,1,0:T(8,128)(2,1)S(1)}, bf16[4,4,8,128]{3,2,1,0:T(8,128)(2,1)S(1)}, u32[]{:S(2)}, u32[]{:S(2)}) collective-permute-start(bf16[4,4,8,128]{3,2,1,0:T(8,128)(2,1)S(1)} %get-tuple-element.24), channel_id=1, source_target_pairs={{0,8},{8,0},{1,9},{9,1},{2,10},{10,2},{3,11},{11,3},{4,12},{12,4},... | collective-permute-start | bytes 98312 | tf_op jit(solution)/shard_map/ppermute | solution.py:348
  (60 shorter events, 14.1 us)
Async XLA Ops:
  0.0 143.5 %copy-start = (bf16[1024,1024]{1,0:T(8,128)(2,1)S(1)}, bf16[1024,1024]{1,0:T(8,128)(2,1)}, u32[]{:S(2)}) copy-start(bf16[1024,1024]{1,0:T(8,128)(2,1)} %param.11) | copy-start | bytes 6291460
  0.0 6.4 %copy-start.5 = (bf16[8,512,1024]{2,1,0:T(8,128)(2,1)S(1)}, bf16[8,512,1024]{2,1,0:T(8,128)(2,1)}, u32[]{:S(2)}) copy-start(bf16[8,512,1024]{2,1,0:T(8,128)(2,1)} %v0_ref.7) | copy-start | bytes 25165828
  5.0 5.2 %copy-start.6 = (bf16[8,8,512]{2,1,0:T(8,128)(2,1)S(1)}, bf16[8,8,512]{2,1,0:T(8,128)(2,1)}, u32[]{:S(2)}) copy-start(bf16[8,8,512]{2,1,0:T(8,128)(2,1)} %param.7) | copy-start | bytes 196612
  5.0 56.5 %collective-permute-start.1 = (bf16[4,512,1024]{2,1,0:T(8,128)(2,1)}, bf16[4,512,1024]{2,1,0:T(8,128)(2,1)}, u32[]{:S(2)}, u32[]{:S(2)}) collective-permute-start(bf16[4,512,1024]{2,1,0:T(8,128)(2,1)} %constant_dynamic-slice_fusion.3), channel_id=1, source_target_pairs={{0,8},{8,0},{1,9},{9,1},{2,10},{10,2},{3,11},{11,3},{4,12},{12,4},... | collective-permute-start | bytes 12582920 | tf_op jit(solution)/shard_map/ppermute | solution.py:307
  8.8 52.7 %copy-start.4 = (s32[8]{0:T(128)S(1)}, s32[8]{0:T(128)}, u32[]{:S(2)}) copy-start(s32[8]{0:T(128)} %lengths.7) | copy-start | bytes 100
  8.8 52.7 %collective-permute-start.2 = (bf16[4,512,1024]{2,1,0:T(8,128)(2,1)}, bf16[4,512,1024]{2,1,0:T(8,128)(2,1)}, u32[]{:S(2)}, u32[]{:S(2)}) collective-permute-start(bf16[4,512,1024]{2,1,0:T(8,128)(2,1)} %constant_dynamic-slice_fusion.2), channel_id=1, source_target_pairs={{0,8},{8,0},{1,9},{9,1},{2,10},{10,2},{3,11},{11,3},{4,12},{12,4},... | collective-permute-start | bytes 12582920 | tf_op jit(solution)/shard_map/ppermute | solution.py:308
  10.1 3.1 %collective-permute-start = (bf16[4,4,8,128]{3,2,1,0:T(8,128)(2,1)S(1)}, bf16[4,4,8,128]{3,2,1,0:T(8,128)(2,1)S(1)}, u32[]{:S(2)}, u32[]{:S(2)}) collective-permute-start(bf16[4,4,8,128]{3,2,1,0:T(8,128)(2,1)S(1)} %get-tuple-element.26), channel_id=1, source_target_pairs={{0,8},{8,0},{1,9},{9,1},{2,10},{10,2},{3,11},{11,3},{4,12},{12,4},... | collective-permute-start | bytes 98312 | tf_op jit(solution)/shard_map/ppermute | solution.py:287
  45.1 12.6 %collective-permute-start.3 = (bf16[4,8,64,128]{3,2,1,0:T(8,128)(2,1)}, bf16[4,8,64,128]{3,2,1,0:T(8,128)(2,1)}, u32[]{:S(2)}, u32[]{:S(2)}) collective-permute-start(bf16[4,8,64,128]{3,2,1,0:T(8,128)(2,1)} %bitcast.12), channel_id=1, source_target_pairs={{0,2},{2,4},{4,6},{6,0},{1,3},{3,5},{5,7},{7,1},{8,10},{10,12},{12... | collective-permute-start | bytes 1572872 | tf_op jit(solution)/shard_map/ppermute | solution.py:267
  45.9 13.2 %collective-permute-start.4 = (bf16[4,8,64,128]{3,2,1,0:T(8,128)(2,1)}, bf16[4,8,64,128]{3,2,1,0:T(8,128)(2,1)}, u32[]{:S(2)}, u32[]{:S(2)}) collective-permute-start(bf16[4,8,64,128]{3,2,1,0:T(8,128)(2,1)} %bitcast.13), channel_id=1, source_target_pairs={{0,16},{16,32},{32,48},{48,0},{1,17},{17,33},{33,49},{49,1},{2,18}... | collective-permute-start | bytes 1572872 | tf_op jit(solution)/shard_map/ppermute | solution.py:267
  46.3 27.0 %collective-permute-start.6 = (bf16[4,8,64,128]{3,2,1,0:T(8,128)(2,1)}, bf16[4,8,64,128]{3,2,1,0:T(8,128)(2,1)S(1)}, u32[]{:S(2)}, u32[]{:S(2)}) collective-permute-start(bf16[4,8,64,128]{3,2,1,0:T(8,128)(2,1)} %bitcast.12), channel_id=1, source_target_pairs={{0,6},{2,0},{4,2},{6,4},{1,7},{3,1},{5,3},{7,5},{8,14},{10,8},{12,... | collective-permute-start | bytes 1572872 | tf_op jit(solution)/shard_map/ppermute | solution.py:267
  57.7 15.6 %collective-permute-start.7 = (bf16[4,8,64,128]{3,2,1,0:T(8,128)(2,1)}, bf16[4,8,64,128]{3,2,1,0:T(8,128)(2,1)S(1)}, u32[]{:S(2)}, u32[]{:S(2)}) collective-permute-start(bf16[4,8,64,128]{3,2,1,0:T(8,128)(2,1)} %bitcast.13), channel_id=1, source_target_pairs={{0,48},{16,0},{32,16},{48,32},{1,49},{17,1},{33,17},{49,33},{2,50}... | collective-permute-start | bytes 1572872 | tf_op jit(solution)/shard_map/ppermute | solution.py:267
  59.1 25.5 %collective-permute-start.9 = (bf16[4,8,64,128]{3,2,1,0:T(8,128)(2,1)}, bf16[4,8,64,128]{3,2,1,0:T(8,128)(2,1)S(1)}, u32[]{:S(2)}, u32[]{:S(2)}) collective-permute-start(bf16[4,8,64,128]{3,2,1,0:T(8,128)(2,1)} %bitcast.12), channel_id=1, source_target_pairs={{0,4},{2,6},{4,0},{6,2},{1,5},{3,7},{5,1},{7,3},{8,12},{10,14},{12... | collective-permute-start | bytes 1572872 | tf_op jit(solution)/shard_map/ppermute | solution.py:267
  61.4 23.2 %collective-permute-start.10 = (bf16[4,8,64,128]{3,2,1,0:T(8,128)(2,1)}, bf16[4,8,64,128]{3,2,1,0:T(8,128)(2,1)S(1)}, u32[]{:S(2)}, u32[]{:S(2)}) collective-permute-start(bf16[4,8,64,128]{3,2,1,0:T(8,128)(2,1)} %bitcast.13), channel_id=1, source_target_pairs={{0,32},{16,48},{32,0},{48,16},{1,33},{17,49},{33,1},{49,17},{2,34}... | collective-permute-start | bytes 1572872 | tf_op jit(solution)/shard_map/ppermute | solution.py:267
  72.2 29.4 %collective-permute-start.5 = (bf16[32,72,128]{2,1,0:T(8,128)(2,1)S(1)}, bf16[32,72,128]{2,1,0:T(8,128)(2,1)S(1)}, u32[]{:S(2)}, u32[]{:S(2)}) collective-permute-start(bf16[32,72,128]{2,1,0:T(8,128)(2,1)S(1)} %bitcast.45), channel_id=1, source_target_pairs={{0,6},{2,0},{4,2},{6,4},{1,7},{3,1},{5,3},{7,5},{8,14},{10,8},{12,... | collective-permute-start | bytes 1769480 | tf_op jit(solution)/shard_map/ppermute | solution.py:267
  84.1 29.6 %collective-permute-start.8 = (bf16[32,72,128]{2,1,0:T(8,128)(2,1)}, bf16[32,72,128]{2,1,0:T(8,128)(2,1)}, u32[]{:S(2)}, u32[]{:S(2)}) collective-permute-start(bf16[32,72,128]{2,1,0:T(8,128)(2,1)} %bitcast.17), channel_id=1, source_target_pairs={{0,2},{2,4},{4,6},{6,0},{1,3},{3,5},{5,7},{7,1},{8,10},{10,12},{12... | collective-permute-start | bytes 1769480 | tf_op jit(solution)/shard_map/ppermute | solution.py:267
  95.3 18.4 %collective-permute-start.11 = (bf16[32,72,128]{2,1,0:T(8,128)(2,1)}, bf16[32,72,128]{2,1,0:T(8,128)(2,1)}, u32[]{:S(2)}, u32[]{:S(2)}) collective-permute-start(bf16[32,72,128]{2,1,0:T(8,128)(2,1)} %bitcast.20), channel_id=1, source_target_pairs={{0,4},{2,6},{4,0},{6,2},{1,5},{3,7},{5,1},{7,3},{8,12},{10,14},{12... | collective-permute-start | bytes 1769480 | tf_op jit(solution)/shard_map/ppermute | solution.py:267
  97.7 19.8 %collective-permute-start.12 = (bf16[32,72,128]{2,1,0:T(8,128)(2,1)}, bf16[32,72,128]{2,1,0:T(8,128)(2,1)}, u32[]{:S(2)}, u32[]{:S(2)}) collective-permute-start(bf16[32,72,128]{2,1,0:T(8,128)(2,1)} %bitcast.22), channel_id=1, source_target_pairs={{0,48},{16,0},{32,16},{48,32},{1,49},{17,1},{33,17},{49,33},{2,50}... | collective-permute-start | bytes 1769480 | tf_op jit(solution)/shard_map/ppermute | solution.py:267
  101.6 18.2 %collective-permute-start.13 = (bf16[32,72,128]{2,1,0:T(8,128)(2,1)}, bf16[32,72,128]{2,1,0:T(8,128)(2,1)}, u32[]{:S(2)}, u32[]{:S(2)}) collective-permute-start(bf16[32,72,128]{2,1,0:T(8,128)(2,1)} %bitcast.23), channel_id=1, source_target_pairs={{0,16},{16,32},{32,48},{48,0},{1,17},{17,33},{33,49},{49,1},{2,18}... | collective-permute-start | bytes 1769480 | tf_op jit(solution)/shard_map/ppermute | solution.py:267
  102.4 17.4 %collective-permute-start.14 = (bf16[32,72,128]{2,1,0:T(8,128)(2,1)}, bf16[32,72,128]{2,1,0:T(8,128)(2,1)}, u32[]{:S(2)}, u32[]{:S(2)}) collective-permute-start(bf16[32,72,128]{2,1,0:T(8,128)(2,1)} %bitcast.24), channel_id=1, source_target_pairs={{0,32},{16,48},{32,0},{48,16},{1,33},{17,49},{33,1},{49,17},{2,34}... | collective-permute-start | bytes 1769480 | tf_op jit(solution)/shard_map/ppermute | solution.py:267
  103.7 16.1 %copy-start.3 = (bf16[32,72,128]{2,1,0:T(8,128)(2,1)S(1)}, bf16[32,72,128]{2,1,0:T(8,128)(2,1)}, u32[]{:S(2)}) copy-start(bf16[32,72,128]{2,1,0:T(8,128)(2,1)} %copy-done.2) | copy-start | bytes 1769476
  113.7 20.6 %copy-start.7 = (s32[8,8]{1,0:T(8,128)S(1)}, s32[8,8]{1,0:T(8,128)}, u32[]{:S(2)}) copy-start(s32[8,8]{1,0:T(8,128)} %param.13) | copy-start | bytes 772
  125.3 22.7 %all-to-all-start.1 = ((bf16[64,72,128]{2,1,0:T(8,128)(2,1)}), bf16[64,72,128]{2,1,0:T(8,128)(2,1)S(1)}, u32[]{:S(2)}, u32[]{:S(2)}) async-start(bf16[64,72,128]{2,1,0:T(8,128)(2,1)} %copy-done.1), calls=%async_computation.1 | async-start | bytes 2359296 | tf_op jit(solution)/shard_map/all_to_all | solution.py:327
  134.2 9.2 %collective-permute-start.15 = (s32[4,8]{1,0:T(4,128)S(1)}, s32[4,8]{1,0:T(4,128)S(1)}, u32[]{:S(2)}, u32[]{:S(2)}) collective-permute-start(s32[4,8]{1,0:T(4,128)S(1)} %get-tuple-element.28), channel_id=1, source_target_pairs={{0,8},{8,0},{1,9},{9,1},{2,10},{10,2},{3,11},{11,3},{4,12},{12,4},... | collective-permute-start | bytes 392 | tf_op jit(solution)/shard_map/ppermute | solution.py:330
  148.6 10.3 %collective-permute-start.16 = (bf16[4,4,8,128]{3,2,1,0:T(8,128)(2,1)S(1)}, bf16[4,4,8,128]{3,2,1,0:T(8,128)(2,1)S(1)}, u32[]{:S(2)}, u32[]{:S(2)}) collective-permute-start(bf16[4,4,8,128]{3,2,1,0:T(8,128)(2,1)S(1)} %get-tuple-element.24), channel_id=1, source_target_pairs={{0,8},{8,0},{1,9},{9,1},{2,10},{10,2},{3,11},{11,3},{4,12},{12,4},... | collective-permute-start | bytes 98312 | tf_op jit(solution)/shard_map/ppermute | solution.py:348
  (2 other events, 1.8 us)

commit v4 on v3

--- a/solution.py
+++ b/solution.py
@@ -20,7 +20,7 @@
 DEAD = -(2.0**100)
 ROWS = 64
 META = 8
-PARTS = 2
+PARTS = 4
 
 
 def packed_tiles(first, second):
@@ -41,8 +41,9 @@
 
 
 def partial_kernel(
-    info, lengths, qa_ref, qb_ref, k0_ref, k1_ref, v0_ref, v1_ref, oa_ref, ob_ref
+    info, lengths, qa_ref, qb_ref, k0_ref, k1_ref, v0_ref, v1_ref, *rest
 ):
+    oa_ref, ob_ref = rest[-2:]
     length = k0_ref.shape[1]
     leads, heads = qa_ref.shape[:2]
     width = 2 * leads * ROWS
@@ -115,53 +116,53 @@
     pl.when(jnp.logical_not(live))(lambda: run(True))
 
 
-def partials(info, lengths, qa, qb, k0, k1, v0, v1):
-    same = qa is qb
-    lead, heads = qa.shape[0] // (2 if same else 1), qa.shape[1]
+def partials(info, lengths, qa, qb, k0, k1, v0, v1, parts=(0, PARTS), into=()):
+    lead, heads = qa.shape[:2]
     length = k0.shape[1]
     share = heads // PARTS
     cache = (1, length, share * HD)
+    begin, steps = parts
 
     def mine(p, info, lengths):
-        return (info[0], 0, p)
+        return (info[0], 0, begin + p)
 
     def other(p, info, lengths):
-        return (info[1], 0, p)
-
-    def first(p, info, lengths):
-        return (0, p, 0, 0)
-
-    def second(p, info, lengths):
-        return (1 if same else 0, p, 0, 0)
+        return (info[1], 0, begin + p)
+
+    def heads_at(p, info, lengths):
+        return (0, begin + p, 0, 0)
 
     out = jax.ShapeDtypeStruct((lead, heads, ROWS + META, HD), jnp.bfloat16)
-    block = pl.BlockSpec((lead, share, ROWS + META, HD), first)
+    asked = pl.BlockSpec((lead, share, ROWS, HD), heads_at)
+    block = pl.BlockSpec((lead, share, ROWS + META, HD), heads_at)
     return pl.pallas_call(
         partial_kernel,
         grid_spec=pltpu.PrefetchScalarGridSpec(
             num_scalar_prefetch=2,
-            grid=(PARTS,),
+            grid=(steps,),
             in_specs=[
-                pl.BlockSpec((lead, share, ROWS, HD), first),
-                pl.BlockSpec((lead, share, ROWS, HD), second),
+                asked,
+                asked,
                 pl.BlockSpec(cache, mine),
                 pl.BlockSpec(cache, other),
                 pl.BlockSpec(cache, mine),
                 pl.BlockSpec(cache, other),
-            ],
+            ]
+            + [pl.BlockSpec(memory_space=pl.ANY)] * len(into),
             out_specs=[block, block],
         ),
         out_shape=[out, out],
+        input_output_aliases={8 + i: i for i in range(len(into))},
         compiler_params=pltpu.CompilerParams(
             dimension_semantics=("arbitrary",),
-            vmem_limit_bytes=40 << 20,
+            vmem_limit_bytes=60 << 20,
         ),
         cost_estimate=pl.CostEstimate(
-            flops=16 * heads * lead * ROWS * HD * length,
-            bytes_accessed=8 * length * heads * HD + 8 * lead * heads * ROWS * HD,
-            transcendentals=4 * heads * lead * ROWS * length,
-        ),
-    )(info, lengths, qa, qb, k0, k1, v0, v1)
+            flops=16 * share * steps * lead * ROWS * HD * length,
+            bytes_accessed=8 * length * share * steps * HD,
+            transcendentals=4 * share * steps * lead * ROWS * length,
+        ),
+    )(info, lengths, qa, qb, k0, k1, v0, v1, *into)
 
 
 def stats_of(notes, low):
@@ -215,7 +216,7 @@
         out_specs=pl.BlockSpec(block, lambda i: (i, 0, 0)),
         out_shape=jax.ShapeDtypeStruct((2 * count, rows, HD), jnp.bfloat16),
         compiler_params=pltpu.CompilerParams(
-            dimension_semantics=("arbitrary",), vmem_limit_bytes=40 << 20
+            dimension_semantics=("arbitrary",), vmem_limit_bytes=60 << 20
         ),
         cost_estimate=pl.CostEstimate(
             flops=16 * left[0].size, bytes_accessed=20 * left[0].size, transcendentals=0
@@ -284,7 +285,10 @@
 
     q = queries.reshape(users, beams, GROUP, HD).transpose(0, 2, 1, 3)
     q_mine, q_give = halves(q)
+    t_mine, t_give = halves(token_ids)
+    q_give, t_give, key_source = lax.optimization_barrier((q_give, t_give, key_cache))
     q_chip = jnp.concatenate([q_mine, swap(q_give)], axis=2).reshape(half, ROWS, HD)
+    tokens = jnp.concatenate([t_mine, swap(t_give)], axis=1)
 
     holders = [
         (a + b + 2 * h + l) % half
@@ -298,36 +302,51 @@
     operand = pl.pallas_call(
         functools.partial(spread_kernel, holders),
         out_shape=jax.ShapeDtypeStruct((chips, ROWS, HD), jnp.bfloat16),
+        compiler_params=pltpu.CompilerParams(vmem_limit_bytes=60 << 20),
     )(q_chip)
+    operand, value_source = lax.optimization_barrier((operand, value_cache))
     got = lax.all_to_all(operand, CHIPS, 0, 0, tiled=True)
     got = got.reshape(chips // KH, KH, ROWS, HD)
     lead = chips // KH // 2
     got_a, got_b = got[:lead], got[lead:]
 
-    k_other = swap(halves(key_cache)[1])
-    v_other = swap(halves(value_cache)[1])
+    k_other = swap(halves(key_source)[1])
+    v_other = swap(halves(value_source)[1])
+    got_a, got_b, k_other, v_other = lax.optimization_barrier(
+        (got_a, got_b, k_other, v_other)
+    )
 
     offset = (row * KH + col) * length
     other = ((row + 1 - 2 * c) * KH + col) * length
 
-    def computed(step, qa, qb):
+    def computed(step, qa, qb, **kept):
         user = (held - step) % half
         info = jnp.stack([c * half + user, user, offset, other]).astype(jnp.int32)
-        return partials(info, lengths, qa, qb, key_cache, k_other, value_cache, v_other)
-
+        return partials(
+            info, lengths, qa, qb, key_cache, k_other, value_cache, v_other, **kept
+        )
+
+    def flat(parts):
+        return [p.reshape(-1, ROWS + META, HD) for p in parts]
+
+    near = [(moved(got_a, "x", s), moved(got_b, "y", s)) for s in (1, -1)]
+    begun = computed(0, got_a, got_b, parts=(0, PARTS // 2))
+    near, begun, far_a, far_b = lax.optimization_barrier((near, begun, got_a, got_b))
+    asked = {1: near[0], -1: near[1], 2: (moved(far_a, "x", 2), moved(far_b, "y", 2))}
     left, right = [], []
-    for step in (0, 1, -1, 2):
-        if step:
-            parts = computed(step, moved(got_a, "x", step), moved(got_b, "y", step))
-        else:
-            parts = computed(0, got, got)
-        one, two = (p.reshape(-1, ROWS + META, HD) for p in parts)
-        left.append(moved(one, "x", -step) if step else one)
-        right.append(moved(two, "y", -step) if step else two)
+    for step, (qa, qb) in asked.items():
+        parts = computed(step, qa, qb)
+        one, two = flat(parts)
+        left.append(moved(one, "x", -step))
+        right.append(moved(two, "y", -step))
+    begun, _ = lax.optimization_barrier((begun, parts))
+    one, two = flat(
+        computed(0, got_a, got_b, parts=(PARTS // 2, PARTS - PARTS // 2), into=begun)
+    )
+    left.append(one)
+    right.append(two)
     arrived = lax.all_to_all(merged(left, right), CHIPS, 0, 0, tiled=True)
 
-    t_mine, t_give = halves(token_ids)
-    tokens = jnp.concatenate([t_mine, swap(t_give)], axis=1)
     codes = jnp.arange(key_table.shape[0], dtype=jnp.int32)
     onehot = (tokens[..., None] == codes).astype(jnp.bfloat16)
     keys = lax.dynamic_slice_in_dim(key_table, col * HD, HD, 1)

time: 160 us -> 148 us (0.925)
  waiting for transfers between devices: 20.8 us -> 10.3 us
  starting transfers between devices: 45.5 us -> 35.9 us
  Pallas kernels: 49.2 us -> 56.2 us
  other arithmetic: 1.78 us -> 3.41 us
    ppermute x12, waiting for transfers between devices: 15.2 us -> 4.95 us  [moved(): lax.ppermute(array, axis, [(i, (i + step) % count) for i in range(count)])]
    pallas_call x4 -> x5, Pallas kernels: 42.2 us -> 48 us  [partials(): pl.pallas_call(partial_kernel, grid_spec=pltpu.PrefetchScalarGridSpec(num...]
    all_to_all x1, starting transfers between devices: 8.9 us -> 5.49 us  [body(): arrived = lax.all_to_all(merged(left, right), CHIPS, 0, 0, tiled=True)]
    ppermute x1, waiting for transfers between devices: 3.03 us -> 0.01 us  [body(): swap(q_give)]
    all_to_all x1, waiting for transfers between devices: 0.83 us -> 3.71 us  [body(): arrived = lax.all_to_all(merged(left, right), CHIPS, 0, 0, tiled=True)]
    ppermute x1, starting transfers between devices: 9.41 us -> 6.62 us  [body(): received = swap(result[:, :, beams:])]
    ppermute x1, starting transfers between devices: 8.37 us -> 5.87 us  [body(): tokens = jnp.concatenate([t_mine, swap(t_give)], axis=1)]
    ppermute x2, starting transfers between devices: 2.77 us -> 0.59 us  [the longest x1 0.59 us: body(): v_other = swap(halves(value_source)[1])]
  transfers between devices with their start and end apart: 18 -> 18, of which waited for: 7 -> 5; matrix products, arithmetic and copies ran while one was open for 5% -> 9% of each run, Pallas kernels for 28% -> 34%
where the time goes in v4:
time: 148 us; the launch traced here: 147 us
  Pallas kernels  56.2 us (38%)
  starting transfers between devices  35.9 us (24%)
  blocking collectives  28.5 us (19%)
  local copies, waits for them, and re-layouts  11.2 us (8%)
  waiting for transfers between devices  10.3 us (7%)
  other arithmetic  3.41 us (2%)
    pallas_call x5, Pallas kernels, partials(): pl.pallas_call(partial_kernel, grid_spec=pltpu.PrefetchScalarGridSpec(num...  48 us
    all_to_all x1, blocking collectives, body(): got = lax.all_to_all(operand, CHIPS, 0, 0, tiled=True)  28.5 us
    ppermute x12, starting transfers between devices, moved(): lax.ppermute(array, axis, [(i, (i + step) % count) for i in range(count)])  15.9 us
    dynamic_slice x2, local copies, waits for them, and re-layouts, halves(): lax.dynamic_slice_in_dim(array, (1 - c) * half, half, 0)  7.35 us
    ppermute x1, starting transfers between devices, body(): received = swap(result[:, :, beams:])  6.62 us
    ppermute x1, starting transfers between devices, body(): tokens = jnp.concatenate([t_mine, swap(t_give)], axis=1)  5.87 us
    pallas_call x1, Pallas kernels, merged(): pl.pallas_call(merge_kernel, grid=(2 * steps,), in_specs=[ahead] * len(le...  5.64 us
    all_to_all x1, starting transfers between devices, body(): arrived = lax.all_to_all(merged(left, right), CHIPS, 0, 0, tiled=True)  5.49 us
  transfers between devices with their start and end apart: 18, of which 5 were waited for; matrix products, arithmetic and copies ran while one was open for 9% of the time, Pallas kernels for 34%

profile of v4, /device:TPU:1, one launch (start us, length us, event | category | flops | bytes accessed | tf_op | source)
XLA Modules:
  0.0 147.2 jit_solution(3142896566853913352)
XLA Ops:
  1.7 1.4 collective-permute-start
  3.1 4.6 %constant_dynamic-slice_fusion.2 = bf16[4,512,1024]{2,1,0:T(8,128)(2,1)} fusion(bf16[8,512,1024]{2,1,0:T(8,128)(2,1)} %k0_ref.9, s32[]{:T(128)S(6)} %select_n.51), kind=kLoop, calls=%fused_computation.21 | loop fusion | bytes 8388612 | tf_op jit(solution)/shard_map/dynamic_slice | solution.py:283
  8.4 2.0 %shard_map.73 = bf16[64,64,128]{2,1,0:T(8,128)(2,1)} custom-call(bf16[4,64,128]{2,1,0:T(8,128)(2,1)} %bitcast.53), custom_call_target="tpu_custom_call" | custom-call | tf_op jit(solution)/shard_map/pallas_call | solution.py:302
  10.4 2.7 %constant_dynamic-slice_fusion.1 = bf16[4,512,1024]{2,1,0:T(8,128)(2,1)S(1)} fusion(bf16[8,512,1024]{2,1,0:T(8,128)(2,1)} %v0_ref.9, s32[]{:T(128)S(6)} %select_n.51), kind=kLoop, calls=%fused_computation.20 | loop fusion | bytes 8388612 | tf_op jit(solution)/shard_map/dynamic_slice | solution.py:283
  13.7 28.5 %all_to_all.10 = bf16[64,64,128]{2,1,0:T(8,128)(2,1)S(1)} all-to-all(bf16[64,64,128]{2,1,0:T(8,128)(2,1)S(1)} %copy-done.3), channel_id=1, replica_groups=mesh['zl'=2,'y'=4,'c'=2,'x'=4,'zh'=2] {'zl','y','x','zh'}, dimensions={0} | all-to-all | bytes 2097152 | tf_op jit(solution)/shard_map/all_to_all | solution.py:308
  43.4 2.2 %collective-permute-start.5 = (bf16[4,8,64,128]{3,2,1,0:T(8,128)(2,1)S(1)}, bf16[4,8,64,128]{3,2,1,0:T(8,128)(2,1)}, u32[]{:S(2)}, u32[]{:S(2)}) collective-permute-start(bf16[4,8,64,128]{3,2,1,0:T(8,128)(2,1)S(1)} %bitcast.46), channel_id=1, source_target_pairs={{0,6},{2,0},{4,2},{6,4},{1,7},{3,1},{5,3},{7,5},{8,14},{10,8},{12,... | collective-permute-start | bytes 1572872 | tf_op jit(solution)/shard_map/ppermute | solution.py:268
  45.6 2.2 %collective-permute-start.6 = (bf16[4,8,64,128]{3,2,1,0:T(8,128)(2,1)S(1)}, bf16[4,8,64,128]{3,2,1,0:T(8,128)(2,1)}, u32[]{:S(2)}, u32[]{:S(2)}) collective-permute-start(bf16[4,8,64,128]{3,2,1,0:T(8,128)(2,1)S(1)} %bitcast.41), channel_id=1, source_target_pairs={{0,48},{16,0},{32,16},{48,32},{1,49},{17,1},{33,17},{49,33},{2,50}... | collective-permute-start | bytes 1572872 | tf_op jit(solution)/shard_map/ppermute | solution.py:268
  49.1 7.0 %shard_map.74 = (bf16[4,8,72,128]{3,2,1,0:T(8,128)(2,1)}, bf16[4,8,72,128]{3,2,1,0:T(8,128)(2,1)}) custom-call(s32[4]{0:T(128)} %get-tuple-element.72.info, s32[8]{0:T(128)} %lengths.9, bf16[4,8,64,128]{3,2,1,0:T(8,128)(2,1)} %bitcast.47, bf16[4,8,64,128]{3,2,1,0:T(8,128)(2,1)} %bitcast.42, bf16[8,512,1024]{2,1,0:T(8,128)(2,1)} %k0_ref.9, ...), custom_call_target="tpu_custom_call" | custom-call | flops 1073741824 | bytes 2097152 | tf_op jit(solution)/shard_map/pallas_call | solution.py:138
  56.5 2.1 %collective-permute-start.10 = (bf16[4,8,64,128]{3,2,1,0:T(8,128)(2,1)}, bf16[4,8,64,128]{3,2,1,0:T(8,128)(2,1)}, u32[]{:S(2)}, u32[]{:S(2)}) collective-permute-start(bf16[4,8,64,128]{3,2,1,0:T(8,128)(2,1)} %bitcast.43), channel_id=1, source_target_pairs={{0,32},{16,48},{32,0},{48,16},{1,33},{17,49},{33,1},{49,17},{2,34}... | collective-permute-start | bytes 1572872 | tf_op jit(solution)/shard_map/ppermute | solution.py:268
  58.6 1.7 %collective-permute-start.9 = (bf16[4,8,64,128]{3,2,1,0:T(8,128)(2,1)}, bf16[4,8,64,128]{3,2,1,0:T(8,128)(2,1)}, u32[]{:S(2)}, u32[]{:S(2)}) collective-permute-start(bf16[4,8,64,128]{3,2,1,0:T(8,128)(2,1)} %bitcast.48), channel_id=1, source_target_pairs={{0,4},{2,6},{4,0},{6,2},{1,5},{3,7},{5,1},{7,3},{8,12},{10,14},{12... | collective-permute-start | bytes 1572872 | tf_op jit(solution)/shard_map/ppermute | solution.py:268
  60.3 11.4 %shard_map.76 = (bf16[4,8,72,128]{3,2,1,0:T(8,128)(2,1)}, bf16[4,8,72,128]{3,2,1,0:T(8,128)(2,1)}) custom-call(s32[4]{0:T(128)} %add_add_fusion.2.info, s32[8]{0:T(128)} %lengths.9, bf16[4,8,64,128]{3,2,1,0:T(8,128)(2,1)} %collective-permute-done.5.qa_ref, bf16[4,8,64,128]{3,2,1,0:T(8,128)(2,1)} %collective-permute-done.6.qb_ref, ...), custom_call_target="tpu_custom_call" | custom-call | flops 2147483648 | bytes 4194304 | tf_op jit(solution)/shard_map/pallas_call | solution.py:138
  71.6 1.8 %collective-permute-start.13 = (bf16[32,72,128]{2,1,0:T(8,128)(2,1)}, bf16[32,72,128]{2,1,0:T(8,128)(2,1)S(1)}, u32[]{:S(2)}, u32[]{:S(2)}) collective-permute-start(bf16[32,72,128]{2,1,0:T(8,128)(2,1)} %bitcast.57), channel_id=1, source_target_pairs={{0,16},{16,32},{32,48},{48,0},{1,17},{17,33},{33,49},{49,1},{2,18}... | collective-permute-start | bytes 1769480 | tf_op jit(solution)/shard_map/ppermute | solution.py:268
  74.6 11.4 %shard_map.75 = (bf16[4,8,72,128]{3,2,1,0:T(8,128)(2,1)}, bf16[4,8,72,128]{3,2,1,0:T(8,128)(2,1)}) custom-call(s32[4]{0:T(128)} %get-tuple-element.71.info, s32[8]{0:T(128)} %lengths.9, bf16[4,8,64,128]{3,2,1,0:T(8,128)(2,1)} %collective-permute-done.3.qa_ref, bf16[4,8,64,128]{3,2,1,0:T(8,128)(2,1)} %collective-permute-done.4.qb_ref, ...), custom_call_target="tpu_custom_call" | custom-call | flops 2147483648 | bytes 4194304 | tf_op jit(solution)/shard_map/pallas_call | solution.py:138
  86.8 2.5 %collective-permute-start.7 = (bf16[32,72,128]{2,1,0:T(8,128)(2,1)}, bf16[32,72,128]{2,1,0:T(8,128)(2,1)}, u32[]{:S(2)}, u32[]{:S(2)}) collective-permute-start(bf16[32,72,128]{2,1,0:T(8,128)(2,1)} %bitcast.58), channel_id=1, source_target_pairs={{0,6},{2,0},{4,2},{6,4},{1,7},{3,1},{5,3},{7,5},{8,14},{10,8},{12,... | collective-permute-start | bytes 1769480 | tf_op jit(solution)/shard_map/ppermute | solution.py:268
  89.3 11.3 %shard_map.77 = (bf16[4,8,72,128]{3,2,1,0:T(8,128)(2,1)}, bf16[4,8,72,128]{3,2,1,0:T(8,128)(2,1)}) custom-call(s32[4]{0:T(128)} %add_add_fusion.3.info, s32[8]{0:T(128)} %lengths.9, bf16[4,8,64,128]{3,2,1,0:T(8,128)(2,1)} %collective-permute-done.9.qa_ref, bf16[4,8,64,128]{3,2,1,0:T(8,128)(2,1)} %collective-permute-done.10.qb_ref, ...), custom_call_target="tpu_custom_call" | custom-call | flops 2147483648 | bytes 4194304 | tf_op jit(solution)/shard_map/pallas_call | solution.py:138
  101.7 7.0 %shard_map.78 = (bf16[4,8,72,128]{3,2,1,0:T(8,128)(2,1)}, bf16[4,8,72,128]{3,2,1,0:T(8,128)(2,1)}) custom-call(s32[4]{0:T(128)} %get-tuple-element.72.info, s32[8]{0:T(128)} %lengths.9, bf16[4,8,64,128]{3,2,1,0:T(8,128)(2,1)} %bitcast.49, bf16[4,8,64,128]{3,2,1,0:T(8,128)(2,1)} %bitcast.44, ...), custom_call_target="tpu_custom_call", output_to_operand_aliasing={{0}: (8, {}), {1}: (9, {})} | custom-call | flops 1073741824 | bytes 2097152 | tf_op jit(solution)/shard_map/pallas_call | solution.py:138
  108.7 4.5 %collective-permute-done.11.refs_2_ = bf16[32,72,128]{2,1,0:T(8,128)(2,1)} collective-permute-done((bf16[32,72,128]{2,1,0:T(8,128)(2,1)}, bf16[32,72,128]{2,1,0:T(8,128)(2,1)}, u32[]{:S(2)}, u32[]{:S(2)}) %collective-permute-start.11) | collective-permute-done | bytes 589856 | tf_op jit(solution)/shard_map/ppermute | solution.py:268
  113.2 5.6 %shard_map.79 = bf16[64,72,128]{2,1,0:T(8,128)(2,1)} custom-call(bf16[32,72,128]{2,1,0:T(8,128)(2,1)} %collective-permute-done.7.refs_0_, bf16[32,72,128]{2,1,0:T(8,128)(2,1)} %copy-done.5, bf16[32,72,128]{2,1,0:T(8,128)(2,1)} %collective-permute-done.11.refs_2_, bf16[32,72,128]{2,1,0:T(8,128)(2,1)} %bitcast.50, ...), custom_call_target="tpu_custom_call" | custom-call | flops 4718592 | bytes 5898240 | tf_op jit(solution)/shard_map/pallas_call | solution.py:212
  118.9 5.5 %all-to-all-start.1 = ((bf16[64,72,128]{2,1,0:T(8,128)(2,1)}), bf16[64,72,128]{2,1,0:T(8,128)(2,1)S(1)}, u32[]{:S(2)}, u32[]{:S(2)}) async-start(bf16[64,72,128]{2,1,0:T(8,128)(2,1)} %shard_map.79), calls=%async_computation.1 | async-start | bytes 2359296 | tf_op jit(solution)/shard_map/all_to_all | solution.py:348
  124.4 5.9 %collective-permute-start.15 = (s32[4,8]{1,0:T(4,128)S(1)}, s32[4,8]{1,0:T(4,128)S(1)}, u32[]{:S(2)}, u32[]{:S(2)}) collective-permute-start(s32[4,8]{1,0:T(4,128)S(1)} %get-tuple-element.62), channel_id=1, source_target_pairs={{0,8},{8,0},{1,9},{9,1},{2,10},{10,2},{3,11},{11,3},{4,12},{12,4},... | collective-permute-start | bytes 392 | tf_op jit(solution)/shard_map/ppermute | solution.py:291
  132.2 1.1 copy.12.value_ref
  133.3 1.2 fusion.2
  134.8 3.7 %all-to-all-done.1.x_ref = bf16[64,72,128]{2,1,0:T(8,128)(2,1)S(1)} async-done(((bf16[64,72,128]{2,1,0:T(8,128)(2,1)}), bf16[64,72,128]{2,1,0:T(8,128)(2,1)S(1)}, u32[]{:S(2)}, u32[]{:S(2)}) %all-to-all-start.1) | async-done | bytes 1179680 | tf_op jit(solution)/shard_map/all_to_all | solution.py:348
  139.1 6.6 %collective-permute-start.16 = (bf16[4,4,8,128]{3,2,1,0:T(8,128)(2,1)S(1)}, bf16[4,4,8,128]{3,2,1,0:T(8,128)(2,1)S(1)}, u32[]{:S(2)}, u32[]{:S(2)}) collective-permute-start(bf16[4,4,8,128]{3,2,1,0:T(8,128)(2,1)S(1)} %get-tuple-element.66), channel_id=1, source_target_pairs={{0,8},{8,0},{1,9},{9,1},{2,10},{10,2},{3,11},{11,3},{4,12},{12,4},... | collective-permute-start | bytes 98312 | tf_op jit(solution)/shard_map/ppermute | solution.py:367
  (56 shorter events, 13.3 us)
Async XLA Ops:
  0.0 131.1 %copy-start = (bf16[1024,1024]{1,0:T(8,128)(2,1)S(1)}, bf16[1024,1024]{1,0:T(8,128)(2,1)}, u32[]{:S(2)}) copy-start(bf16[1024,1024]{1,0:T(8,128)(2,1)} %param.11) | copy-start | bytes 6291460
  1.7 6.1 %collective-permute-start = (bf16[4,4,8,128]{3,2,1,0:T(8,128)(2,1)S(1)}, bf16[4,4,8,128]{3,2,1,0:T(8,128)(2,1)S(1)}, u32[]{:S(2)}, u32[]{:S(2)}) collective-permute-start(bf16[4,4,8,128]{3,2,1,0:T(8,128)(2,1)S(1)} %get-tuple-element.34), channel_id=1, source_target_pairs={{0,8},{8,0},{1,9},{9,1},{2,10},{10,2},{3,11},{11,3},{4,12},{12,4},... | collective-permute-start | bytes 98312 | tf_op jit(solution)/shard_map/ppermute | solution.py:290
  7.8 34.5 %collective-permute-start.1 = (bf16[4,512,1024]{2,1,0:T(8,128)(2,1)}, bf16[4,512,1024]{2,1,0:T(8,128)(2,1)}, u32[]{:S(2)}, u32[]{:S(2)}) collective-permute-start(bf16[4,512,1024]{2,1,0:T(8,128)(2,1)} %constant_dynamic-slice_fusion.2), channel_id=1, source_target_pairs={{0,8},{8,0},{1,9},{9,1},{2,10},{10,2},{3,11},{11,3},{4,12},{12,4},... | collective-permute-start | bytes 12582920 | tf_op jit(solution)/shard_map/ppermute | solution.py:313
  10.4 3.3 %copy-start.3 = (bf16[64,64,128]{2,1,0:T(8,128)(2,1)S(1)}, bf16[64,64,128]{2,1,0:T(8,128)(2,1)}, u32[]{:S(2)}) copy-start(bf16[64,64,128]{2,1,0:T(8,128)(2,1)} %shard_map.73) | copy-start | bytes 3145732
  13.1 29.2 %collective-permute-start.2 = (bf16[4,512,1024]{2,1,0:T(8,128)(2,1)S(1)}, bf16[4,512,1024]{2,1,0:T(8,128)(2,1)}, u32[]{:S(2)}, u32[]{:S(2)}) collective-permute-start(bf16[4,512,1024]{2,1,0:T(8,128)(2,1)S(1)} %constant_dynamic-slice_fusion.1), channel_id=1, source_target_pairs={{0,8},{8,0},{1,9},{9,1},{2,10},{10,2},{3,11},{11,3},{4,12},{12,4},... | collective-permute-start | bytes 12582920 | tf_op jit(solution)/shard_map/ppermute | solution.py:314
  42.3 6.8 %copy-start.1 = (bf16[32,64,128]{2,1,0:T(8,128)(2,1)}, bf16[32,64,128]{2,1,0:T(8,128)(2,1)S(1)}, u32[]{:S(2)}) copy-start(bf16[32,64,128]{2,1,0:T(8,128)(2,1)S(1)} %get-tuple-element.63) | copy-start | bytes 1572868
  42.3 6.8 %copy-start.2 = (bf16[32,64,128]{2,1,0:T(8,128)(2,1)}, bf16[32,64,128]{2,1,0:T(8,128)(2,1)S(1)}, u32[]{:S(2)}) copy-start(bf16[32,64,128]{2,1,0:T(8,128)(2,1)S(1)} %get-tuple-element.64) | copy-start | bytes 1572868
  42.3 13.7 %collective-permute-start.3 = (bf16[4,8,64,128]{3,2,1,0:T(8,128)(2,1)S(1)}, bf16[4,8,64,128]{3,2,1,0:T(8,128)(2,1)}, u32[]{:S(2)}, u32[]{:S(2)}) collective-permute-start(bf16[4,8,64,128]{3,2,1,0:T(8,128)(2,1)S(1)} %bitcast.45), channel_id=1, source_target_pairs={{0,2},{2,4},{4,6},{6,0},{1,3},{3,5},{5,7},{7,1},{8,10},{10,12},{12... | collective-permute-start | bytes 1572872 | tf_op jit(solution)/shard_map/ppermute | solution.py:268
  43.0 13.1 %collective-permute-start.4 = (bf16[4,8,64,128]{3,2,1,0:T(8,128)(2,1)S(1)}, bf16[4,8,64,128]{3,2,1,0:T(8,128)(2,1)}, u32[]{:S(2)}, u32[]{:S(2)}) collective-permute-start(bf16[4,8,64,128]{3,2,1,0:T(8,128)(2,1)S(1)} %bitcast.40), channel_id=1, source_target_pairs={{0,16},{16,32},{32,48},{48,0},{1,17},{17,33},{33,49},{49,1},{2,18}... | collective-permute-start | bytes 1572872 | tf_op jit(solution)/shard_map/ppermute | solution.py:268
  43.4 12.7 %collective-permute-start.5 = (bf16[4,8,64,128]{3,2,1,0:T(8,128)(2,1)S(1)}, bf16[4,8,64,128]{3,2,1,0:T(8,128)(2,1)}, u32[]{:S(2)}, u32[]{:S(2)}) collective-permute-start(bf16[4,8,64,128]{3,2,1,0:T(8,128)(2,1)S(1)} %bitcast.46), channel_id=1, source_target_pairs={{0,6},{2,0},{4,2},{6,4},{1,7},{3,1},{5,3},{7,5},{8,14},{10,8},{12,... | collective-permute-start | bytes 1572872 | tf_op jit(solution)/shard_map/ppermute | solution.py:268
  45.6 10.9 %collective-permute-start.6 = (bf16[4,8,64,128]{3,2,1,0:T(8,128)(2,1)S(1)}, bf16[4,8,64,128]{3,2,1,0:T(8,128)(2,1)}, u32[]{:S(2)}, u32[]{:S(2)}) collective-permute-start(bf16[4,8,64,128]{3,2,1,0:T(8,128)(2,1)S(1)} %bitcast.41), channel_id=1, source_target_pairs={{0,48},{16,0},{32,16},{48,32},{1,49},{17,1},{33,17},{49,33},{2,50}... | collective-permute-start | bytes 1572872 | tf_op jit(solution)/shard_map/ppermute | solution.py:268
  56.5 30.3 %collective-permute-start.10 = (bf16[4,8,64,128]{3,2,1,0:T(8,128)(2,1)}, bf16[4,8,64,128]{3,2,1,0:T(8,128)(2,1)}, u32[]{:S(2)}, u32[]{:S(2)}) collective-permute-start(bf16[4,8,64,128]{3,2,1,0:T(8,128)(2,1)} %bitcast.43), channel_id=1, source_target_pairs={{0,32},{16,48},{32,0},{48,16},{1,33},{17,49},{33,1},{49,17},{2,34}... | collective-permute-start | bytes 1572872 | tf_op jit(solution)/shard_map/ppermute | solution.py:268
  58.6 30.8 %collective-permute-start.9 = (bf16[4,8,64,128]{3,2,1,0:T(8,128)(2,1)}, bf16[4,8,64,128]{3,2,1,0:T(8,128)(2,1)}, u32[]{:S(2)}, u32[]{:S(2)}) collective-permute-start(bf16[4,8,64,128]{3,2,1,0:T(8,128)(2,1)} %bitcast.48), channel_id=1, source_target_pairs={{0,4},{2,6},{4,0},{6,2},{1,5},{3,7},{5,1},{7,3},{8,12},{10,14},{12... | collective-permute-start | bytes 1572872 | tf_op jit(solution)/shard_map/ppermute | solution.py:268
  71.6 29.1 %collective-permute-start.13 = (bf16[32,72,128]{2,1,0:T(8,128)(2,1)}, bf16[32,72,128]{2,1,0:T(8,128)(2,1)S(1)}, u32[]{:S(2)}, u32[]{:S(2)}) collective-permute-start(bf16[32,72,128]{2,1,0:T(8,128)(2,1)} %bitcast.57), channel_id=1, source_target_pairs={{0,16},{16,32},{32,48},{48,0},{1,17},{17,33},{33,49},{49,1},{2,18}... | collective-permute-start | bytes 1769480 | tf_op jit(solution)/shard_map/ppermute | solution.py:268
  74.0 34.7 %collective-permute-start.8 = (bf16[32,72,128]{2,1,0:T(8,128)(2,1)}, bf16[32,72,128]{2,1,0:T(8,128)(2,1)S(1)}, u32[]{:S(2)}, u32[]{:S(2)}) collective-permute-start(bf16[32,72,128]{2,1,0:T(8,128)(2,1)} %bitcast.56), channel_id=1, source_target_pairs={{0,2},{2,4},{4,6},{6,0},{1,3},{3,5},{5,7},{7,1},{8,10},{10,12},{12... | collective-permute-start | bytes 1769480 | tf_op jit(solution)/shard_map/ppermute | solution.py:268
  86.0 22.7 %collective-permute-start.12 = (bf16[32,72,128]{2,1,0:T(8,128)(2,1)}, bf16[32,72,128]{2,1,0:T(8,128)(2,1)}, u32[]{:S(2)}, u32[]{:S(2)}) collective-permute-start(bf16[32,72,128]{2,1,0:T(8,128)(2,1)} %bitcast.59), channel_id=1, source_target_pairs={{0,48},{16,0},{32,16},{48,32},{1,49},{17,1},{33,17},{49,33},{2,50}... | collective-permute-start | bytes 1769480 | tf_op jit(solution)/shard_map/ppermute | solution.py:268
  86.8 21.8 %collective-permute-start.7 = (bf16[32,72,128]{2,1,0:T(8,128)(2,1)}, bf16[32,72,128]{2,1,0:T(8,128)(2,1)}, u32[]{:S(2)}, u32[]{:S(2)}) collective-permute-start(bf16[32,72,128]{2,1,0:T(8,128)(2,1)} %bitcast.58), channel_id=1, source_target_pairs={{0,6},{2,0},{4,2},{6,4},{1,7},{3,1},{5,3},{7,5},{8,14},{10,8},{12,... | collective-permute-start | bytes 1769480 | tf_op jit(solution)/shard_map/ppermute | solution.py:268
  100.7 12.6 %collective-permute-start.11 = (bf16[32,72,128]{2,1,0:T(8,128)(2,1)}, bf16[32,72,128]{2,1,0:T(8,128)(2,1)}, u32[]{:S(2)}, u32[]{:S(2)}) collective-permute-start(bf16[32,72,128]{2,1,0:T(8,128)(2,1)} %bitcast.61), channel_id=1, source_target_pairs={{0,4},{2,6},{4,0},{6,2},{1,5},{3,7},{5,1},{7,3},{8,12},{10,14},{12... | collective-permute-start | bytes 1769480 | tf_op jit(solution)/shard_map/ppermute | solution.py:268
  100.7 8.0 %copy-start.4 = (bf16[32,72,128]{2,1,0:T(8,128)(2,1)}, bf16[32,72,128]{2,1,0:T(8,128)(2,1)S(1)}, u32[]{:S(2)}) copy-start(bf16[32,72,128]{2,1,0:T(8,128)(2,1)S(1)} %collective-permute-done.13.refs_5_) | copy-start | bytes 1769476
  100.7 12.5 %collective-permute-start.14 = (bf16[32,72,128]{2,1,0:T(8,128)(2,1)}, bf16[32,72,128]{2,1,0:T(8,128)(2,1)}, u32[]{:S(2)}, u32[]{:S(2)}) collective-permute-start(bf16[32,72,128]{2,1,0:T(8,128)(2,1)} %bitcast.60), channel_id=1, source_target_pairs={{0,32},{16,48},{32,0},{48,16},{1,33},{17,49},{33,1},{49,17},{2,34}... | collective-permute-start | bytes 1769480 | tf_op jit(solution)/shard_map/ppermute | solution.py:268
  108.7 4.5 %copy-start.5 = (bf16[32,72,128]{2,1,0:T(8,128)(2,1)}, bf16[32,72,128]{2,1,0:T(8,128)(2,1)S(1)}, u32[]{:S(2)}) copy-start(bf16[32,72,128]{2,1,0:T(8,128)(2,1)S(1)} %collective-permute-done.8.refs_1_) | copy-start | bytes 1769476
  118.9 19.6 %all-to-all-start.1 = ((bf16[64,72,128]{2,1,0:T(8,128)(2,1)}), bf16[64,72,128]{2,1,0:T(8,128)(2,1)S(1)}, u32[]{:S(2)}, u32[]{:S(2)}) async-start(bf16[64,72,128]{2,1,0:T(8,128)(2,1)} %shard_map.79), calls=%async_computation.1 | async-start | bytes 2359296 | tf_op jit(solution)/shard_map/all_to_all | solution.py:348
  124.4 6.7 %collective-permute-start.15 = (s32[4,8]{1,0:T(4,128)S(1)}, s32[4,8]{1,0:T(4,128)S(1)}, u32[]{:S(2)}, u32[]{:S(2)}) collective-permute-start(s32[4,8]{1,0:T(4,128)S(1)} %get-tuple-element.62), channel_id=1, source_target_pairs={{0,8},{8,0},{1,9},{9,1},{2,10},{10,2},{3,11},{11,3},{4,12},{12,4},... | collective-permute-start | bytes 392 | tf_op jit(solution)/shard_map/ppermute | solution.py:291
  139.1 7.5 %collective-permute-start.16 = (bf16[4,4,8,128]{3,2,1,0:T(8,128)(2,1)S(1)}, bf16[4,4,8,128]{3,2,1,0:T(8,128)(2,1)S(1)}, u32[]{:S(2)}, u32[]{:S(2)}) collective-permute-start(bf16[4,4,8,128]{3,2,1,0:T(8,128)(2,1)S(1)} %get-tuple-element.66), channel_id=1, source_target_pairs={{0,8},{8,0},{1,9},{9,1},{2,10},{10,2},{3,11},{11,3},{4,12},{12,4},... | collective-permute-start | bytes 98312 | tf_op jit(solution)/shard_map/ppermute | solution.py:367

commit v5 on v4

--- a/solution.py
+++ b/solution.py
@@ -20,7 +20,7 @@
 DEAD = -(2.0**100)
 ROWS = 64
 META = 8
-PARTS = 4
+PARTS = 2
 
 
 def packed_tiles(first, second):
@@ -35,99 +35,98 @@
     return out
 
 
-def spread_kernel(holders, q_ref, o_ref):
-    for t, w in enumerate(holders):
-        o_ref[t] = q_ref[w]
-
-
 def partial_kernel(
-    info, lengths, qa_ref, qb_ref, k0_ref, k1_ref, v0_ref, v1_ref, *rest
+    step, info, lengths, qa_ref, qb_ref, k0_ref, k1_ref, v0_ref, v1_ref, *rest
 ):
     oa_ref, ob_ref = rest[-2:]
     length = k0_ref.shape[1]
     leads, heads = qa_ref.shape[:2]
     width = 2 * leads * ROWS
-    limit0 = lengths[info[0]] - info[2]
-    limit1 = lengths[info[0]] - info[3]
+    user = (info[1] + (KH - step)) % (lengths.shape[0] // 2)
+    limit0 = lengths[info[0] + user] - info[2]
+    limit1 = lengths[info[0] + user] - info[3]
+    limits = (limit0, limit1)
     rows_dims = (((1,), (1,)), ((), ()))
     first_dims = (((0,), (0,)), ((), ()))
 
-    def run(masked):
-        def head(j):
-            if isinstance(j, int):
-                cols = slice(j * HD, (j + 1) * HD)
-            else:
-                cols = pl.ds(pl.multiple_of(j * HD, HD), HD)
-            q = jnp.concatenate(
-                [
-                    qa_ref[:, j].reshape(width // 2, HD),
-                    qb_ref[:, j].reshape(width // 2, HD),
-                ]
+    def columns(j):
+        if isinstance(j, int):
+            return slice(j * HD, (j + 1) * HD)
+        return pl.ds(pl.multiple_of(j * HD, HD), HD)
+
+    def scores(j):
+        cols = columns(j)
+        q = jnp.concatenate(
+            [
+                qa_ref[:, j].reshape(width // 2, HD),
+                qb_ref[:, j].reshape(width // 2, HD),
+            ]
+        )
+        return [
+            lax.dot_general(k[0, :, cols], q, rows_dims, preferred_element_type=jnp.float32)
+            for k in (k0_ref, k1_ref)
+        ]
+
+    def weights(s, masked):
+        s = [part * SCALE2 for part in s]
+        if masked:
+            at = lax.broadcasted_iota(jnp.int32, (length, width), 0)
+            s = [jnp.where(at < limit, part, DEAD) for limit, part in zip(limits, s)]
+        peak = jnp.maximum(*[jnp.max(part, axis=0, keepdims=True) for part in s])
+        peak = peak.astype(jnp.bfloat16).astype(jnp.float32)
+        w = [jnp.exp2(part - peak) for part in s]
+        total = sum(jnp.sum(part, axis=0, keepdims=True) for part in w)
+        return [part.astype(jnp.bfloat16) for part in w], total, peak
+
+    def store(j, w, total, peak):
+        cols = columns(j)
+        numer = sum(
+            lax.dot_general(
+                v[0, :, cols], part, first_dims, preferred_element_type=jnp.float32
             )
-            s0 = lax.dot_general(
-                k0_ref[0, :, cols], q, rows_dims, preferred_element_type=jnp.float32
-            )
-            s1 = lax.dot_general(
-                k1_ref[0, :, cols], q, rows_dims, preferred_element_type=jnp.float32
-            )
-            s0 = s0 * SCALE2
-            s1 = s1 * SCALE2
-            if masked:
-                at = lax.broadcasted_iota(jnp.int32, (length, width), 0)
-                s0 = jnp.where(at < limit0, s0, DEAD)
-                s1 = jnp.where(at < limit1, s1, DEAD)
-            peak = jnp.maximum(
-                jnp.max(s0, axis=0, keepdims=True), jnp.max(s1, axis=0, keepdims=True)
-            )
-            peak = peak.astype(jnp.bfloat16).astype(jnp.float32)
-            w0 = jnp.exp2(s0 - peak)
-            w1 = jnp.exp2(s1 - peak)
-            total = jnp.sum(w0, axis=0, keepdims=True) + jnp.sum(w1, axis=0, keepdims=True)
-            numer = lax.dot_general(
-                v0_ref[0, :, cols],
-                w0.astype(jnp.bfloat16),
-                first_dims,
-                preferred_element_type=jnp.float32,
-            ) + lax.dot_general(
-                v1_ref[0, :, cols],
-                w1.astype(jnp.bfloat16),
-                first_dims,
-                preferred_element_type=jnp.float32,
-            )
-            numer = numer * (1.0 / total)
-            high = total.astype(jnp.bfloat16).astype(jnp.float32)
-            low = total - high
-            top = lax.broadcasted_iota(jnp.int32, (META, width), 0) == 0
-            tiles = packed_tiles(numer[:HALF], numer[HALF:])
-            notes = packed_tiles(jnp.where(top, peak, low), jnp.where(top, high, low))
-            for d in range(2 * leads):
-                o_ref = oa_ref if d < leads else ob_ref
-                o_ref[d % leads, j, :ROWS, :] = tiles[d].astype(jnp.bfloat16)
-                o_ref[d % leads, j, ROWS:, :] = notes[d].astype(jnp.bfloat16)
-
-        if masked:
-            pl.loop(0, heads)(head)
-        else:
-            for j in range(heads):
-                head(j)
+            for v, part in zip((v0_ref, v1_ref), w)
+        )
+        numer = numer * (1.0 / total)
+        high = total.astype(jnp.bfloat16).astype(jnp.float32)
+        low = total - high
+        top = lax.broadcasted_iota(jnp.int32, (META, width), 0) == 0
+        tiles = packed_tiles(numer[:HALF], numer[HALF:])
+        notes = packed_tiles(jnp.where(top, peak, low), jnp.where(top, high, low))
+        for d in range(2 * leads):
+            o_ref = oa_ref if d < leads else ob_ref
+            o_ref[d % leads, j, :ROWS, :] = tiles[d].astype(jnp.bfloat16)
+            o_ref[d % leads, j, ROWS:, :] = notes[d].astype(jnp.bfloat16)
 
     live = (limit0 >= length) & (limit1 >= length)
-    pl.when(live)(lambda: run(False))
-    pl.when(jnp.logical_not(live))(lambda: run(True))
-
-
-def partials(info, lengths, qa, qb, k0, k1, v0, v1, parts=(0, PARTS), into=()):
+
+    @pl.when(live)
+    def _():
+        s = scores(0)
+        for j in range(heads):
+            ahead = scores(j + 1) if j + 1 < heads else None
+            store(j, *weights(s, False))
+            s = ahead
+
+    @pl.when(jnp.logical_not(live))
+    def _():
+        @pl.loop(0, heads)
+        def _(j):
+            store(j, *weights(scores(j), True))
+
+
+def partials(step, info, lengths, qa, qb, k0, k1, v0, v1, parts=(0, PARTS), into=()):
     lead, heads = qa.shape[:2]
     length = k0.shape[1]
     share = heads // PARTS
     cache = (1, length, share * HD)
     begin, steps = parts
+    half = lengths.shape[0] // 2
 
     def mine(p, info, lengths):
-        return (info[0], 0, begin + p)
+        return (info[0] + (info[1] + (KH - step)) % half, 0, begin + p)
 
     def other(p, info, lengths):
-        return (info[1], 0, begin + p)
+        return ((info[1] + (KH - step)) % half, 0, begin + p)
 
     def heads_at(p, info, lengths):
         return (0, begin + p, 0, 0)
@@ -136,7 +135,7 @@
     asked = pl.BlockSpec((lead, share, ROWS, HD), heads_at)
     block = pl.BlockSpec((lead, share, ROWS + META, HD), heads_at)
     return pl.pallas_call(
-        partial_kernel,
+        functools.partial(partial_kernel, step),
         grid_spec=pltpu.PrefetchScalarGridSpec(
             num_scalar_prefetch=2,
             grid=(steps,),
@@ -194,30 +193,23 @@
             o_ref[t, ROWS:, :] = jnp.where(first, line, rest).astype(jnp.bfloat16)
             return 0
 
-        lax.fori_loop(0, parts[0].shape[0], one, 0, unroll=4)
+        lax.fori_loop(0, parts[0].shape[0], one, 0, unroll=8)
 
     per = (len(refs) - 1) // 2
-    half = pl.num_programs(0) // 2
-    pl.when(pl.program_id(0) < half)(lambda: join(refs[:per]))
-    pl.when(pl.program_id(0) >= half)(lambda: join(refs[per : 2 * per]))
+    pl.when(pl.program_id(0) == 0)(lambda: join(refs[:per]))
+    pl.when(pl.program_id(0) == 1)(lambda: join(refs[per : 2 * per]))
 
 
 def merged(left, right):
     count, rows, _ = left[0].shape
-    steps = 2
-    size = count // steps
-    block = (size, rows, HD)
-    ahead = pl.BlockSpec(block, lambda i: (jnp.minimum(i, steps - 1), 0, 0))
-    behind = pl.BlockSpec(block, lambda i: (jnp.maximum(i - steps, 0), 0, 0))
+    vmem = pl.BlockSpec(memory_space=pltpu.VMEM)
     return pl.pallas_call(
         merge_kernel,
-        grid=(2 * steps,),
-        in_specs=[ahead] * len(left) + [behind] * len(right),
-        out_specs=pl.BlockSpec(block, lambda i: (i, 0, 0)),
+        grid=(2,),
+        in_specs=[vmem] * (len(left) + len(right)),
+        out_specs=pl.BlockSpec((count, rows, HD), lambda i: (i, 0, 0)),
         out_shape=jax.ShapeDtypeStruct((2 * count, rows, HD), jnp.bfloat16),
-        compiler_params=pltpu.CompilerParams(
-            dimension_semantics=("arbitrary",), vmem_limit_bytes=60 << 20
-        ),
+        compiler_params=pltpu.CompilerParams(dimension_semantics=("arbitrary",), vmem_limit_bytes=52 << 20),
         cost_estimate=pl.CostEstimate(
             flops=16 * left[0].size, bytes_accessed=20 * left[0].size, transcendentals=0
         ),
@@ -299,11 +291,10 @@
     ]
     chips = len(holders)
     held = (x + y + 2 * zh + zl) % half
-    operand = pl.pallas_call(
-        functools.partial(spread_kernel, holders),
-        out_shape=jax.ShapeDtypeStruct((chips, ROWS, HD), jnp.bfloat16),
-        compiler_params=pltpu.CompilerParams(vmem_limit_bytes=60 << 20),
-    )(q_chip)
+    marks = np.asarray(holders).reshape(chips, 1, 1)
+    operand = jnp.broadcast_to(q_chip[0], (chips, ROWS, HD))
+    for w in range(1, half):
+        operand = jnp.where(marks == w, q_chip[w], operand)
     operand, value_source = lax.optimization_barrier((operand, value_cache))
     got = lax.all_to_all(operand, CHIPS, 0, 0, tiled=True)
     got = got.reshape(chips // KH, KH, ROWS, HD)
@@ -319,11 +310,11 @@
     offset = (row * KH + col) * length
     other = ((row + 1 - 2 * c) * KH + col) * length
 
+    info = jnp.stack([c * half, held, offset, other]).astype(jnp.int32)
+
     def computed(step, qa, qb, **kept):
-        user = (held - step) % half
-        info = jnp.stack([c * half + user, user, offset, other]).astype(jnp.int32)
         return partials(
-            info, lengths, qa, qb, key_cache, k_other, value_cache, v_other, **kept
+            step, info, lengths, qa, qb, key_cache, k_other, value_cache, v_other, **kept
         )
 
     def flat(parts):

time: 148 us -> 143 us (0.966)
  Pallas kernels: 56.2 us -> 47.9 us
  starting transfers between devices: 35.9 us -> 42.5 us
  local copies, waits for them, and re-layouts: 11.2 us -> 8.41 us
  waiting for transfers between devices: 10.3 us -> 12.1 us
  other arithmetic: 3.41 us -> 1.68 us
    pallas_call x7 -> x6, Pallas kernels: 55.6 us -> 47.4 us  [the longest x5 42.5 us: partials(): pl.pallas_call(functools.partial(partial_kernel, step), grid_spec=pltpu.P...]
    ppermute x12, starting transfers between devices: 15.9 us -> 20.8 us  [moved(): lax.ppermute(array, axis, [(i, (i + step) % count) for i in range(count)])]
    dynamic_slice x2 -> x3, local copies, waits for them, and re-layouts: 7.35 us -> 4.67 us  [halves(): lax.dynamic_slice_in_dim(array, (1 - c) * half, half, 0)]
    all_to_all x1, starting transfers between devices: 5.49 us -> 8 us  [body(): arrived = lax.all_to_all(merged(left, right), CHIPS, 0, 0, tiled=True)]
  transfers between devices with their start and end apart: 18 -> 18, of which waited for: 5 -> 8; matrix products, arithmetic and copies ran while one was open for 9% -> 6% of each run, Pallas kernels for 34% -> 30%
where the time goes in v5:
time: 143 us
  Pallas kernels  47.9 us (33%)
  starting transfers between devices  42.5 us (30%)
  blocking collectives  28.5 us (20%)
  waiting for transfers between devices  12.1 us (8%)
  local copies, waits for them, and re-layouts  8.41 us (6%)
  other arithmetic  1.68 us (1%)
  matrix products  1.43 us (1%)
    pallas_call x5, Pallas kernels, partials(): pl.pallas_call(functools.partial(partial_kernel, step), grid_spec=pltpu.P...  42.5 us
    all_to_all x1, blocking collectives, body(): got = lax.all_to_all(operand, CHIPS, 0, 0, tiled=True)  28.5 us
    ppermute x12, starting transfers between devices, moved(): lax.ppermute(array, axis, [(i, (i + step) % count) for i in range(count)])  20.8 us
    all_to_all x1, starting transfers between devices, body(): arrived = lax.all_to_all(merged(left, right), CHIPS, 0, 0, tiled=True)  8 us
    ppermute x1, starting transfers between devices, body(): received = swap(result[:, :, beams:])  6.36 us
    ppermute x12, waiting for transfers between devices, moved(): lax.ppermute(array, axis, [(i, (i + step) % count) for i in range(count)])  5.43 us
    all_to_all x1, waiting for transfers between devices, body(): arrived = lax.all_to_all(merged(left, right), CHIPS, 0, 0, tiled=True)  5.01 us
    pallas_call x1, Pallas kernels, merged(): pl.pallas_call(merge_kernel, grid=(2,), in_specs=[vmem] * (len(left) + le...  4.86 us
  transfers between devices with their start and end apart: 18, of which 8 were waited for; matrix products, arithmetic and copies ran while one was open for 6% of the time, Pallas kernels for 30%

profile of v5, /device:TPU:1, one launch (start us, length us, event | category | flops | bytes accessed | tf_op | source)
XLA Modules:
  0.0 142.8 jit_solution(11103389345324045681)
XLA Ops:
  1.7 1.5 %collective-permute-start = (bf16[4,4,8,128]{3,2,1,0:T(8,128)(2,1)S(1)}, bf16[4,4,8,128]{3,2,1,0:T(8,128)(2,1)S(1)}, u32[]{:S(2)}, u32[]{:S(2)}) collective-permute-start(bf16[4,4,8,128]{3,2,1,0:T(8,128)(2,1)S(1)} %get-tuple-element.34), channel_id=1, source_target_pairs={{0,8},{8,0},{1,9},{9,1},{2,10},{10,2},{3,11},{11,3},{4,12},{12,4},... | collective-permute-start | bytes 98312 | tf_op jit(solution)/shard_map/ppermute | solution.py:282
  3.2 3.3 %constant_dynamic-slice_fusion.2 = bf16[4,512,1024]{2,1,0:T(8,128)(2,1)S(1)} fusion(bf16[8,512,1024]{2,1,0:T(8,128)(2,1)} %k0_ref.9, s32[]{:T(128)S(6)} %select_n.42), kind=kLoop, calls=%fused_computation.34 | loop fusion | bytes 8388612 | tf_op jit(solution)/shard_map/dynamic_slice | solution.py:275
  8.3 28.5 %all_to_all.10 = bf16[64,64,128]{2,1,0:T(8,128)(2,1)S(1)} all-to-all(bf16[64,64,128]{2,1,0:T(8,128)(2,1)S(1)} %select_select_fusion), channel_id=1, replica_groups=mesh['zl'=2,'y'=4,'c'=2,'x'=4,'zh'=2] {'zl','y','x','zh'}, dimensions={0} | all-to-all | bytes 2097152 | tf_op jit(solution)/shard_map/all_to_all | solution.py:299
  38.1 2.2 %collective-permute-start.5 = (bf16[4,8,64,128]{3,2,1,0:T(8,128)(2,1)S(1)}, bf16[4,8,64,128]{3,2,1,0:T(8,128)(2,1)}, u32[]{:S(2)}, u32[]{:S(2)}) collective-permute-start(bf16[4,8,64,128]{3,2,1,0:T(8,128)(2,1)S(1)} %bitcast.43), channel_id=1, source_target_pairs={{0,6},{2,0},{4,2},{6,4},{1,7},{3,1},{5,3},{7,5},{8,14},{10,8},{12,... | collective-permute-start | bytes 1572872 | tf_op jit(solution)/shard_map/ppermute | solution.py:260
  40.2 2.2 %collective-permute-start.6 = (bf16[4,8,64,128]{3,2,1,0:T(8,128)(2,1)S(1)}, bf16[4,8,64,128]{3,2,1,0:T(8,128)(2,1)}, u32[]{:S(2)}, u32[]{:S(2)}) collective-permute-start(bf16[4,8,64,128]{3,2,1,0:T(8,128)(2,1)S(1)} %bitcast.38), channel_id=1, source_target_pairs={{0,48},{16,0},{32,16},{48,32},{1,49},{17,1},{33,17},{49,33},{2,50}... | collective-permute-start | bytes 1572872 | tf_op jit(solution)/shard_map/ppermute | solution.py:260
  43.0 6.5 %shard_map.100 = (bf16[4,8,72,128]{3,2,1,0:T(8,128)(2,1)}, bf16[4,8,72,128]{3,2,1,0:T(8,128)(2,1)}) custom-call(s32[4]{0:T(128)} %pad_add_fusion.1.info, s32[8]{0:T(128)} %lengths.9, bf16[4,8,64,128]{3,2,1,0:T(8,128)(2,1)} %bitcast.44, bf16[4,8,64,128]{3,2,1,0:T(8,128)(2,1)} %bitcast.39, bf16[8,512,1024]{2,1,0:T(8,128)(2,1)} %k0_ref.9, ...), custom_call_target="tpu_custom_call" | custom-call | flops 1073741824 | bytes 2097152 | tf_op jit(solution)/shard_map/pallas_call | solution.py:137
  51.2 2.1 %collective-permute-start.10 = (bf16[4,8,64,128]{3,2,1,0:T(8,128)(2,1)}, bf16[4,8,64,128]{3,2,1,0:T(8,128)(2,1)S(1)}, u32[]{:S(2)}, u32[]{:S(2)}) collective-permute-start(bf16[4,8,64,128]{3,2,1,0:T(8,128)(2,1)} %bitcast.40), channel_id=1, source_target_pairs={{0,32},{16,48},{32,0},{48,16},{1,33},{17,49},{33,1},{49,17},{2,34}... | collective-permute-start | bytes 1572872 | tf_op jit(solution)/shard_map/ppermute | solution.py:260
  53.3 1.7 %collective-permute-start.9 = (bf16[4,8,64,128]{3,2,1,0:T(8,128)(2,1)}, bf16[4,8,64,128]{3,2,1,0:T(8,128)(2,1)}, u32[]{:S(2)}, u32[]{:S(2)}) collective-permute-start(bf16[4,8,64,128]{3,2,1,0:T(8,128)(2,1)} %bitcast.45), channel_id=1, source_target_pairs={{0,4},{2,6},{4,0},{6,2},{1,5},{3,7},{5,1},{7,3},{8,12},{10,14},{12... | collective-permute-start | bytes 1572872 | tf_op jit(solution)/shard_map/ppermute | solution.py:260
  54.9 9.9 %shard_map.102 = (bf16[4,8,72,128]{3,2,1,0:T(8,128)(2,1)}, bf16[4,8,72,128]{3,2,1,0:T(8,128)(2,1)}) custom-call(s32[4]{0:T(128)} %pad_add_fusion.1.info, s32[8]{0:T(128)} %lengths.9, bf16[4,8,64,128]{3,2,1,0:T(8,128)(2,1)} %collective-permute-done.5.qa_ref, bf16[4,8,64,128]{3,2,1,0:T(8,128)(2,1)} %collective-permute-done.6.qb_ref, ...), custom_call_target="tpu_custom_call" | custom-call | flops 2147483648 | bytes 4194304 | tf_op jit(solution)/shard_map/pallas_call | solution.py:137
  64.8 1.8 %collective-permute-start.13 = (bf16[32,72,128]{2,1,0:T(8,128)(2,1)}, bf16[32,72,128]{2,1,0:T(8,128)(2,1)S(1)}, u32[]{:S(2)}, u32[]{:S(2)}) collective-permute-start(bf16[32,72,128]{2,1,0:T(8,128)(2,1)} %bitcast.59), channel_id=1, source_target_pairs={{0,16},{16,32},{32,48},{48,0},{1,17},{17,33},{33,49},{49,1},{2,18}... | collective-permute-start | bytes 1769480 | tf_op jit(solution)/shard_map/ppermute | solution.py:260
  67.2 9.9 %shard_map.101 = (bf16[4,8,72,128]{3,2,1,0:T(8,128)(2,1)}, bf16[4,8,72,128]{3,2,1,0:T(8,128)(2,1)}) custom-call(s32[4]{0:T(128)} %pad_add_fusion.1.info, s32[8]{0:T(128)} %lengths.9, bf16[4,8,64,128]{3,2,1,0:T(8,128)(2,1)} %collective-permute-done.3.qa_ref, bf16[4,8,64,128]{3,2,1,0:T(8,128)(2,1)} %collective-permute-done.4.qb_ref, ...), custom_call_target="tpu_custom_call" | custom-call | flops 2147483648 | bytes 4194304 | tf_op jit(solution)/shard_map/pallas_call | solution.py:137
  77.0 1.0 collective-permute-start.12
  78.9 2.7 %collective-permute-start.7 = (bf16[32,72,128]{2,1,0:T(8,128)(2,1)}, bf16[32,72,128]{2,1,0:T(8,128)(2,1)S(1)}, u32[]{:S(2)}, u32[]{:S(2)}) collective-permute-start(bf16[32,72,128]{2,1,0:T(8,128)(2,1)} %bitcast.57), channel_id=1, source_target_pairs={{0,6},{2,0},{4,2},{6,4},{1,7},{3,1},{5,3},{7,5},{8,14},{10,8},{12,... | collective-permute-start | bytes 1769480 | tf_op jit(solution)/shard_map/ppermute | solution.py:260
  81.5 9.9 %shard_map.103 = (bf16[4,8,72,128]{3,2,1,0:T(8,128)(2,1)}, bf16[4,8,72,128]{3,2,1,0:T(8,128)(2,1)}) custom-call(s32[4]{0:T(128)} %pad_add_fusion.1.info, s32[8]{0:T(128)} %lengths.9, bf16[4,8,64,128]{3,2,1,0:T(8,128)(2,1)} %collective-permute-done.9.qa_ref, bf16[4,8,64,128]{3,2,1,0:T(8,128)(2,1)} %copy-done.5, bf16[8,512,1024]{2,1,0:T(8,128)(2,1)} %k0_ref.9, ...), custom_call_target="tpu_custom_call" | custom-call | flops 2147483648 | bytes 4194304 | tf_op jit(solution)/shard_map/pallas_call | solution.py:137
  92.0 4.9 %collective-permute-start.14 = (bf16[32,72,128]{2,1,0:T(8,128)(2,1)}, bf16[32,72,128]{2,1,0:T(8,128)(2,1)}, u32[]{:S(2)}, u32[]{:S(2)}) collective-permute-start(bf16[32,72,128]{2,1,0:T(8,128)(2,1)} %bitcast.60), channel_id=1, source_target_pairs={{0,32},{16,48},{32,0},{48,16},{1,33},{17,49},{33,1},{49,17},{2,34}... | collective-permute-start | bytes 1769480 | tf_op jit(solution)/shard_map/ppermute | solution.py:260
  96.9 6.5 %shard_map.104 = (bf16[4,8,72,128]{3,2,1,0:T(8,128)(2,1)}, bf16[4,8,72,128]{3,2,1,0:T(8,128)(2,1)}) custom-call(s32[4]{0:T(128)} %pad_add_fusion.1.info, s32[8]{0:T(128)} %lengths.9, bf16[4,8,64,128]{3,2,1,0:T(8,128)(2,1)} %bitcast.46, bf16[4,8,64,128]{3,2,1,0:T(8,128)(2,1)} %bitcast.41, ...), custom_call_target="tpu_custom_call", output_to_operand_aliasing={{0}: (8, {}), {1}: (9, {})} | custom-call | flops 1073741824 | bytes 2097152 | tf_op jit(solution)/shard_map/pallas_call | solution.py:137
  104.3 2.9 %collective-permute-done.14.refs_6_ = bf16[32,72,128]{2,1,0:T(8,128)(2,1)} collective-permute-done((bf16[32,72,128]{2,1,0:T(8,128)(2,1)}, bf16[32,72,128]{2,1,0:T(8,128)(2,1)}, u32[]{:S(2)}, u32[]{:S(2)}) %collective-permute-start.14) | collective-permute-done | bytes 589856 | tf_op jit(solution)/shard_map/ppermute | solution.py:260
  107.1 4.9 %shard_map.105 = bf16[64,72,128]{2,1,0:T(8,128)(2,1)} custom-call(bf16[32,72,128]{2,1,0:T(8,128)(2,1)S(1)} %collective-permute-done.7.refs_0_, bf16[32,72,128]{2,1,0:T(8,128)(2,1)S(1)} %collective-permute-done.8.refs_1_, bf16[32,72,128]{2,1,0:T(8,128)(2,1)} %collective-permute-done.11.refs_2_, bf16[32,72,128]{2,1,0:T(8,128)(2,1)} %bitcast.47, ...), custom_call_target="tpu_custom_call" | custom-call | flops 4718592 | bytes 5898240 | tf_op jit(solution)/shard_map/pallas_call | solution.py:206
  112.0 8.0 %all-to-all-start.1 = ((bf16[64,72,128]{2,1,0:T(8,128)(2,1)}), bf16[64,72,128]{2,1,0:T(8,128)(2,1)S(1)}, u32[]{:S(2)}, u32[]{:S(2)}) async-start(bf16[64,72,128]{2,1,0:T(8,128)(2,1)} %shard_map.105), calls=%async_computation.1 | async-start | bytes 2359296 | tf_op jit(solution)/shard_map/all_to_all | solution.py:339
  120.0 4.8 %collective-permute-start.15 = (s32[4,8]{1,0:T(4,128)S(1)}, s32[4,8]{1,0:T(4,128)S(1)}, u32[]{:S(2)}, u32[]{:S(2)}) collective-permute-start(s32[4,8]{1,0:T(4,128)S(1)} %get-tuple-element.62), channel_id=1, source_target_pairs={{0,8},{8,0},{1,9},{9,1},{2,10},{10,2},{3,11},{11,3},{4,12},{12,4},... | collective-permute-start | bytes 392 | tf_op jit(solution)/shard_map/ppermute | solution.py:283
  126.8 1.1 copy.15.value_ref
  127.9 1.2 fusion.2
  129.4 5.0 %all-to-all-done.1.x_ref = bf16[64,72,128]{2,1,0:T(8,128)(2,1)S(1)} async-done(((bf16[64,72,128]{2,1,0:T(8,128)(2,1)}), bf16[64,72,128]{2,1,0:T(8,128)(2,1)S(1)}, u32[]{:S(2)}, u32[]{:S(2)}) %all-to-all-start.1) | async-done | bytes 1179680 | tf_op jit(solution)/shard_map/all_to_all | solution.py:339
  135.0 6.4 %collective-permute-start.16 = (bf16[4,4,8,128]{3,2,1,0:T(8,128)(2,1)S(1)}, bf16[4,4,8,128]{3,2,1,0:T(8,128)(2,1)S(1)}, u32[]{:S(2)}, u32[]{:S(2)}) collective-permute-start(bf16[4,4,8,128]{3,2,1,0:T(8,128)(2,1)S(1)} %get-tuple-element.66), channel_id=1, source_target_pairs={{0,8},{8,0},{1,9},{9,1},{2,10},{10,2},{3,11},{11,3},{4,12},{12,4},... | collective-permute-start | bytes 98312 | tf_op jit(solution)/shard_map/ppermute | solution.py:358
  (60 shorter events, 14.1 us)
Async XLA Ops:
  0.0 125.7 %copy-start = (bf16[1024,1024]{1,0:T(8,128)(2,1)S(1)}, bf16[1024,1024]{1,0:T(8,128)(2,1)}, u32[]{:S(2)}) copy-start(bf16[1024,1024]{1,0:T(8,128)(2,1)} %param.14) | copy-start | bytes 6291460
  1.7 5.0 %copy-start.8 = (pred[64]{0:T(512)(128)(4,1)S(1)}, pred[64]{0:T(512)(128)(4,1)}, u32[]{:S(2)}) copy-start(pred[64]{0:T(512)(128)(4,1)} %constant.62) | copy-start | bytes 196
  1.7 5.2 %copy-start.1 = (bf16[8,512,1024]{2,1,0:T(8,128)(2,1)S(1)}, bf16[8,512,1024]{2,1,0:T(8,128)(2,1)}, u32[]{:S(2)}) copy-start(bf16[8,512,1024]{2,1,0:T(8,128)(2,1)} %v0_ref.9) | copy-start | bytes 25165828
  1.7 4.9 %collective-permute-start = (bf16[4,4,8,128]{3,2,1,0:T(8,128)(2,1)S(1)}, bf16[4,4,8,128]{3,2,1,0:T(8,128)(2,1)S(1)}, u32[]{:S(2)}, u32[]{:S(2)}) collective-permute-start(bf16[4,4,8,128]{3,2,1,0:T(8,128)(2,1)S(1)} %get-tuple-element.34), channel_id=1, source_target_pairs={{0,8},{8,0},{1,9},{9,1},{2,10},{10,2},{3,11},{11,3},{4,12},{12,4},... | collective-permute-start | bytes 98312 | tf_op jit(solution)/shard_map/ppermute | solution.py:282
  6.5 30.5 %collective-permute-start.1 = (bf16[4,512,1024]{2,1,0:T(8,128)(2,1)S(1)}, bf16[4,512,1024]{2,1,0:T(8,128)(2,1)}, u32[]{:S(2)}, u32[]{:S(2)}) collective-permute-start(bf16[4,512,1024]{2,1,0:T(8,128)(2,1)S(1)} %constant_dynamic-slice_fusion.2), channel_id=1, source_target_pairs={{0,8},{8,0},{1,9},{9,1},{2,10},{10,2},{3,11},{11,3},{4,12},{12,4},... | collective-permute-start | bytes 12582920 | tf_op jit(solution)/shard_map/ppermute | solution.py:304
  7.4 29.5 %collective-permute-start.2 = (bf16[4,512,1024]{2,1,0:T(8,128)(2,1)S(1)}, bf16[4,512,1024]{2,1,0:T(8,128)(2,1)}, u32[]{:S(2)}, u32[]{:S(2)}) collective-permute-start(bf16[4,512,1024]{2,1,0:T(8,128)(2,1)S(1)} %constant_dynamic-slice_fusion.1), channel_id=1, source_target_pairs={{0,8},{8,0},{1,9},{9,1},{2,10},{10,2},{3,11},{11,3},{4,12},{12,4},... | collective-permute-start | bytes 12582920 | tf_op jit(solution)/shard_map/ppermute | solution.py:305
  36.9 6.0 %copy-start.2 = (bf16[32,64,128]{2,1,0:T(8,128)(2,1)}, bf16[32,64,128]{2,1,0:T(8,128)(2,1)S(1)}, u32[]{:S(2)}) copy-start(bf16[32,64,128]{2,1,0:T(8,128)(2,1)S(1)} %get-tuple-element.63) | copy-start | bytes 1572868
  37.0 6.0 %copy-start.3 = (bf16[32,64,128]{2,1,0:T(8,128)(2,1)}, bf16[32,64,128]{2,1,0:T(8,128)(2,1)S(1)}, u32[]{:S(2)}) copy-start(bf16[32,64,128]{2,1,0:T(8,128)(2,1)S(1)} %get-tuple-element.64) | copy-start | bytes 1572868
  37.0 13.0 %collective-permute-start.3 = (bf16[4,8,64,128]{3,2,1,0:T(8,128)(2,1)S(1)}, bf16[4,8,64,128]{3,2,1,0:T(8,128)(2,1)}, u32[]{:S(2)}, u32[]{:S(2)}) collective-permute-start(bf16[4,8,64,128]{3,2,1,0:T(8,128)(2,1)S(1)} %bitcast.42), channel_id=1, source_target_pairs={{0,2},{2,4},{4,6},{6,0},{1,3},{3,5},{5,7},{7,1},{8,10},{10,12},{12... | collective-permute-start | bytes 1572872 | tf_op jit(solution)/shard_map/ppermute | solution.py:260
  37.7 12.7 %collective-permute-start.4 = (bf16[4,8,64,128]{3,2,1,0:T(8,128)(2,1)S(1)}, bf16[4,8,64,128]{3,2,1,0:T(8,128)(2,1)}, u32[]{:S(2)}, u32[]{:S(2)}) collective-permute-start(bf16[4,8,64,128]{3,2,1,0:T(8,128)(2,1)S(1)} %bitcast.37), channel_id=1, source_target_pairs={{0,16},{16,32},{32,48},{48,0},{1,17},{17,33},{33,49},{49,1},{2,18}... | collective-permute-start | bytes 1572872 | tf_op jit(solution)/shard_map/ppermute | solution.py:260
  38.1 12.3 %collective-permute-start.5 = (bf16[4,8,64,128]{3,2,1,0:T(8,128)(2,1)S(1)}, bf16[4,8,64,128]{3,2,1,0:T(8,128)(2,1)}, u32[]{:S(2)}, u32[]{:S(2)}) collective-permute-start(bf16[4,8,64,128]{3,2,1,0:T(8,128)(2,1)S(1)} %bitcast.43), channel_id=1, source_target_pairs={{0,6},{2,0},{4,2},{6,4},{1,7},{3,1},{5,3},{7,5},{8,14},{10,8},{12,... | collective-permute-start | bytes 1572872 | tf_op jit(solution)/shard_map/ppermute | solution.py:260
  40.2 11.0 %collective-permute-start.6 = (bf16[4,8,64,128]{3,2,1,0:T(8,128)(2,1)S(1)}, bf16[4,8,64,128]{3,2,1,0:T(8,128)(2,1)}, u32[]{:S(2)}, u32[]{:S(2)}) collective-permute-start(bf16[4,8,64,128]{3,2,1,0:T(8,128)(2,1)S(1)} %bitcast.38), channel_id=1, source_target_pairs={{0,48},{16,0},{32,16},{48,32},{1,49},{17,1},{33,17},{49,33},{2,50}... | collective-permute-start | bytes 1572872 | tf_op jit(solution)/shard_map/ppermute | solution.py:260
  51.2 26.9 %collective-permute-start.10 = (bf16[4,8,64,128]{3,2,1,0:T(8,128)(2,1)}, bf16[4,8,64,128]{3,2,1,0:T(8,128)(2,1)S(1)}, u32[]{:S(2)}, u32[]{:S(2)}) collective-permute-start(bf16[4,8,64,128]{3,2,1,0:T(8,128)(2,1)} %bitcast.40), channel_id=1, source_target_pairs={{0,32},{16,48},{32,0},{48,16},{1,33},{17,49},{33,1},{49,17},{2,34}... | collective-permute-start | bytes 1572872 | tf_op jit(solution)/shard_map/ppermute | solution.py:260
  53.3 28.3 %collective-permute-start.9 = (bf16[4,8,64,128]{3,2,1,0:T(8,128)(2,1)}, bf16[4,8,64,128]{3,2,1,0:T(8,128)(2,1)}, u32[]{:S(2)}, u32[]{:S(2)}) collective-permute-start(bf16[4,8,64,128]{3,2,1,0:T(8,128)(2,1)} %bitcast.45), channel_id=1, source_target_pairs={{0,4},{2,6},{4,0},{6,2},{1,5},{3,7},{5,1},{7,3},{8,12},{10,14},{12... | collective-permute-start | bytes 1572872 | tf_op jit(solution)/shard_map/ppermute | solution.py:260
  64.8 27.3 %collective-permute-start.13 = (bf16[32,72,128]{2,1,0:T(8,128)(2,1)}, bf16[32,72,128]{2,1,0:T(8,128)(2,1)S(1)}, u32[]{:S(2)}, u32[]{:S(2)}) collective-permute-start(bf16[32,72,128]{2,1,0:T(8,128)(2,1)} %bitcast.59), channel_id=1, source_target_pairs={{0,16},{16,32},{32,48},{48,0},{1,17},{17,33},{33,49},{49,1},{2,18}... | collective-permute-start | bytes 1769480 | tf_op jit(solution)/shard_map/ppermute | solution.py:260
  66.6 36.9 %collective-permute-start.8 = (bf16[32,72,128]{2,1,0:T(8,128)(2,1)}, bf16[32,72,128]{2,1,0:T(8,128)(2,1)S(1)}, u32[]{:S(2)}, u32[]{:S(2)}) collective-permute-start(bf16[32,72,128]{2,1,0:T(8,128)(2,1)} %bitcast.56), channel_id=1, source_target_pairs={{0,2},{2,4},{4,6},{6,0},{1,3},{3,5},{5,7},{7,1},{8,10},{10,12},{12... | collective-permute-start | bytes 1769480 | tf_op jit(solution)/shard_map/ppermute | solution.py:260
  77.0 26.4 %collective-permute-start.12 = (bf16[32,72,128]{2,1,0:T(8,128)(2,1)}, bf16[32,72,128]{2,1,0:T(8,128)(2,1)}, u32[]{:S(2)}, u32[]{:S(2)}) collective-permute-start(bf16[32,72,128]{2,1,0:T(8,128)(2,1)} %bitcast.58), channel_id=1, source_target_pairs={{0,48},{16,0},{32,16},{48,32},{1,49},{17,1},{33,17},{49,33},{2,50}... | collective-permute-start | bytes 1769480 | tf_op jit(solution)/shard_map/ppermute | solution.py:260
  78.9 24.6 %collective-permute-start.7 = (bf16[32,72,128]{2,1,0:T(8,128)(2,1)}, bf16[32,72,128]{2,1,0:T(8,128)(2,1)S(1)}, u32[]{:S(2)}, u32[]{:S(2)}) collective-permute-start(bf16[32,72,128]{2,1,0:T(8,128)(2,1)} %bitcast.57), channel_id=1, source_target_pairs={{0,6},{2,0},{4,2},{6,4},{1,7},{3,1},{5,3},{7,5},{8,14},{10,8},{12,... | collective-permute-start | bytes 1769480 | tf_op jit(solution)/shard_map/ppermute | solution.py:260
  91.4 12.8 %collective-permute-start.11 = (bf16[32,72,128]{2,1,0:T(8,128)(2,1)}, bf16[32,72,128]{2,1,0:T(8,128)(2,1)}, u32[]{:S(2)}, u32[]{:S(2)}) collective-permute-start(bf16[32,72,128]{2,1,0:T(8,128)(2,1)} %bitcast.61), channel_id=1, source_target_pairs={{0,4},{2,6},{4,0},{6,2},{1,5},{3,7},{5,1},{7,3},{8,12},{10,14},{12... | collective-permute-start | bytes 1769480 | tf_op jit(solution)/shard_map/ppermute | solution.py:260
  92.0 11.4 %copy-start.4 = (bf16[32,72,128]{2,1,0:T(8,128)(2,1)}, bf16[32,72,128]{2,1,0:T(8,128)(2,1)S(1)}, u32[]{:S(2)}) copy-start(bf16[32,72,128]{2,1,0:T(8,128)(2,1)S(1)} %collective-permute-done.13.refs_5_) | copy-start | bytes 1769476
  92.0 15.1 %collective-permute-start.14 = (bf16[32,72,128]{2,1,0:T(8,128)(2,1)}, bf16[32,72,128]{2,1,0:T(8,128)(2,1)}, u32[]{:S(2)}, u32[]{:S(2)}) collective-permute-start(bf16[32,72,128]{2,1,0:T(8,128)(2,1)} %bitcast.60), channel_id=1, source_target_pairs={{0,32},{16,48},{32,0},{48,16},{1,33},{17,49},{33,1},{49,17},{2,34}... | collective-permute-start | bytes 1769480 | tf_op jit(solution)/shard_map/ppermute | solution.py:260
  112.0 22.4 %all-to-all-start.1 = ((bf16[64,72,128]{2,1,0:T(8,128)(2,1)}), bf16[64,72,128]{2,1,0:T(8,128)(2,1)S(1)}, u32[]{:S(2)}, u32[]{:S(2)}) async-start(bf16[64,72,128]{2,1,0:T(8,128)(2,1)} %shard_map.105), calls=%async_computation.1 | async-start | bytes 2359296 | tf_op jit(solution)/shard_map/all_to_all | solution.py:339
  120.0 5.6 %collective-permute-start.15 = (s32[4,8]{1,0:T(4,128)S(1)}, s32[4,8]{1,0:T(4,128)S(1)}, u32[]{:S(2)}, u32[]{:S(2)}) collective-permute-start(s32[4,8]{1,0:T(4,128)S(1)} %get-tuple-element.62), channel_id=1, source_target_pairs={{0,8},{8,0},{1,9},{9,1},{2,10},{10,2},{3,11},{11,3},{4,12},{12,4},... | collective-permute-start | bytes 392 | tf_op jit(solution)/shard_map/ppermute | solution.py:283
  135.0 7.2 %collective-permute-start.16 = (bf16[4,4,8,128]{3,2,1,0:T(8,128)(2,1)S(1)}, bf16[4,4,8,128]{3,2,1,0:T(8,128)(2,1)S(1)}, u32[]{:S(2)}, u32[]{:S(2)}) collective-permute-start(bf16[4,4,8,128]{3,2,1,0:T(8,128)(2,1)S(1)} %get-tuple-element.66), channel_id=1, source_target_pairs={{0,8},{8,0},{1,9},{9,1},{2,10},{10,2},{3,11},{11,3},{4,12},{12,4},... | collective-permute-start | bytes 98312 | tf_op jit(solution)/shard_map/ppermute | solution.py:358
  (3 other events, 10.7 us)

commit v6 on v5

--- a/solution.py
+++ b/solution.py
@@ -107,7 +107,20 @@
             store(j, *weights(s, False))
             s = ahead
 
-    @pl.when(jnp.logical_not(live))
+    dead = (limit0 <= 0) & (limit1 <= 0)
+
+    @pl.when(dead)
+    def _():
+        shape = (heads, META, HD)
+        side = lax.broadcasted_iota(jnp.int32, shape, 2) < ROWS
+        first = lax.broadcasted_iota(jnp.int32, shape, 1) == 0
+        note = jnp.where(first, jnp.where(side, DEAD, 1.0), 0.0).astype(jnp.bfloat16)
+        for d in range(2 * leads):
+            o_ref = oa_ref if d < leads else ob_ref
+            o_ref[d % leads, :, :ROWS, :] = jnp.zeros((heads, ROWS, HD), jnp.bfloat16)
+            o_ref[d % leads, :, ROWS:, :] = note
+
+    @pl.when(jnp.logical_not(live | dead))
     def _():
         @pl.loop(0, heads)
         def _(j):
@@ -171,31 +184,47 @@
 
 
 def merge_kernel(*refs):
-    o_ref = refs[-1]
-    low = lax.broadcasted_iota(jnp.int32, (1, HD), 1) < ROWS
-    first = lax.broadcasted_iota(jnp.int32, (META, HD), 0) == 0
+    o_ref, w_ref = refs[-2:]
+    low = lax.broadcasted_iota(jnp.int32, (8, HD), 1) < ROWS
+    first = lax.broadcasted_iota(jnp.int32, (8, META, HD), 1) == 0
 
     def join(parts):
-        def one(t, _):
-            pairs = [stats_of(r[t, ROWS:, :].astype(jnp.float32), low) for r in parts]
-            peak = functools.reduce(jnp.maximum, [p for p, _ in pairs])
-            weights = [m * jnp.exp2(p - peak) for p, m in pairs]
+        def note(i, _):
+            at = pl.ds(pl.multiple_of(i * 8, 8), 8)
+            peaks, masses = [], []
+            for r in parts:
+                notes = r[at, ROWS:, :].astype(jnp.float32)
+                line = notes[:, 0, :]
+                turned = pltpu.roll(line, ROWS, 1)
+                peaks.append(jnp.where(low, line, turned))
+                masses.append(jnp.where(low, turned, line) + notes[:, 1, :])
+            peak = functools.reduce(jnp.maximum, peaks)
+            weights = [m * jnp.exp2(p - peak) for p, m in zip(peaks, masses)]
             total = functools.reduce(jnp.add, weights)
             inverse = 1.0 / total
+            for n, w in enumerate(weights):
+                w_ref[n, at, :] = w * inverse
+            high = total.astype(jnp.bfloat16).astype(jnp.float32)
+            line = jnp.where(low, peak, high)
+            rest = total - high
+            o_ref[at, ROWS:, :] = jnp.where(first, line[:, None], rest[:, None]).astype(
+                jnp.bfloat16
+            )
+            return 0
+
+        def add(t, _):
             acc = None
-            for r, w in zip(parts, weights):
-                term = r[t, :ROWS, :].astype(jnp.float32) * (w * inverse)
+            for n, r in enumerate(parts):
+                term = r[t, :ROWS, :].astype(jnp.float32) * w_ref[n, pl.ds(t, 1), :]
                 acc = term if acc is None else acc + term
             o_ref[t, :ROWS, :] = acc.astype(jnp.bfloat16)
-            high = total.astype(jnp.bfloat16).astype(jnp.float32)
-            rest = total - high
-            line = jnp.where(low, peak, high)
-            o_ref[t, ROWS:, :] = jnp.where(first, line, rest).astype(jnp.bfloat16)
             return 0
 
-        lax.fori_loop(0, parts[0].shape[0], one, 0, unroll=8)
-
-    per = (len(refs) - 1) // 2
+        count = parts[0].shape[0]
+        lax.fori_loop(0, count // 8, note, 0, unroll=2)
+        lax.fori_loop(0, count, add, 0, unroll=4)
+
+    per = (len(refs) - 2) // 2
     pl.when(pl.program_id(0) == 0)(lambda: join(refs[:per]))
     pl.when(pl.program_id(0) == 1)(lambda: join(refs[per : 2 * per]))
 
@@ -208,6 +237,7 @@
         grid=(2,),
         in_specs=[vmem] * (len(left) + len(right)),
         out_specs=pl.BlockSpec((count, rows, HD), lambda i: (i, 0, 0)),
+        scratch_shapes=[pltpu.VMEM((len(left), count, HD), jnp.float32)],
         out_shape=jax.ShapeDtypeStruct((2 * count, rows, HD), jnp.bfloat16),
         compiler_params=pltpu.CompilerParams(dimension_semantics=("arbitrary",), vmem_limit_bytes=52 << 20),
         cost_estimate=pl.CostEstimate(

time: 143 us -> 141 us (0.986)
  starting transfers between devices: 42.5 us -> 37.2 us
  waiting for transfers between devices: 12.1 us -> 16.2 us
    all_to_all x1, waiting for transfers between devices: 5.01 us -> 10.1 us  [body(): arrived = lax.all_to_all(merged(left, right), CHIPS, 0, 0, tiled=True)]
    ppermute x12, starting transfers between devices: 20.8 us -> 16.2 us  [moved(): lax.ppermute(array, axis, [(i, (i + step) % count) for i in range(count)])]
    all_to_all x1, starting transfers between devices: 8 us -> 12.5 us  [body(): arrived = lax.all_to_all(merged(left, right), CHIPS, 0, 0, tiled=True)]
    ppermute x1, starting transfers between devices: 6.36 us -> 3.8 us  [body(): received = swap(result[:, :, beams:])]
    ppermute x1, starting transfers between devices: 4.83 us -> 2.31 us  [body(): tokens = jnp.concatenate([t_mine, swap(t_give)], axis=1)]
  transfers between devices with their start and end apart: 18 -> 18, of which waited for: 8 -> 7; matrix products, arithmetic and copies ran while one was open for 6% -> 6% of each run, Pallas kernels for 30% -> 30%
where the time goes in v6:
time: 141 us
  Pallas kernels  47.4 us (34%)
  starting transfers between devices  37.2 us (26%)
  blocking collectives  28.5 us (20%)
  waiting for transfers between devices  16.2 us (11%)
  local copies, waits for them, and re-layouts  8.41 us (6%)
  other arithmetic  1.68 us (1%)
  matrix products  1.43 us (1%)
    pallas_call x5, Pallas kernels, partials(): pl.pallas_call(functools.partial(partial_kernel, step), grid_spec=pltpu.P...  42.6 us
    all_to_all x1, blocking collectives, body(): got = lax.all_to_all(operand, CHIPS, 0, 0, tiled=True)  28.5 us
    ppermute x12, starting transfers between devices, moved(): lax.ppermute(array, axis, [(i, (i + step) % count) for i in range(count)])  16.2 us
    all_to_all x1, starting transfers between devices, body(): arrived = lax.all_to_all(merged(left, right), CHIPS, 0, 0, tiled=True)  12.5 us
    all_to_all x1, waiting for transfers between devices, body(): arrived = lax.all_to_all(merged(left, right), CHIPS, 0, 0, tiled=True)  10.1 us
    dynamic_slice x3, local copies, waits for them, and re-layouts, halves(): lax.dynamic_slice_in_dim(array, (1 - c) * half, half, 0)  4.67 us
    ppermute x12, waiting for transfers between devices, moved(): lax.ppermute(array, axis, [(i, (i + step) % count) for i in range(count)])  4.39 us
    pallas_call x1, Pallas kernels, merged(): pl.pallas_call(merge_kernel, grid=(2,), in_specs=[vmem] * (len(left) + le...  4.25 us
  transfers between devices with their start and end apart: 18, of which 7 were waited for; matrix products, arithmetic and copies ran while one was open for 6% of the time, Pallas kernels for 30%

profile of v6, /device:TPU:1, one launch (start us, length us, event | category | flops | bytes accessed | tf_op | source)
XLA Modules:
  0.0 141.1 jit_solution(5168584303885464640)
XLA Ops:
  0.0 0.9 dynamic-slice_bitcast_fusion
  1.7 1.5 %collective-permute-start = (bf16[4,4,8,128]{3,2,1,0:T(8,128)(2,1)S(1)}, bf16[4,4,8,128]{3,2,1,0:T(8,128)(2,1)S(1)}, u32[]{:S(2)}, u32[]{:S(2)}) collective-permute-start(bf16[4,4,8,128]{3,2,1,0:T(8,128)(2,1)S(1)} %get-tuple-element.34), channel_id=1, source_target_pairs={{0,8},{8,0},{1,9},{9,1},{2,10},{10,2},{3,11},{11,3},{4,12},{12,4},... | collective-permute-start | bytes 98312 | tf_op jit(solution)/shard_map/ppermute | solution.py:312
  3.2 3.3 %constant_dynamic-slice_fusion.2 = bf16[4,512,1024]{2,1,0:T(8,128)(2,1)S(1)} fusion(bf16[8,512,1024]{2,1,0:T(8,128)(2,1)} %k0_ref.9, s32[]{:T(128)S(6)} %select_n.42), kind=kLoop, calls=%fused_computation.34 | loop fusion | bytes 8388612 | tf_op jit(solution)/shard_map/dynamic_slice | solution.py:305
  8.3 28.5 %all_to_all.10 = bf16[64,64,128]{2,1,0:T(8,128)(2,1)S(1)} all-to-all(bf16[64,64,128]{2,1,0:T(8,128)(2,1)S(1)} %select_select_fusion), channel_id=1, replica_groups=mesh['zl'=2,'y'=4,'c'=2,'x'=4,'zh'=2] {'zl','y','x','zh'}, dimensions={0} | all-to-all | bytes 2097152 | tf_op jit(solution)/shard_map/all_to_all | solution.py:329
  38.1 2.2 %collective-permute-start.5 = (bf16[4,8,64,128]{3,2,1,0:T(8,128)(2,1)S(1)}, bf16[4,8,64,128]{3,2,1,0:T(8,128)(2,1)}, u32[]{:S(2)}, u32[]{:S(2)}) collective-permute-start(bf16[4,8,64,128]{3,2,1,0:T(8,128)(2,1)S(1)} %bitcast.43), channel_id=1, source_target_pairs={{0,6},{2,0},{4,2},{6,4},{1,7},{3,1},{5,3},{7,5},{8,14},{10,8},{12,... | collective-permute-start | bytes 1572872 | tf_op jit(solution)/shard_map/ppermute | solution.py:290
  40.2 2.2 %collective-permute-start.6 = (bf16[4,8,64,128]{3,2,1,0:T(8,128)(2,1)S(1)}, bf16[4,8,64,128]{3,2,1,0:T(8,128)(2,1)}, u32[]{:S(2)}, u32[]{:S(2)}) collective-permute-start(bf16[4,8,64,128]{3,2,1,0:T(8,128)(2,1)S(1)} %bitcast.38), channel_id=1, source_target_pairs={{0,48},{16,0},{32,16},{48,32},{1,49},{17,1},{33,17},{49,33},{2,50}... | collective-permute-start | bytes 1572872 | tf_op jit(solution)/shard_map/ppermute | solution.py:290
  43.0 6.5 %shard_map.100 = (bf16[4,8,72,128]{3,2,1,0:T(8,128)(2,1)}, bf16[4,8,72,128]{3,2,1,0:T(8,128)(2,1)}) custom-call(s32[4]{0:T(128)} %pad_add_fusion.1.info, s32[8]{0:T(128)} %lengths.9, bf16[4,8,64,128]{3,2,1,0:T(8,128)(2,1)} %bitcast.44, bf16[4,8,64,128]{3,2,1,0:T(8,128)(2,1)} %bitcast.39, bf16[8,512,1024]{2,1,0:T(8,128)(2,1)} %k0_ref.9, ...), custom_call_target="tpu_custom_call" | custom-call | flops 1073741824 | bytes 2097152 | tf_op jit(solution)/shard_map/pallas_call | solution.py:150
  51.2 2.1 %collective-permute-start.10 = (bf16[4,8,64,128]{3,2,1,0:T(8,128)(2,1)}, bf16[4,8,64,128]{3,2,1,0:T(8,128)(2,1)S(1)}, u32[]{:S(2)}, u32[]{:S(2)}) collective-permute-start(bf16[4,8,64,128]{3,2,1,0:T(8,128)(2,1)} %bitcast.40), channel_id=1, source_target_pairs={{0,32},{16,48},{32,0},{48,16},{1,33},{17,49},{33,1},{49,17},{2,34}... | collective-permute-start | bytes 1572872 | tf_op jit(solution)/shard_map/ppermute | solution.py:290
  53.3 1.7 %collective-permute-start.9 = (bf16[4,8,64,128]{3,2,1,0:T(8,128)(2,1)}, bf16[4,8,64,128]{3,2,1,0:T(8,128)(2,1)}, u32[]{:S(2)}, u32[]{:S(2)}) collective-permute-start(bf16[4,8,64,128]{3,2,1,0:T(8,128)(2,1)} %bitcast.45), channel_id=1, source_target_pairs={{0,4},{2,6},{4,0},{6,2},{1,5},{3,7},{5,1},{7,3},{8,12},{10,14},{12... | collective-permute-start | bytes 1572872 | tf_op jit(solution)/shard_map/ppermute | solution.py:290
  54.9 9.9 %shard_map.102 = (bf16[4,8,72,128]{3,2,1,0:T(8,128)(2,1)}, bf16[4,8,72,128]{3,2,1,0:T(8,128)(2,1)}) custom-call(s32[4]{0:T(128)} %pad_add_fusion.1.info, s32[8]{0:T(128)} %lengths.9, bf16[4,8,64,128]{3,2,1,0:T(8,128)(2,1)} %collective-permute-done.5.qa_ref, bf16[4,8,64,128]{3,2,1,0:T(8,128)(2,1)} %collective-permute-done.6.qb_ref, ...), custom_call_target="tpu_custom_call" | custom-call | flops 2147483648 | bytes 4194304 | tf_op jit(solution)/shard_map/pallas_call | solution.py:150
  64.8 1.8 %collective-permute-start.13 = (bf16[32,72,128]{2,1,0:T(8,128)(2,1)}, bf16[32,72,128]{2,1,0:T(8,128)(2,1)S(1)}, u32[]{:S(2)}, u32[]{:S(2)}) collective-permute-start(bf16[32,72,128]{2,1,0:T(8,128)(2,1)} %bitcast.59), channel_id=1, source_target_pairs={{0,16},{16,32},{32,48},{48,0},{1,17},{17,33},{33,49},{49,1},{2,18}... | collective-permute-start | bytes 1769480 | tf_op jit(solution)/shard_map/ppermute | solution.py:290
  66.6 9.9 %shard_map.101 = (bf16[4,8,72,128]{3,2,1,0:T(8,128)(2,1)}, bf16[4,8,72,128]{3,2,1,0:T(8,128)(2,1)}) custom-call(s32[4]{0:T(128)} %pad_add_fusion.1.info, s32[8]{0:T(128)} %lengths.9, bf16[4,8,64,128]{3,2,1,0:T(8,128)(2,1)} %collective-permute-done.3.qa_ref, bf16[4,8,64,128]{3,2,1,0:T(8,128)(2,1)} %collective-permute-done.4.qb_ref, ...), custom_call_target="tpu_custom_call" | custom-call | flops 2147483648 | bytes 4194304 | tf_op jit(solution)/shard_map/pallas_call | solution.py:150
  76.4 2.3 %collective-permute-start.12 = (bf16[32,72,128]{2,1,0:T(8,128)(2,1)}, bf16[32,72,128]{2,1,0:T(8,128)(2,1)}, u32[]{:S(2)}, u32[]{:S(2)}) collective-permute-start(bf16[32,72,128]{2,1,0:T(8,128)(2,1)} %bitcast.58), channel_id=1, source_target_pairs={{0,48},{16,0},{32,16},{48,32},{1,49},{17,1},{33,17},{49,33},{2,50}... | collective-permute-start | bytes 1769480 | tf_op jit(solution)/shard_map/ppermute | solution.py:290
  79.9 9.9 %shard_map.103 = (bf16[4,8,72,128]{3,2,1,0:T(8,128)(2,1)}, bf16[4,8,72,128]{3,2,1,0:T(8,128)(2,1)}) custom-call(s32[4]{0:T(128)} %pad_add_fusion.1.info, s32[8]{0:T(128)} %lengths.9, bf16[4,8,64,128]{3,2,1,0:T(8,128)(2,1)} %collective-permute-done.9.qa_ref, bf16[4,8,64,128]{3,2,1,0:T(8,128)(2,1)} %copy-done.5, bf16[8,512,1024]{2,1,0:T(8,128)(2,1)} %k0_ref.9, ...), custom_call_target="tpu_custom_call" | custom-call | flops 2147483648 | bytes 4194304 | tf_op jit(solution)/shard_map/pallas_call | solution.py:150
  89.9 2.5 %collective-permute-start.14 = (bf16[32,72,128]{2,1,0:T(8,128)(2,1)}, bf16[32,72,128]{2,1,0:T(8,128)(2,1)}, u32[]{:S(2)}, u32[]{:S(2)}) collective-permute-start(bf16[32,72,128]{2,1,0:T(8,128)(2,1)} %bitcast.60), channel_id=1, source_target_pairs={{0,32},{16,48},{32,0},{48,16},{1,33},{17,49},{33,1},{49,17},{2,34}... | collective-permute-start | bytes 1769480 | tf_op jit(solution)/shard_map/ppermute | solution.py:290
  92.4 6.5 %shard_map.104 = (bf16[4,8,72,128]{3,2,1,0:T(8,128)(2,1)}, bf16[4,8,72,128]{3,2,1,0:T(8,128)(2,1)}) custom-call(s32[4]{0:T(128)} %pad_add_fusion.1.info, s32[8]{0:T(128)} %lengths.9, bf16[4,8,64,128]{3,2,1,0:T(8,128)(2,1)} %bitcast.46, bf16[4,8,64,128]{3,2,1,0:T(8,128)(2,1)} %bitcast.41, ...), custom_call_target="tpu_custom_call", output_to_operand_aliasing={{0}: (8, {}), {1}: (9, {})} | custom-call | flops 1073741824 | bytes 2097152 | tf_op jit(solution)/shard_map/pallas_call | solution.py:150
  98.9 2.6 %collective-permute-done.11.refs_2_ = bf16[32,72,128]{2,1,0:T(8,128)(2,1)} collective-permute-done((bf16[32,72,128]{2,1,0:T(8,128)(2,1)}, bf16[32,72,128]{2,1,0:T(8,128)(2,1)}, u32[]{:S(2)}, u32[]{:S(2)}) %collective-permute-start.11) | collective-permute-done | bytes 589856 | tf_op jit(solution)/shard_map/ppermute | solution.py:290
  101.5 4.3 %shard_map.105 = bf16[64,72,128]{2,1,0:T(8,128)(2,1)} custom-call(bf16[32,72,128]{2,1,0:T(8,128)(2,1)S(1)} %collective-permute-done.7.refs_0_, bf16[32,72,128]{2,1,0:T(8,128)(2,1)S(1)} %collective-permute-done.8.refs_1_, bf16[32,72,128]{2,1,0:T(8,128)(2,1)} %collective-permute-done.11.refs_2_, bf16[32,72,128]{2,1,0:T(8,128)(2,1)} %bitcast.47, ...), custom_call_target="tpu_custom_call" | custom-call | flops 4718592 | bytes 5898240 | tf_op jit(solution)/shard_map/pallas_call | solution.py:235
  105.8 12.5 %all-to-all-start.1 = ((bf16[64,72,128]{2,1,0:T(8,128)(2,1)}), bf16[64,72,128]{2,1,0:T(8,128)(2,1)S(1)}, u32[]{:S(2)}, u32[]{:S(2)}) async-start(bf16[64,72,128]{2,1,0:T(8,128)(2,1)} %shard_map.105), calls=%async_computation.1 | async-start | bytes 2359296 | tf_op jit(solution)/shard_map/all_to_all | solution.py:369
  118.2 2.3 %collective-permute-start.15 = (s32[4,8]{1,0:T(4,128)S(1)}, s32[4,8]{1,0:T(4,128)S(1)}, u32[]{:S(2)}, u32[]{:S(2)}) collective-permute-start(s32[4,8]{1,0:T(4,128)S(1)} %get-tuple-element.62), channel_id=1, source_target_pairs={{0,8},{8,0},{1,9},{9,1},{2,10},{10,2},{3,11},{11,3},{4,12},{12,4},... | collective-permute-start | bytes 392 | tf_op jit(solution)/shard_map/ppermute | solution.py:313
  122.5 1.1 copy.15.value_ref
  123.6 1.2 fusion.2
  125.1 10.1 %all-to-all-done.1.x_ref = bf16[64,72,128]{2,1,0:T(8,128)(2,1)S(1)} async-done(((bf16[64,72,128]{2,1,0:T(8,128)(2,1)}), bf16[64,72,128]{2,1,0:T(8,128)(2,1)S(1)}, u32[]{:S(2)}, u32[]{:S(2)}) %all-to-all-start.1) | async-done | bytes 1179680 | tf_op jit(solution)/shard_map/all_to_all | solution.py:369
  135.8 3.8 %collective-permute-start.16 = (bf16[4,4,8,128]{3,2,1,0:T(8,128)(2,1)S(1)}, bf16[4,4,8,128]{3,2,1,0:T(8,128)(2,1)S(1)}, u32[]{:S(2)}, u32[]{:S(2)}) collective-permute-start(bf16[4,4,8,128]{3,2,1,0:T(8,128)(2,1)S(1)} %get-tuple-element.66), channel_id=1, source_target_pairs={{0,8},{8,0},{1,9},{9,1},{2,10},{10,2},{3,11},{11,3},{4,12},{12,4},... | collective-permute-start | bytes 98312 | tf_op jit(solution)/shard_map/ppermute | solution.py:388
  (60 shorter events, 11.6 us)
Async XLA Ops:
  0.0 121.4 %copy-start = (bf16[1024,1024]{1,0:T(8,128)(2,1)S(1)}, bf16[1024,1024]{1,0:T(8,128)(2,1)}, u32[]{:S(2)}) copy-start(bf16[1024,1024]{1,0:T(8,128)(2,1)} %param.14) | copy-start | bytes 6291460
  1.7 5.0 %copy-start.8 = (pred[64]{0:T(512)(128)(4,1)S(1)}, pred[64]{0:T(512)(128)(4,1)}, u32[]{:S(2)}) copy-start(pred[64]{0:T(512)(128)(4,1)} %constant.62) | copy-start | bytes 196
  1.7 5.2 %copy-start.1 = (bf16[8,512,1024]{2,1,0:T(8,128)(2,1)S(1)}, bf16[8,512,1024]{2,1,0:T(8,128)(2,1)}, u32[]{:S(2)}) copy-start(bf16[8,512,1024]{2,1,0:T(8,128)(2,1)} %v0_ref.9) | copy-start | bytes 25165828
  1.7 4.9 %collective-permute-start = (bf16[4,4,8,128]{3,2,1,0:T(8,128)(2,1)S(1)}, bf16[4,4,8,128]{3,2,1,0:T(8,128)(2,1)S(1)}, u32[]{:S(2)}, u32[]{:S(2)}) collective-permute-start(bf16[4,4,8,128]{3,2,1,0:T(8,128)(2,1)S(1)} %get-tuple-element.34), channel_id=1, source_target_pairs={{0,8},{8,0},{1,9},{9,1},{2,10},{10,2},{3,11},{11,3},{4,12},{12,4},... | collective-permute-start | bytes 98312 | tf_op jit(solution)/shard_map/ppermute | solution.py:312
  6.5 30.5 %collective-permute-start.1 = (bf16[4,512,1024]{2,1,0:T(8,128)(2,1)S(1)}, bf16[4,512,1024]{2,1,0:T(8,128)(2,1)}, u32[]{:S(2)}, u32[]{:S(2)}) collective-permute-start(bf16[4,512,1024]{2,1,0:T(8,128)(2,1)S(1)} %constant_dynamic-slice_fusion.2), channel_id=1, source_target_pairs={{0,8},{8,0},{1,9},{9,1},{2,10},{10,2},{3,11},{11,3},{4,12},{12,4},... | collective-permute-start | bytes 12582920 | tf_op jit(solution)/shard_map/ppermute | solution.py:334
  7.4 29.5 %collective-permute-start.2 = (bf16[4,512,1024]{2,1,0:T(8,128)(2,1)S(1)}, bf16[4,512,1024]{2,1,0:T(8,128)(2,1)}, u32[]{:S(2)}, u32[]{:S(2)}) collective-permute-start(bf16[4,512,1024]{2,1,0:T(8,128)(2,1)S(1)} %constant_dynamic-slice_fusion.1), channel_id=1, source_target_pairs={{0,8},{8,0},{1,9},{9,1},{2,10},{10,2},{3,11},{11,3},{4,12},{12,4},... | collective-permute-start | bytes 12582920 | tf_op jit(solution)/shard_map/ppermute | solution.py:335
  36.9 6.0 %copy-start.2 = (bf16[32,64,128]{2,1,0:T(8,128)(2,1)}, bf16[32,64,128]{2,1,0:T(8,128)(2,1)S(1)}, u32[]{:S(2)}) copy-start(bf16[32,64,128]{2,1,0:T(8,128)(2,1)S(1)} %get-tuple-element.63) | copy-start | bytes 1572868
  37.0 6.0 %copy-start.3 = (bf16[32,64,128]{2,1,0:T(8,128)(2,1)}, bf16[32,64,128]{2,1,0:T(8,128)(2,1)S(1)}, u32[]{:S(2)}) copy-start(bf16[32,64,128]{2,1,0:T(8,128)(2,1)S(1)} %get-tuple-element.64) | copy-start | bytes 1572868
  37.0 13.0 %collective-permute-start.3 = (bf16[4,8,64,128]{3,2,1,0:T(8,128)(2,1)S(1)}, bf16[4,8,64,128]{3,2,1,0:T(8,128)(2,1)}, u32[]{:S(2)}, u32[]{:S(2)}) collective-permute-start(bf16[4,8,64,128]{3,2,1,0:T(8,128)(2,1)S(1)} %bitcast.42), channel_id=1, source_target_pairs={{0,2},{2,4},{4,6},{6,0},{1,3},{3,5},{5,7},{7,1},{8,10},{10,12},{12... | collective-permute-start | bytes 1572872 | tf_op jit(solution)/shard_map/ppermute | solution.py:290
  37.7 12.7 %collective-permute-start.4 = (bf16[4,8,64,128]{3,2,1,0:T(8,128)(2,1)S(1)}, bf16[4,8,64,128]{3,2,1,0:T(8,128)(2,1)}, u32[]{:S(2)}, u32[]{:S(2)}) collective-permute-start(bf16[4,8,64,128]{3,2,1,0:T(8,128)(2,1)S(1)} %bitcast.37), channel_id=1, source_target_pairs={{0,16},{16,32},{32,48},{48,0},{1,17},{17,33},{33,49},{49,1},{2,18}... | collective-permute-start | bytes 1572872 | tf_op jit(solution)/shard_map/ppermute | solution.py:290
  38.1 12.3 %collective-permute-start.5 = (bf16[4,8,64,128]{3,2,1,0:T(8,128)(2,1)S(1)}, bf16[4,8,64,128]{3,2,1,0:T(8,128)(2,1)}, u32[]{:S(2)}, u32[]{:S(2)}) collective-permute-start(bf16[4,8,64,128]{3,2,1,0:T(8,128)(2,1)S(1)} %bitcast.43), channel_id=1, source_target_pairs={{0,6},{2,0},{4,2},{6,4},{1,7},{3,1},{5,3},{7,5},{8,14},{10,8},{12,... | collective-permute-start | bytes 1572872 | tf_op jit(solution)/shard_map/ppermute | solution.py:290
  40.2 11.0 %collective-permute-start.6 = (bf16[4,8,64,128]{3,2,1,0:T(8,128)(2,1)S(1)}, bf16[4,8,64,128]{3,2,1,0:T(8,128)(2,1)}, u32[]{:S(2)}, u32[]{:S(2)}) collective-permute-start(bf16[4,8,64,128]{3,2,1,0:T(8,128)(2,1)S(1)} %bitcast.38), channel_id=1, source_target_pairs={{0,48},{16,0},{32,16},{48,32},{1,49},{17,1},{33,17},{49,33},{2,50}... | collective-permute-start | bytes 1572872 | tf_op jit(solution)/shard_map/ppermute | solution.py:290
  51.2 27.6 %collective-permute-start.10 = (bf16[4,8,64,128]{3,2,1,0:T(8,128)(2,1)}, bf16[4,8,64,128]{3,2,1,0:T(8,128)(2,1)S(1)}, u32[]{:S(2)}, u32[]{:S(2)}) collective-permute-start(bf16[4,8,64,128]{3,2,1,0:T(8,128)(2,1)} %bitcast.40), channel_id=1, source_target_pairs={{0,32},{16,48},{32,0},{48,16},{1,33},{17,49},{33,1},{49,17},{2,34}... | collective-permute-start | bytes 1572872 | tf_op jit(solution)/shard_map/ppermute | solution.py:290
  53.3 26.7 %collective-permute-start.9 = (bf16[4,8,64,128]{3,2,1,0:T(8,128)(2,1)}, bf16[4,8,64,128]{3,2,1,0:T(8,128)(2,1)}, u32[]{:S(2)}, u32[]{:S(2)}) collective-permute-start(bf16[4,8,64,128]{3,2,1,0:T(8,128)(2,1)} %bitcast.45), channel_id=1, source_target_pairs={{0,4},{2,6},{4,0},{6,2},{1,5},{3,7},{5,1},{7,3},{8,12},{10,14},{12... | collective-permute-start | bytes 1572872 | tf_op jit(solution)/shard_map/ppermute | solution.py:290
  64.8 25.1 %collective-permute-start.13 = (bf16[32,72,128]{2,1,0:T(8,128)(2,1)}, bf16[32,72,128]{2,1,0:T(8,128)(2,1)S(1)}, u32[]{:S(2)}, u32[]{:S(2)}) collective-permute-start(bf16[32,72,128]{2,1,0:T(8,128)(2,1)} %bitcast.59), channel_id=1, source_target_pairs={{0,16},{16,32},{32,48},{48,0},{1,17},{17,33},{33,49},{49,1},{2,18}... | collective-permute-start | bytes 1769480 | tf_op jit(solution)/shard_map/ppermute | solution.py:290
  66.6 32.3 %collective-permute-start.8 = (bf16[32,72,128]{2,1,0:T(8,128)(2,1)}, bf16[32,72,128]{2,1,0:T(8,128)(2,1)S(1)}, u32[]{:S(2)}, u32[]{:S(2)}) collective-permute-start(bf16[32,72,128]{2,1,0:T(8,128)(2,1)} %bitcast.56), channel_id=1, source_target_pairs={{0,2},{2,4},{4,6},{6,0},{1,3},{3,5},{5,7},{7,1},{8,10},{10,12},{12... | collective-permute-start | bytes 1769480 | tf_op jit(solution)/shard_map/ppermute | solution.py:290
  76.4 22.4 %collective-permute-start.12 = (bf16[32,72,128]{2,1,0:T(8,128)(2,1)}, bf16[32,72,128]{2,1,0:T(8,128)(2,1)}, u32[]{:S(2)}, u32[]{:S(2)}) collective-permute-start(bf16[32,72,128]{2,1,0:T(8,128)(2,1)} %bitcast.58), channel_id=1, source_target_pairs={{0,48},{16,0},{32,16},{48,32},{1,49},{17,1},{33,17},{49,33},{2,50}... | collective-permute-start | bytes 1769480 | tf_op jit(solution)/shard_map/ppermute | solution.py:290
  79.6 19.3 %collective-permute-start.7 = (bf16[32,72,128]{2,1,0:T(8,128)(2,1)}, bf16[32,72,128]{2,1,0:T(8,128)(2,1)S(1)}, u32[]{:S(2)}, u32[]{:S(2)}) collective-permute-start(bf16[32,72,128]{2,1,0:T(8,128)(2,1)} %bitcast.57), channel_id=1, source_target_pairs={{0,6},{2,0},{4,2},{6,4},{1,7},{3,1},{5,3},{7,5},{8,14},{10,8},{12,... | collective-permute-start | bytes 1769480 | tf_op jit(solution)/shard_map/ppermute | solution.py:290
  89.8 11.7 %collective-permute-start.11 = (bf16[32,72,128]{2,1,0:T(8,128)(2,1)}, bf16[32,72,128]{2,1,0:T(8,128)(2,1)}, u32[]{:S(2)}, u32[]{:S(2)}) collective-permute-start(bf16[32,72,128]{2,1,0:T(8,128)(2,1)} %bitcast.61), channel_id=1, source_target_pairs={{0,4},{2,6},{4,0},{6,2},{1,5},{3,7},{5,1},{7,3},{8,12},{10,14},{12... | collective-permute-start | bytes 1769480 | tf_op jit(solution)/shard_map/ppermute | solution.py:290
  89.9 9.0 %copy-start.4 = (bf16[32,72,128]{2,1,0:T(8,128)(2,1)}, bf16[32,72,128]{2,1,0:T(8,128)(2,1)S(1)}, u32[]{:S(2)}) copy-start(bf16[32,72,128]{2,1,0:T(8,128)(2,1)S(1)} %collective-permute-done.13.refs_5_) | copy-start | bytes 1769476
  89.9 11.6 %collective-permute-start.14 = (bf16[32,72,128]{2,1,0:T(8,128)(2,1)}, bf16[32,72,128]{2,1,0:T(8,128)(2,1)}, u32[]{:S(2)}, u32[]{:S(2)}) collective-permute-start(bf16[32,72,128]{2,1,0:T(8,128)(2,1)} %bitcast.60), channel_id=1, source_target_pairs={{0,32},{16,48},{32,0},{48,16},{1,33},{17,49},{33,1},{49,17},{2,34}... | collective-permute-start | bytes 1769480 | tf_op jit(solution)/shard_map/ppermute | solution.py:290
  105.8 29.4 %all-to-all-start.1 = ((bf16[64,72,128]{2,1,0:T(8,128)(2,1)}), bf16[64,72,128]{2,1,0:T(8,128)(2,1)S(1)}, u32[]{:S(2)}, u32[]{:S(2)}) async-start(bf16[64,72,128]{2,1,0:T(8,128)(2,1)} %shard_map.105), calls=%async_computation.1 | async-start | bytes 2359296 | tf_op jit(solution)/shard_map/all_to_all | solution.py:369
  118.2 3.1 %collective-permute-start.15 = (s32[4,8]{1,0:T(4,128)S(1)}, s32[4,8]{1,0:T(4,128)S(1)}, u32[]{:S(2)}, u32[]{:S(2)}) collective-permute-start(s32[4,8]{1,0:T(4,128)S(1)} %get-tuple-element.62), channel_id=1, source_target_pairs={{0,8},{8,0},{1,9},{9,1},{2,10},{10,2},{3,11},{11,3},{4,12},{12,4},... | collective-permute-start | bytes 392 | tf_op jit(solution)/shard_map/ppermute | solution.py:313
  135.8 4.7 %collective-permute-start.16 = (bf16[4,4,8,128]{3,2,1,0:T(8,128)(2,1)S(1)}, bf16[4,4,8,128]{3,2,1,0:T(8,128)(2,1)S(1)}, u32[]{:S(2)}, u32[]{:S(2)}) collective-permute-start(bf16[4,4,8,128]{3,2,1,0:T(8,128)(2,1)S(1)} %get-tuple-element.66), channel_id=1, source_target_pairs={{0,8},{8,0},{1,9},{9,1},{2,10},{10,2},{3,11},{11,3},{4,12},{12,4},... | collective-permute-start | bytes 98312 | tf_op jit(solution)/shard_map/ppermute | solution.py:388
  (3 other events, 10.7 us)

commit v7 on v6

--- a/solution.py
+++ b/solution.py
@@ -35,13 +35,15 @@
     return out
 
 
-def partial_kernel(
-    step, info, lengths, qa_ref, qb_ref, k0_ref, k1_ref, v0_ref, v1_ref, *rest
-):
-    oa_ref, ob_ref = rest[-2:]
+def partial_kernel(step, asks, results, info, lengths, *refs):
+    q_refs = refs[:asks]
+    k0_ref, k1_ref, v0_ref, v1_ref = refs[asks : asks + 4]
     length = k0_ref.shape[1]
-    leads, heads = qa_ref.shape[:2]
-    width = 2 * leads * ROWS
+    heads = q_refs[0].shape[1]
+    leads = sum(r.shape[0] for r in q_refs)
+    o_refs = refs[len(refs) - results :]
+    each = leads // len(o_refs)
+    width = leads * ROWS
     user = (info[1] + (KH - step)) % (lengths.shape[0] // 2)
     limit0 = lengths[info[0] + user] - info[2]
     limit1 = lengths[info[0] + user] - info[3]
@@ -56,12 +58,8 @@
 
     def scores(j):
         cols = columns(j)
-        q = jnp.concatenate(
-            [
-                qa_ref[:, j].reshape(width // 2, HD),
-                qb_ref[:, j].reshape(width // 2, HD),
-            ]
-        )
+        q = [r[:, j].reshape(r.shape[0] * ROWS, HD) for r in q_refs]
+        q = jnp.concatenate(q) if len(q) > 1 else q[0]
         return [
             lax.dot_general(k[0, :, cols], q, rows_dims, preferred_element_type=jnp.float32)
             for k in (k0_ref, k1_ref)
@@ -92,10 +90,9 @@
         top = lax.broadcasted_iota(jnp.int32, (META, width), 0) == 0
         tiles = packed_tiles(numer[:HALF], numer[HALF:])
         notes = packed_tiles(jnp.where(top, peak, low), jnp.where(top, high, low))
-        for d in range(2 * leads):
-            o_ref = oa_ref if d < leads else ob_ref
-            o_ref[d % leads, j, :ROWS, :] = tiles[d].astype(jnp.bfloat16)
-            o_ref[d % leads, j, ROWS:, :] = notes[d].astype(jnp.bfloat16)
+        for d in range(leads):
+            o_refs[d // each][d % each, j, :ROWS, :] = tiles[d].astype(jnp.bfloat16)
+            o_refs[d // each][d % each, j, ROWS:, :] = notes[d].astype(jnp.bfloat16)
 
     live = (limit0 >= length) & (limit1 >= length)
 
@@ -115,10 +112,10 @@
         side = lax.broadcasted_iota(jnp.int32, shape, 2) < ROWS
         first = lax.broadcasted_iota(jnp.int32, shape, 1) == 0
         note = jnp.where(first, jnp.where(side, DEAD, 1.0), 0.0).astype(jnp.bfloat16)
-        for d in range(2 * leads):
-            o_ref = oa_ref if d < leads else ob_ref
-            o_ref[d % leads, :, :ROWS, :] = jnp.zeros((heads, ROWS, HD), jnp.bfloat16)
-            o_ref[d % leads, :, ROWS:, :] = note
+        for d in range(leads):
+            empty = jnp.zeros((heads, ROWS, HD), jnp.bfloat16)
+            o_refs[d // each][d % each, :, :ROWS, :] = empty
+            o_refs[d // each][d % each, :, ROWS:, :] = note
 
     @pl.when(jnp.logical_not(live | dead))
     def _():
@@ -127,11 +124,11 @@
             store(j, *weights(scores(j), True))
 
 
-def partials(step, info, lengths, qa, qb, k0, k1, v0, v1, parts=(0, PARTS), into=()):
-    lead, heads = qa.shape[:2]
-    length = k0.shape[1]
+def partials(step, info, lengths, asked, caches, results=1, parts=(0, PARTS), into=()):
+    heads = asked[0].shape[1]
+    lead = sum(q.shape[0] for q in asked)
+    length = caches[0].shape[1]
     share = heads // PARTS
-    cache = (1, length, share * HD)
     begin, steps = parts
     half = lengths.shape[0] // 2
 
@@ -144,37 +141,31 @@
     def heads_at(p, info, lengths):
         return (0, begin + p, 0, 0)
 
-    out = jax.ShapeDtypeStruct((lead, heads, ROWS + META, HD), jnp.bfloat16)
-    asked = pl.BlockSpec((lead, share, ROWS, HD), heads_at)
-    block = pl.BlockSpec((lead, share, ROWS + META, HD), heads_at)
+    cache = (1, length, share * HD)
+    each = lead // results
+    out = jax.ShapeDtypeStruct((each, heads, ROWS + META, HD), jnp.bfloat16)
     return pl.pallas_call(
-        functools.partial(partial_kernel, step),
+        functools.partial(partial_kernel, step, len(asked), results),
         grid_spec=pltpu.PrefetchScalarGridSpec(
             num_scalar_prefetch=2,
             grid=(steps,),
-            in_specs=[
-                asked,
-                asked,
-                pl.BlockSpec(cache, mine),
-                pl.BlockSpec(cache, other),
-                pl.BlockSpec(cache, mine),
-                pl.BlockSpec(cache, other),
-            ]
+            in_specs=[pl.BlockSpec((q.shape[0], share, ROWS, HD), heads_at) for q in asked]
+            + [pl.BlockSpec(cache, mine), pl.BlockSpec(cache, other)] * 2
             + [pl.BlockSpec(memory_space=pl.ANY)] * len(into),
-            out_specs=[block, block],
-        ),
-        out_shape=[out, out],
-        input_output_aliases={8 + i: i for i in range(len(into))},
+            out_specs=[pl.BlockSpec((each, share, ROWS + META, HD), heads_at)] * results,
+        ),
+        out_shape=[out] * results,
+        input_output_aliases={6 + len(asked) + i: i for i in range(len(into))},
         compiler_params=pltpu.CompilerParams(
             dimension_semantics=("arbitrary",),
             vmem_limit_bytes=60 << 20,
         ),
         cost_estimate=pl.CostEstimate(
-            flops=16 * share * steps * lead * ROWS * HD * length,
+            flops=8 * share * steps * lead * ROWS * HD * length,
             bytes_accessed=8 * length * share * steps * HD,
-            transcendentals=4 * share * steps * lead * ROWS * length,
-        ),
-    )(info, lengths, qa, qb, k0, k1, v0, v1, *into)
+            transcendentals=2 * share * steps * lead * ROWS * length,
+        ),
+    )(info, lengths, *asked, *caches, *into)
 
 
 def stats_of(notes, low):
@@ -183,8 +174,9 @@
     return jnp.where(low, line, turned), jnp.where(low, turned, line) + notes[1:2]
 
 
-def merge_kernel(*refs):
+def merge_kernel(cuts, *refs):
     o_ref, w_ref = refs[-2:]
+    count = o_ref.shape[0]
     low = lax.broadcasted_iota(jnp.int32, (8, HD), 1) < ROWS
     first = lax.broadcasted_iota(jnp.int32, (8, META, HD), 1) == 0
 
@@ -192,8 +184,8 @@
         def note(i, _):
             at = pl.ds(pl.multiple_of(i * 8, 8), 8)
             peaks, masses = [], []
-            for r in parts:
-                notes = r[at, ROWS:, :].astype(jnp.float32)
+            for r, base in parts:
+                notes = r[pl.ds(pl.multiple_of(base + i * 8, 8), 8), ROWS:, :].astype(jnp.float32)
                 line = notes[:, 0, :]
                 turned = pltpu.roll(line, ROWS, 1)
                 peaks.append(jnp.where(low, line, turned))
@@ -214,36 +206,45 @@
 
         def add(t, _):
             acc = None
-            for n, r in enumerate(parts):
-                term = r[t, :ROWS, :].astype(jnp.float32) * w_ref[n, pl.ds(t, 1), :]
+            for n, (r, base) in enumerate(parts):
+                term = r[base + t, :ROWS, :].astype(jnp.float32) * w_ref[n, pl.ds(t, 1), :]
                 acc = term if acc is None else acc + term
             o_ref[t, :ROWS, :] = acc.astype(jnp.bfloat16)
             return 0
 
-        count = parts[0].shape[0]
         lax.fori_loop(0, count // 8, note, 0, unroll=2)
         lax.fori_loop(0, count, add, 0, unroll=4)
 
-    per = (len(refs) - 2) // 2
-    pl.when(pl.program_id(0) == 0)(lambda: join(refs[:per]))
-    pl.when(pl.program_id(0) == 1)(lambda: join(refs[per : 2 * per]))
-
-
-def merged(left, right):
-    count, rows, _ = left[0].shape
+    for h in range(2):
+        parts, at = [], 0
+        for cut in cuts:
+            parts.append((refs[at], h * count) if cut == 1 else (refs[at + h], 0))
+            at += cut
+        pl.when(pl.program_id(0) == h)(functools.partial(join, parts))
+
+
+def merged(parts):
+    cuts = [len(p) for p in parts]
+    arrays = [array for p in parts for array in p]
+    rows = ROWS + META
+    total = sum(array.shape[0] for array in parts[0])
     vmem = pl.BlockSpec(memory_space=pltpu.VMEM)
     return pl.pallas_call(
-        merge_kernel,
+        functools.partial(merge_kernel, cuts),
         grid=(2,),
-        in_specs=[vmem] * (len(left) + len(right)),
-        out_specs=pl.BlockSpec((count, rows, HD), lambda i: (i, 0, 0)),
-        scratch_shapes=[pltpu.VMEM((len(left), count, HD), jnp.float32)],
-        out_shape=jax.ShapeDtypeStruct((2 * count, rows, HD), jnp.bfloat16),
-        compiler_params=pltpu.CompilerParams(dimension_semantics=("arbitrary",), vmem_limit_bytes=52 << 20),
+        in_specs=[vmem] * len(arrays),
+        out_specs=pl.BlockSpec((total // 2, rows, HD), lambda i: (i, 0, 0)),
+        scratch_shapes=[pltpu.VMEM((len(parts), total // 2, HD), jnp.float32)],
+        out_shape=jax.ShapeDtypeStruct((total, rows, HD), jnp.bfloat16),
+        compiler_params=pltpu.CompilerParams(
+            dimension_semantics=("arbitrary",), vmem_limit_bytes=52 << 20
+        ),
         cost_estimate=pl.CostEstimate(
-            flops=16 * left[0].size, bytes_accessed=20 * left[0].size, transcendentals=0
-        ),
-    )(*left, *right)
+            flops=8 * total * rows * HD,
+            bytes_accessed=10 * total * rows * HD,
+            transcendentals=0,
+        ),
+    )(*arrays)
 
 
 def combine_kernel(holders, x_ref, own_ref, value_ref, o_ref, w_ref):
@@ -286,6 +287,10 @@
 
 
 def moved(array, axis, step):
+    if axis == "z":
+        at = [(z % 2) * 2 + z // 2 for z in range(4)]
+        pairs = [(at[z], at[(z + step) % 4]) for z in range(4)]
+        return lax.ppermute(array, ("zl", "zh"), pairs)
     count = SIZES[FINE.index(axis)]
     return lax.ppermute(array, axis, [(i, (i + step) % count) for i in range(count)])
 
@@ -328,45 +333,41 @@
     operand, value_source = lax.optimization_barrier((operand, value_cache))
     got = lax.all_to_all(operand, CHIPS, 0, 0, tiled=True)
     got = got.reshape(chips // KH, KH, ROWS, HD)
-    lead = chips // KH // 2
-    got_a, got_b = got[:lead], got[lead:]
 
     k_other = swap(halves(key_source)[1])
     v_other = swap(halves(value_source)[1])
-    got_a, got_b, k_other, v_other = lax.optimization_barrier(
-        (got_a, got_b, k_other, v_other)
-    )
+    got, k_other, v_other = lax.optimization_barrier((got, k_other, v_other))
 
     offset = (row * KH + col) * length
     other = ((row + 1 - 2 * c) * KH + col) * length
 
     info = jnp.stack([c * half, held, offset, other]).astype(jnp.int32)
 
-    def computed(step, qa, qb, **kept):
-        return partials(
-            step, info, lengths, qa, qb, key_cache, k_other, value_cache, v_other, **kept
-        )
+    caches = (key_cache, k_other, value_cache, v_other)
+    lead = got.shape[0] // 2
+    computed = functools.partial(partials, info=info, lengths=lengths, caches=caches)
 
     def flat(parts):
         return [p.reshape(-1, ROWS + META, HD) for p in parts]
 
-    near = [(moved(got_a, "x", s), moved(got_b, "y", s)) for s in (1, -1)]
-    begun = computed(0, got_a, got_b, parts=(0, PARTS // 2))
-    near, begun, far_a, far_b = lax.optimization_barrier((near, begun, got_a, got_b))
-    asked = {1: near[0], -1: near[1], 2: (moved(far_a, "x", 2), moved(far_b, "y", 2))}
-    left, right = [], []
-    for step, (qa, qb) in asked.items():
-        parts = computed(step, qa, qb)
-        one, two = flat(parts)
-        left.append(moved(one, "x", -step))
-        right.append(moved(two, "y", -step))
-    begun, _ = lax.optimization_barrier((begun, parts))
-    one, two = flat(
-        computed(0, got_a, got_b, parts=(PARTS // 2, PARTS - PARTS // 2), into=begun)
+    ask1 = [moved(got[:lead], "x", 1), moved(got[lead:], "y", 1)]
+    ask3 = [moved(got, "z", -1)]
+    begun = computed(0, asked=[got], parts=(0, PARTS // 2))
+    ask1, begun, far = lax.optimization_barrier((ask1, begun, got))
+    ask2 = [moved(far, "z", 2)]
+    (sum1,) = flat(computed(1, asked=ask1))
+    back = [[moved(sum1, "x", -1)]]
+    ask3, sum1 = lax.optimization_barrier((ask3, sum1))
+    (sum3,) = flat(computed(-1, asked=ask3))
+    back.append([moved(sum3, "y", 1)])
+    ask2, sum3 = lax.optimization_barrier((ask2, sum3))
+    near, far = flat(computed(2, asked=ask2, results=2))
+    back.append([moved(near, "x", -2), moved(far, "z", -2)])
+    begun, _ = lax.optimization_barrier((begun, near))
+    back.append(
+        flat(computed(0, asked=[got], parts=(PARTS // 2, PARTS - PARTS // 2), into=begun))
     )
-    left.append(one)
-    right.append(two)
-    arrived = lax.all_to_all(merged(left, right), CHIPS, 0, 0, tiled=True)
+    arrived = lax.all_to_all(merged(back), CHIPS, 0, 0, tiled=True)
 
     codes = jnp.arange(key_table.shape[0], dtype=jnp.int32)
     onehot = (tokens[..., None] == codes).astype(jnp.bfloat16)

time: 141 us -> 146 us (1.035)
  starting transfers between devices: 37.2 us -> 46 us
  waiting for transfers between devices: 16.2 us -> 11.4 us
    ppermute x12 -> x5, starting transfers between devices: 16.2 us -> 5.12 us  [moved(): lax.ppermute(array, axis, [(i, (i + step) % count) for i in range(count)])]
    all_to_all x1, waiting for transfers between devices: 10.1 us -> 0.01 us  [body(): arrived = lax.all_to_all(merged(back), CHIPS, 0, 0, tiled=True)]
    ppermute x1, starting transfers between devices: 2.31 us -> 9.94 us  [body(): tokens = jnp.concatenate([t_mine, swap(t_give)], axis=1)]
    ppermute x1, starting transfers between devices: 3.8 us -> 10.2 us  [body(): received = swap(result[:, :, beams:])]
    all_to_all x1, starting transfers between devices: 12.5 us -> 16.2 us  [body(): arrived = lax.all_to_all(merged(back), CHIPS, 0, 0, tiled=True)]
    ppermute x0 -> x3, waiting for transfers between devices: none -> 3.58 us  [moved(): return lax.ppermute(array, ('zl', 'zh'), pairs)]
    ppermute x0 -> x3, starting transfers between devices: none -> 2.83 us  [moved(): return lax.ppermute(array, ('zl', 'zh'), pairs)]
    ppermute x12 -> x5, waiting for transfers between devices: 4.39 us -> 6.11 us  [moved(): lax.ppermute(array, axis, [(i, (i + step) % count) for i in range(count)])]
  transfers between devices with their start and end apart: 18 -> 14, of which waited for: 7 -> 8; matrix products, arithmetic and copies ran while one was open for 6% -> 6% of each run, Pallas kernels for 30% -> 29%
where the time goes in v7:
time: 146 us; the launch traced here: 145 us
  Pallas kernels  47.4 us (32%)
  starting transfers between devices  46 us (32%)
  blocking collectives  27.8 us (19%)
  waiting for transfers between devices  11.4 us (8%)
  local copies, waits for them, and re-layouts  9.54 us (7%)
  other arithmetic  1.76 us (1%)
    pallas_call x5, Pallas kernels, partials(): pl.pallas_call(functools.partial(partial_kernel, step, len(asked), result...  42.6 us
    all_to_all x1, blocking collectives, body(): got = lax.all_to_all(operand, CHIPS, 0, 0, tiled=True)  27.8 us
    all_to_all x1, starting transfers between devices, body(): arrived = lax.all_to_all(merged(back), CHIPS, 0, 0, tiled=True)  16.2 us
    ppermute x1, starting transfers between devices, body(): received = swap(result[:, :, beams:])  10.2 us
    ppermute x1, starting transfers between devices, body(): tokens = jnp.concatenate([t_mine, swap(t_give)], axis=1)  9.94 us
    ppermute x5, waiting for transfers between devices, moved(): lax.ppermute(array, axis, [(i, (i + step) % count) for i in range(count)])  6.11 us
    ppermute x5, starting transfers between devices, moved(): lax.ppermute(array, axis, [(i, (i + step) % count) for i in range(count)])  5.12 us
    pallas_call x1, Pallas kernels, merged(): pl.pallas_call(functools.partial(merge_kernel, cuts), grid=(2,), in_specs...  4.25 us
  transfers between devices with their start and end apart: 14, of which 8 were waited for; matrix products, arithmetic and copies ran while one was open for 6% of the time, Pallas kernels for 29%

profile of v7, /device:TPU:1, one launch (start us, length us, event | category | flops | bytes accessed | tf_op | source)
XLA Modules:
  0.0 145.4 jit_solution(1377906790859909756)
XLA Ops:
  0.0 0.9 dynamic-slice_bitcast_fusion
  1.7 1.5 %collective-permute-start = (bf16[4,4,8,128]{3,2,1,0:T(8,128)(2,1)S(1)}, bf16[4,4,8,128]{3,2,1,0:T(8,128)(2,1)S(1)}, u32[]{:S(2)}, u32[]{:S(2)}) collective-permute-start(bf16[4,4,8,128]{3,2,1,0:T(8,128)(2,1)S(1)} %get-tuple-element.22), channel_id=1, source_target_pairs={{0,8},{8,0},{1,9},{9,1},{2,10},{10,2},{3,11},{11,3},{4,12},{12,4},... | collective-permute-start | bytes 98312 | tf_op jit(solution)/shard_map/ppermute | solution.py:317
  3.2 2.8 %constant_dynamic-slice_fusion.2 = bf16[4,512,1024]{2,1,0:T(8,128)(2,1)S(1)} fusion(bf16[8,512,1024]{2,1,0:T(8,128)(2,1)} %refs_1_.7, s32[]{:T(128)S(6)} %select_n.42), kind=kLoop, calls=%fused_computation.34 | loop fusion | bytes 8388612 | tf_op jit(solution)/shard_map/dynamic_slice | solution.py:310
  6.5 1.4 copy-done.1
  8.4 27.8 %all_to_all.10 = bf16[64,64,128]{2,1,0:T(8,128)(2,1)S(1)} all-to-all(bf16[64,64,128]{2,1,0:T(8,128)(2,1)S(1)} %select_select_fusion), channel_id=1, replica_groups=mesh['zl'=2,'y'=4,'c'=2,'x'=4,'zh'=2] {'zl','y','x','zh'}, dimensions={0} | all-to-all | bytes 2097152 | tf_op jit(solution)/shard_map/all_to_all | solution.py:334
  36.2 1.1 collective-permute-start.6
  37.3 1.1 fusion.15
  40.1 6.5 %shard_map.100.refs_5_ = bf16[8,8,72,128]{3,2,1,0:T(8,128)(2,1)} custom-call(s32[4]{0:T(128)} %pad_add_fusion.1.info, s32[8]{0:T(128)} %lengths.9, bf16[8,8,64,128]{3,2,1,0:T(8,128)(2,1)} %bitcast.35, bf16[8,512,1024]{2,1,0:T(8,128)(2,1)} %refs_1_.7, bf16[4,512,1024]{2,1,0:T(8,128)(2,1)} %collective-permute-done.1.refs_2_.refs_3_, ...), custom_call_target="tpu_custom_call" | custom-call | flops 1073741824 | bytes 2097152 | tf_op jit(solution)/shard_map/pallas_call | solution.py:147
  46.6 4.0 %collective-permute-done.3.refs_0_ = bf16[4,8,64,128]{3,2,1,0:T(8,128)(2,1)} collective-permute-done((bf16[4,8,64,128]{3,2,1,0:T(8,128)(2,1)}, bf16[4,8,64,128]{3,2,1,0:T(8,128)(2,1)}, u32[]{:S(2)}, u32[]{:S(2)}) %collective-permute-start.3) | collective-permute-done | bytes 524320 | tf_op jit(solution)/shard_map/ppermute | solution.py:295
  50.6 1.1 collective-permute-done.4.refs_1_
  52.6 9.9 %shard_map.101 = bf16[8,8,72,128]{3,2,1,0:T(8,128)(2,1)} custom-call(s32[4]{0:T(128)} %pad_add_fusion.1.info, s32[8]{0:T(128)} %lengths.9, bf16[4,8,64,128]{3,2,1,0:T(8,128)(2,1)} %collective-permute-done.3.refs_0_, bf16[4,8,64,128]{3,2,1,0:T(8,128)(2,1)} %collective-permute-done.4.refs_1_, bf16[8,512,1024]{2,1,0:T(8,128)(2,1)} %refs_1_.7, ...), custom_call_target="tpu_custom_call" | custom-call | flops 2147483648 | bytes 4194304 | tf_op jit(solution)/shard_map/pallas_call | solution.py:147
  62.5 1.5 %collective-permute-start.5 = (bf16[64,72,128]{2,1,0:T(8,128)(2,1)}, bf16[64,72,128]{2,1,0:T(8,128)(2,1)}, u32[]{:S(2)}, u32[]{:S(2)}) collective-permute-start(bf16[64,72,128]{2,1,0:T(8,128)(2,1)} %bitcast.40), channel_id=1, source_target_pairs={{0,6},{2,0},{4,2},{6,4},{1,7},{3,1},{5,3},{7,5},{8,14},{10,8},{12,... | collective-permute-start | bytes 3538952 | tf_op jit(solution)/shard_map/ppermute | solution.py:295
  64.0 9.8 %shard_map.102 = bf16[8,8,72,128]{3,2,1,0:T(8,128)(2,1)} custom-call(s32[4]{0:T(128)} %pad_add_fusion.1.info, s32[8]{0:T(128)} %lengths.9, bf16[8,8,64,128]{3,2,1,0:T(8,128)(2,1)} %collective-permute-done.6.refs_0_, bf16[8,512,1024]{2,1,0:T(8,128)(2,1)} %refs_1_.7, bf16[4,512,1024]{2,1,0:T(8,128)(2,1)} %collective-permute-done.1.refs_2_.refs_3_, ...), custom_call_target="tpu_custom_call" | custom-call | flops 2147483648 | bytes 4194304 | tf_op jit(solution)/shard_map/pallas_call | solution.py:147
  73.8 1.1 collective-permute-done.8.refs_0_
  74.9 9.9 %shard_map.103 = (bf16[4,8,72,128]{3,2,1,0:T(8,128)(2,1)}, bf16[4,8,72,128]{3,2,1,0:T(8,128)(2,1)}) custom-call(s32[4]{0:T(128)} %pad_add_fusion.1.info, s32[8]{0:T(128)} %lengths.9, bf16[8,8,64,128]{3,2,1,0:T(8,128)(2,1)} %collective-permute-done.8.refs_0_, bf16[8,512,1024]{2,1,0:T(8,128)(2,1)} %refs_1_.7, ...), custom_call_target="tpu_custom_call" | custom-call | flops 2147483648 | bytes 4194304 | tf_op jit(solution)/shard_map/pallas_call | solution.py:147
  85.6 2.5 %collective-permute-start.9 = (bf16[32,72,128]{2,1,0:T(8,128)(2,1)}, bf16[32,72,128]{2,1,0:T(8,128)(2,1)S(1)}, u32[]{:S(2)}, u32[]{:S(2)}) collective-permute-start(bf16[32,72,128]{2,1,0:T(8,128)(2,1)} %bitcast.48), channel_id=1, source_target_pairs={{0,4},{2,6},{4,0},{6,2},{1,5},{3,7},{5,1},{7,3},{8,12},{10,14},{12... | collective-permute-start | bytes 1769480 | tf_op jit(solution)/shard_map/ppermute | solution.py:295
  88.2 6.5 %shard_map.104 = bf16[8,8,72,128]{3,2,1,0:T(8,128)(2,1)} custom-call(s32[4]{0:T(128)} %pad_add_fusion.1.info, s32[8]{0:T(128)} %lengths.9, bf16[8,8,64,128]{3,2,1,0:T(8,128)(2,1)} %bitcast.37, bf16[8,512,1024]{2,1,0:T(8,128)(2,1)} %refs_1_.7, bf16[4,512,1024]{2,1,0:T(8,128)(2,1)} %collective-permute-done.1.refs_2_.refs_3_, ...), custom_call_target="tpu_custom_call", output_to_operand_aliasing={{}: (7, {})} | custom-call | flops 1073741824 | bytes 2097152 | tf_op jit(solution)/shard_map/pallas_call | solution.py:147
  94.6 2.5 %collective-permute-done.10.refs_3_ = bf16[32,72,128]{2,1,0:T(8,128)(2,1)S(1)} collective-permute-done((bf16[32,72,128]{2,1,0:T(8,128)(2,1)}, bf16[32,72,128]{2,1,0:T(8,128)(2,1)S(1)}, u32[]{:S(2)}, u32[]{:S(2)}) %collective-permute-start.10) | collective-permute-done | bytes 589856 | tf_op jit(solution)/shard_map/ppermute | solution.py:293
  98.1 4.2 %shard_map.105 = bf16[64,72,128]{2,1,0:T(8,128)(2,1)} custom-call(bf16[64,72,128]{2,1,0:T(8,128)(2,1)} %collective-permute-done.5.refs_0_, bf16[64,72,128]{2,1,0:T(8,128)(2,1)} %collective-permute-done.7.refs_1_, bf16[32,72,128]{2,1,0:T(8,128)(2,1)S(1)} %collective-permute-done.9.refs_2_, bf16[32,72,128]{2,1,0:T(8,128)(2,1)S(1)} %collective-permute-done.10.refs_3_, ...), custom_call_target="tpu_custom_call" | custom-call | flops 4718592 | bytes 5898240 | tf_op jit(solution)/shard_map/pallas_call | solution.py:232
  102.4 16.2 %all-to-all-start.1 = ((bf16[64,72,128]{2,1,0:T(8,128)(2,1)}), bf16[64,72,128]{2,1,0:T(8,128)(2,1)S(1)}, u32[]{:S(2)}, u32[]{:S(2)}) async-start(bf16[64,72,128]{2,1,0:T(8,128)(2,1)} %shard_map.105), calls=%async_computation.1 | async-start | bytes 2359296 | tf_op jit(solution)/shard_map/all_to_all | solution.py:370
  118.6 9.9 %collective-permute-start.11 = (s32[4,8]{1,0:T(4,128)S(1)}, s32[4,8]{1,0:T(4,128)S(1)}, u32[]{:S(2)}, u32[]{:S(2)}) collective-permute-start(s32[4,8]{1,0:T(4,128)S(1)} %get-tuple-element.38), channel_id=1, source_target_pairs={{0,8},{8,0},{1,9},{9,1},{2,10},{10,2},{3,11},{11,3},{4,12},{12,4},... | collective-permute-start | bytes 392 | tf_op jit(solution)/shard_map/ppermute | solution.py:318
  130.5 1.1 copy.14.value_ref
  131.6 1.2 fusion.2
  133.7 10.2 %collective-permute-start.12 = (bf16[4,4,8,128]{3,2,1,0:T(8,128)(2,1)S(1)}, bf16[4,4,8,128]{3,2,1,0:T(8,128)(2,1)S(1)}, u32[]{:S(2)}, u32[]{:S(2)}) collective-permute-start(bf16[4,4,8,128]{3,2,1,0:T(8,128)(2,1)S(1)} %get-tuple-element.42), channel_id=1, source_target_pairs={{0,8},{8,0},{1,9},{9,1},{2,10},{10,2},{3,11},{11,3},{4,12},{12,4},... | collective-permute-start | bytes 98312 | tf_op jit(solution)/shard_map/ppermute | solution.py:389
  (46 shorter events, 10.5 us)
Async XLA Ops:
  0.0 129.4 %copy-start = (bf16[1024,1024]{1,0:T(8,128)(2,1)S(1)}, bf16[1024,1024]{1,0:T(8,128)(2,1)}, u32[]{:S(2)}) copy-start(bf16[1024,1024]{1,0:T(8,128)(2,1)} %param.14) | copy-start | bytes 6291460
  1.7 4.4 %copy-start.3 = (pred[64]{0:T(512)(128)(4,1)S(1)}, pred[64]{0:T(512)(128)(4,1)}, u32[]{:S(2)}) copy-start(pred[64]{0:T(512)(128)(4,1)} %constant.60) | copy-start | bytes 196
  1.7 4.5 %copy-start.4 = (pred[64]{0:T(512)(128)(4,1)S(1)}, pred[64]{0:T(512)(128)(4,1)}, u32[]{:S(2)}) copy-start(pred[64]{0:T(512)(128)(4,1)} %constant.61) | copy-start | bytes 196
  1.7 4.5 %copy-start.5 = (pred[64]{0:T(512)(128)(4,1)S(1)}, pred[64]{0:T(512)(128)(4,1)}, u32[]{:S(2)}) copy-start(pred[64]{0:T(512)(128)(4,1)} %constant.62) | copy-start | bytes 196
  1.7 4.4 %collective-permute-start = (bf16[4,4,8,128]{3,2,1,0:T(8,128)(2,1)S(1)}, bf16[4,4,8,128]{3,2,1,0:T(8,128)(2,1)S(1)}, u32[]{:S(2)}, u32[]{:S(2)}) collective-permute-start(bf16[4,4,8,128]{3,2,1,0:T(8,128)(2,1)S(1)} %get-tuple-element.22), channel_id=1, source_target_pairs={{0,8},{8,0},{1,9},{9,1},{2,10},{10,2},{3,11},{11,3},{4,12},{12,4},... | collective-permute-start | bytes 98312 | tf_op jit(solution)/shard_map/ppermute | solution.py:317
  3.2 4.6 %copy-start.1 = (bf16[8,512,1024]{2,1,0:T(8,128)(2,1)S(1)}, bf16[8,512,1024]{2,1,0:T(8,128)(2,1)}, u32[]{:S(2)}) copy-start(bf16[8,512,1024]{2,1,0:T(8,128)(2,1)} %refs_3_.7) | copy-start | bytes 25165828
  6.0 30.1 %collective-permute-start.1 = (bf16[4,512,1024]{2,1,0:T(8,128)(2,1)S(1)}, bf16[4,512,1024]{2,1,0:T(8,128)(2,1)}, u32[]{:S(2)}, u32[]{:S(2)}) collective-permute-start(bf16[4,512,1024]{2,1,0:T(8,128)(2,1)S(1)} %constant_dynamic-slice_fusion.2), channel_id=1, source_target_pairs={{0,8},{8,0},{1,9},{9,1},{2,10},{10,2},{3,11},{11,3},{4,12},{12,4},... | collective-permute-start | bytes 12582920 | tf_op jit(solution)/shard_map/ppermute | solution.py:337
  8.3 27.9 %collective-permute-start.2 = (bf16[4,512,1024]{2,1,0:T(8,128)(2,1)S(1)}, bf16[4,512,1024]{2,1,0:T(8,128)(2,1)}, u32[]{:S(2)}, u32[]{:S(2)}) collective-permute-start(bf16[4,512,1024]{2,1,0:T(8,128)(2,1)S(1)} %constant_dynamic-slice_fusion.1), channel_id=1, source_target_pairs={{0,8},{8,0},{1,9},{9,1},{2,10},{10,2},{3,11},{11,3},{4,12},{12,4},... | collective-permute-start | bytes 12582920 | tf_op jit(solution)/shard_map/ppermute | solution.py:338
  36.2 4.0 %copy-start.2 = (bf16[64,64,128]{2,1,0:T(8,128)(2,1)}, bf16[64,64,128]{2,1,0:T(8,128)(2,1)S(1)}, u32[]{:S(2)}) copy-start(bf16[64,64,128]{2,1,0:T(8,128)(2,1)S(1)} %all_to_all.10) | copy-start | bytes 3145732
  36.2 27.8 %collective-permute-start.6 = (bf16[8,8,64,128]{3,2,1,0:T(8,128)(2,1)S(1)}, bf16[8,8,64,128]{3,2,1,0:T(8,128)(2,1)}, u32[]{:S(2)}, u32[]{:S(2)}) collective-permute-start(bf16[8,8,64,128]{3,2,1,0:T(8,128)(2,1)S(1)} %bitcast.33), channel_id=1, source_target_pairs={{0,65},{64,0},{1,64},{65,1},{2,67},{66,2},{3,66},{67,3},{4,69},{68... | collective-permute-start | bytes 3145736 | tf_op jit(solution)/shard_map/ppermute | solution.py:293
  38.4 12.2 %collective-permute-start.3 = (bf16[4,8,64,128]{3,2,1,0:T(8,128)(2,1)}, bf16[4,8,64,128]{3,2,1,0:T(8,128)(2,1)}, u32[]{:S(2)}, u32[]{:S(2)}) collective-permute-start(bf16[4,8,64,128]{3,2,1,0:T(8,128)(2,1)} %get-tuple-element.40), channel_id=1, source_target_pairs={{0,2},{2,4},{4,6},{6,0},{1,3},{3,5},{5,7},{7,1},{8,10},{10,12},{12... | collective-permute-start | bytes 1572872 | tf_op jit(solution)/shard_map/ppermute | solution.py:295
  39.2 12.6 %collective-permute-start.4 = (bf16[4,8,64,128]{3,2,1,0:T(8,128)(2,1)}, bf16[4,8,64,128]{3,2,1,0:T(8,128)(2,1)}, u32[]{:S(2)}, u32[]{:S(2)}) collective-permute-start(bf16[4,8,64,128]{3,2,1,0:T(8,128)(2,1)} %get-tuple-element.39), channel_id=1, source_target_pairs={{0,16},{16,32},{32,48},{48,0},{1,17},{17,33},{33,49},{49,1},{2,18}... | collective-permute-start | bytes 1572872 | tf_op jit(solution)/shard_map/ppermute | solution.py:295
  51.7 23.2 %collective-permute-start.8 = (bf16[8,8,64,128]{3,2,1,0:T(8,128)(2,1)}, bf16[8,8,64,128]{3,2,1,0:T(8,128)(2,1)}, u32[]{:S(2)}, u32[]{:S(2)}) collective-permute-start(bf16[8,8,64,128]{3,2,1,0:T(8,128)(2,1)} %bitcast.36), channel_id=1, source_target_pairs={{0,1},{64,65},{1,0},{65,64},{2,3},{66,67},{3,2},{67,66},{4,5},{68,... | collective-permute-start | bytes 3145736 | tf_op jit(solution)/shard_map/ppermute | solution.py:293
  62.5 32.2 %collective-permute-start.5 = (bf16[64,72,128]{2,1,0:T(8,128)(2,1)}, bf16[64,72,128]{2,1,0:T(8,128)(2,1)}, u32[]{:S(2)}, u32[]{:S(2)}) collective-permute-start(bf16[64,72,128]{2,1,0:T(8,128)(2,1)} %bitcast.40), channel_id=1, source_target_pairs={{0,6},{2,0},{4,2},{6,4},{1,7},{3,1},{5,3},{7,5},{8,14},{10,8},{12,... | collective-permute-start | bytes 3538952 | tf_op jit(solution)/shard_map/ppermute | solution.py:295
  73.8 24.3 %collective-permute-start.7 = (bf16[64,72,128]{2,1,0:T(8,128)(2,1)}, bf16[64,72,128]{2,1,0:T(8,128)(2,1)}, u32[]{:S(2)}, u32[]{:S(2)}) collective-permute-start(bf16[64,72,128]{2,1,0:T(8,128)(2,1)} %bitcast.39), channel_id=1, source_target_pairs={{0,16},{16,32},{32,48},{48,0},{1,17},{17,33},{33,49},{49,1},{2,18}... | collective-permute-start | bytes 3538952 | tf_op jit(solution)/shard_map/ppermute | solution.py:295
  84.8 12.3 %collective-permute-start.10 = (bf16[32,72,128]{2,1,0:T(8,128)(2,1)}, bf16[32,72,128]{2,1,0:T(8,128)(2,1)S(1)}, u32[]{:S(2)}, u32[]{:S(2)}) collective-permute-start(bf16[32,72,128]{2,1,0:T(8,128)(2,1)} %bitcast.49), channel_id=1, source_target_pairs={{0,1},{64,65},{1,0},{65,64},{2,3},{66,67},{3,2},{67,66},{4,5},{68,... | collective-permute-start | bytes 1769480 | tf_op jit(solution)/shard_map/ppermute | solution.py:293
  85.6 11.7 %collective-permute-start.9 = (bf16[32,72,128]{2,1,0:T(8,128)(2,1)}, bf16[32,72,128]{2,1,0:T(8,128)(2,1)S(1)}, u32[]{:S(2)}, u32[]{:S(2)}) collective-permute-start(bf16[32,72,128]{2,1,0:T(8,128)(2,1)} %bitcast.48), channel_id=1, source_target_pairs={{0,4},{2,6},{4,0},{6,2},{1,5},{3,7},{5,1},{7,3},{8,12},{10,14},{12... | collective-permute-start | bytes 1769480 | tf_op jit(solution)/shard_map/ppermute | solution.py:295
  102.4 30.7 %all-to-all-start.1 = ((bf16[64,72,128]{2,1,0:T(8,128)(2,1)}), bf16[64,72,128]{2,1,0:T(8,128)(2,1)S(1)}, u32[]{:S(2)}, u32[]{:S(2)}) async-start(bf16[64,72,128]{2,1,0:T(8,128)(2,1)} %shard_map.105), calls=%async_computation.1 | async-start | bytes 2359296 | tf_op jit(solution)/shard_map/all_to_all | solution.py:370
  118.6 10.8 %collective-permute-start.11 = (s32[4,8]{1,0:T(4,128)S(1)}, s32[4,8]{1,0:T(4,128)S(1)}, u32[]{:S(2)}, u32[]{:S(2)}) collective-permute-start(s32[4,8]{1,0:T(4,128)S(1)} %get-tuple-element.38), channel_id=1, source_target_pairs={{0,8},{8,0},{1,9},{9,1},{2,10},{10,2},{3,11},{11,3},{4,12},{12,4},... | collective-permute-start | bytes 392 | tf_op jit(solution)/shard_map/ppermute | solution.py:318
  133.7 11.1 %collective-permute-start.12 = (bf16[4,4,8,128]{3,2,1,0:T(8,128)(2,1)S(1)}, bf16[4,4,8,128]{3,2,1,0:T(8,128)(2,1)S(1)}, u32[]{:S(2)}, u32[]{:S(2)}) collective-permute-start(bf16[4,4,8,128]{3,2,1,0:T(8,128)(2,1)S(1)} %get-tuple-element.42), channel_id=1, source_target_pairs={{0,8},{8,0},{1,9},{9,1},{2,10},{10,2},{3,11},{11,3},{4,12},{12,4},... | collective-permute-start | bytes 98312 | tf_op jit(solution)/shard_map/ppermute | solution.py:389

commit v8 on v7

--- a/solution.py
+++ b/solution.py
@@ -351,10 +351,10 @@
         return [p.reshape(-1, ROWS + META, HD) for p in parts]
 
     ask1 = [moved(got[:lead], "x", 1), moved(got[lead:], "y", 1)]
-    ask3 = [moved(got, "z", -1)]
+    ask3 = [moved(got[:lead], "x", -1), moved(got[lead:], "y", -1)]
+    ask2 = [moved(got, "z", 2)]
     begun = computed(0, asked=[got], parts=(0, PARTS // 2))
-    ask1, begun, far = lax.optimization_barrier((ask1, begun, got))
-    ask2 = [moved(far, "z", 2)]
+    ask1, ask3, begun = lax.optimization_barrier((ask1, ask3, begun))
     (sum1,) = flat(computed(1, asked=ask1))
     back = [[moved(sum1, "x", -1)]]
     ask3, sum1 = lax.optimization_barrier((ask3, sum1))

time: 146 us -> 148 us (1.014)
  waiting for transfers between devices: 11.4 us -> 18.9 us
  starting transfers between devices: 46 us -> 40.1 us
    all_to_all x1, waiting for transfers between devices: 0.01 us -> 9.9 us  [body(): arrived = lax.all_to_all(merged(back), CHIPS, 0, 0, tiled=True)]
    ppermute x1, starting transfers between devices: 9.94 us -> 2.41 us  [body(): tokens = jnp.concatenate([t_mine, swap(t_give)], axis=1)]
    all_to_all x1, starting transfers between devices: 16.2 us -> 22.6 us  [body(): arrived = lax.all_to_all(merged(back), CHIPS, 0, 0, tiled=True)]
    ppermute x1, starting transfers between devices: 10.2 us -> 3.89 us  [body(): received = swap(result[:, :, beams:])]
    ppermute x3 -> x2, waiting for transfers between devices: 3.58 us -> 0.01 us  [moved(): return lax.ppermute(array, ('zl', 'zh'), pairs)]
    ppermute x5 -> x7, starting transfers between devices: 5.12 us -> 8.04 us  [moved(): lax.ppermute(array, axis, [(i, (i + step) % count) for i in range(count)])]
    ppermute x5 -> x7, waiting for transfers between devices: 6.11 us -> 7.33 us  [moved(): lax.ppermute(array, axis, [(i, (i + step) % count) for i in range(count)])]
  transfers between devices with their start and end apart: 14 -> 15, of which waited for: 8 -> 6; matrix products, arithmetic and copies ran while one was open for 6% -> 5% of each run, Pallas kernels for 29% -> 29%
where the time goes in v8:
time: 148 us; the launch traced here: 147 us
  Pallas kernels  47.6 us (32%)
  starting transfers between devices  40.1 us (27%)
  blocking collectives  27.8 us (19%)
  waiting for transfers between devices  18.9 us (13%)
  local copies, waits for them, and re-layouts  9.7 us (7%)
  other arithmetic  1.72 us (1%)
    pallas_call x5, Pallas kernels, partials(): pl.pallas_call(functools.partial(partial_kernel, step, len(asked), result...  42.7 us
    all_to_all x1, blocking collectives, body(): got = lax.all_to_all(operand, CHIPS, 0, 0, tiled=True)  27.8 us
    all_to_all x1, starting transfers between devices, body(): arrived = lax.all_to_all(merged(back), CHIPS, 0, 0, tiled=True)  22.6 us
    all_to_all x1, waiting for transfers between devices, body(): arrived = lax.all_to_all(merged(back), CHIPS, 0, 0, tiled=True)  9.9 us
    ppermute x7, starting transfers between devices, moved(): lax.ppermute(array, axis, [(i, (i + step) % count) for i in range(count)])  8.04 us
    ppermute x7, waiting for transfers between devices, moved(): lax.ppermute(array, axis, [(i, (i + step) % count) for i in range(count)])  7.33 us
    pallas_call x1, Pallas kernels, merged(): pl.pallas_call(functools.partial(merge_kernel, cuts), grid=(2,), in_specs...  4.31 us
    dynamic_slice x3, local copies, waits for them, and re-layouts, halves(): lax.dynamic_slice_in_dim(array, (1 - c) * half, half, 0)  4.17 us
  transfers between devices with their start and end apart: 15, of which 6 were waited for; matrix products, arithmetic and copies ran while one was open for 5% of the time, Pallas kernels for 29%

profile of v8, /device:TPU:1, one launch (start us, length us, event | category | flops | bytes accessed | tf_op | source)
XLA Modules:
  0.0 147.4 jit_solution(12114810450391546971)
XLA Ops:
  0.0 0.9 dynamic-slice_bitcast_fusion
  1.7 1.5 %collective-permute-start = (bf16[4,4,8,128]{3,2,1,0:T(8,128)(2,1)S(1)}, bf16[4,4,8,128]{3,2,1,0:T(8,128)(2,1)S(1)}, u32[]{:S(2)}, u32[]{:S(2)}) collective-permute-start(bf16[4,4,8,128]{3,2,1,0:T(8,128)(2,1)S(1)} %get-tuple-element.24), channel_id=1, source_target_pairs={{0,8},{8,0},{1,9},{9,1},{2,10},{10,2},{3,11},{11,3},{4,12},{12,4},... | collective-permute-start | bytes 98312 | tf_op jit(solution)/shard_map/ppermute | solution.py:317
  3.2 2.8 %constant_dynamic-slice_fusion.2 = bf16[4,512,1024]{2,1,0:T(8,128)(2,1)S(1)} fusion(bf16[8,512,1024]{2,1,0:T(8,128)(2,1)} %refs_1_.5, s32[]{:T(128)S(6)} %select_n.42), kind=kLoop, calls=%fused_computation.34 | loop fusion | bytes 8388612 | tf_op jit(solution)/shard_map/dynamic_slice | solution.py:310
  6.5 1.4 copy-done.1
  8.4 27.8 %all_to_all.10 = bf16[64,64,128]{2,1,0:T(8,128)(2,1)S(1)} all-to-all(bf16[64,64,128]{2,1,0:T(8,128)(2,1)S(1)} %select_select_fusion), channel_id=1, replica_groups=mesh['zl'=2,'y'=4,'c'=2,'x'=4,'zh'=2] {'zl','y','x','zh'}, dimensions={0} | all-to-all | bytes 2097152 | tf_op jit(solution)/shard_map/all_to_all | solution.py:334
  36.2 1.3 fusion.15
  38.9 2.1 %collective-permute-start.5 = (bf16[4,8,64,128]{3,2,1,0:T(8,128)(2,1)}, bf16[4,8,64,128]{3,2,1,0:T(8,128)(2,1)}, u32[]{:S(2)}, u32[]{:S(2)}) collective-permute-start(bf16[4,8,64,128]{3,2,1,0:T(8,128)(2,1)} %get-tuple-element.44), channel_id=1, source_target_pairs={{0,6},{2,0},{4,2},{6,4},{1,7},{3,1},{5,3},{7,5},{8,14},{10,8},{12,... | collective-permute-start | bytes 1572872 | tf_op jit(solution)/shard_map/ppermute | solution.py:295
  41.0 1.8 %collective-permute-start.6 = (bf16[4,8,64,128]{3,2,1,0:T(8,128)(2,1)}, bf16[4,8,64,128]{3,2,1,0:T(8,128)(2,1)}, u32[]{:S(2)}, u32[]{:S(2)}) collective-permute-start(bf16[4,8,64,128]{3,2,1,0:T(8,128)(2,1)} %get-tuple-element.43), channel_id=1, source_target_pairs={{0,48},{16,0},{32,16},{48,32},{1,49},{17,1},{33,17},{49,33},{2,50}... | collective-permute-start | bytes 1572872 | tf_op jit(solution)/shard_map/ppermute | solution.py:295
  42.8 1.2 collective-permute-start.9
  44.6 6.6 %shard_map.100.refs_5_ = bf16[8,8,72,128]{3,2,1,0:T(8,128)(2,1)} custom-call(s32[4]{0:T(128)} %pad_add_fusion.1.info, s32[8]{0:T(128)} %lengths.9, bf16[8,8,64,128]{3,2,1,0:T(8,128)(2,1)} %bitcast.35, bf16[8,512,1024]{2,1,0:T(8,128)(2,1)} %refs_1_.5, bf16[4,512,1024]{2,1,0:T(8,128)(2,1)} %collective-permute-done.1.refs_2_.refs_3_, ...), custom_call_target="tpu_custom_call" | custom-call | flops 1073741824 | bytes 2097152 | tf_op jit(solution)/shard_map/pallas_call | solution.py:147
  51.9 9.9 %shard_map.101 = bf16[8,8,72,128]{3,2,1,0:T(8,128)(2,1)} custom-call(s32[4]{0:T(128)} %pad_add_fusion.1.info, s32[8]{0:T(128)} %lengths.9, bf16[4,8,64,128]{3,2,1,0:T(8,128)(2,1)} %collective-permute-done.3.refs_0_, bf16[4,8,64,128]{3,2,1,0:T(8,128)(2,1)} %collective-permute-done.4.refs_1_, bf16[8,512,1024]{2,1,0:T(8,128)(2,1)} %refs_1_.5, ...), custom_call_target="tpu_custom_call" | custom-call | flops 2147483648 | bytes 4194304 | tf_op jit(solution)/shard_map/pallas_call | solution.py:147
  61.8 9.9 %shard_map.102 = bf16[8,8,72,128]{3,2,1,0:T(8,128)(2,1)} custom-call(s32[4]{0:T(128)} %pad_add_fusion.1.info, s32[8]{0:T(128)} %lengths.9, bf16[4,8,64,128]{3,2,1,0:T(8,128)(2,1)} %collective-permute-done.5.refs_0_, bf16[4,8,64,128]{3,2,1,0:T(8,128)(2,1)} %collective-permute-done.6.refs_1_, bf16[8,512,1024]{2,1,0:T(8,128)(2,1)} %refs_1_.5, ...), custom_call_target="tpu_custom_call" | custom-call | flops 2147483648 | bytes 4194304 | tf_op jit(solution)/shard_map/pallas_call | solution.py:147
  71.6 1.2 collective-permute-start.8
  72.8 1.5 %collective-permute-start.7 = (bf16[64,72,128]{2,1,0:T(8,128)(2,1)}, bf16[64,72,128]{2,1,0:T(8,128)(2,1)}, u32[]{:S(2)}, u32[]{:S(2)}) collective-permute-start(bf16[64,72,128]{2,1,0:T(8,128)(2,1)} %bitcast.38), channel_id=1, source_target_pairs={{0,6},{2,0},{4,2},{6,4},{1,7},{3,1},{5,3},{7,5},{8,14},{10,8},{12,... | collective-permute-start | bytes 3538952 | tf_op jit(solution)/shard_map/ppermute | solution.py:295
  74.3 9.9 %shard_map.103 = (bf16[4,8,72,128]{3,2,1,0:T(8,128)(2,1)}, bf16[4,8,72,128]{3,2,1,0:T(8,128)(2,1)}) custom-call(s32[4]{0:T(128)} %pad_add_fusion.1.info, s32[8]{0:T(128)} %lengths.9, bf16[8,8,64,128]{3,2,1,0:T(8,128)(2,1)} %collective-permute-done.9.refs_0_, bf16[8,512,1024]{2,1,0:T(8,128)(2,1)} %refs_1_.5, ...), custom_call_target="tpu_custom_call" | custom-call | flops 2147483648 | bytes 4194304 | tf_op jit(solution)/shard_map/pallas_call | solution.py:147
  84.5 6.5 %shard_map.104 = bf16[8,8,72,128]{3,2,1,0:T(8,128)(2,1)} custom-call(s32[4]{0:T(128)} %pad_add_fusion.1.info, s32[8]{0:T(128)} %lengths.9, bf16[8,8,64,128]{3,2,1,0:T(8,128)(2,1)} %bitcast.36, bf16[8,512,1024]{2,1,0:T(8,128)(2,1)} %refs_1_.5, bf16[4,512,1024]{2,1,0:T(8,128)(2,1)} %collective-permute-done.1.refs_2_.refs_3_, ...), custom_call_target="tpu_custom_call", output_to_operand_aliasing={{}: (7, {})} | custom-call | flops 1073741824 | bytes 2097152 | tf_op jit(solution)/shard_map/pallas_call | solution.py:147
  91.0 5.9 %collective-permute-done.10.refs_2_ = bf16[32,72,128]{2,1,0:T(8,128)(2,1)S(1)} collective-permute-done((bf16[32,72,128]{2,1,0:T(8,128)(2,1)}, bf16[32,72,128]{2,1,0:T(8,128)(2,1)S(1)}, u32[]{:S(2)}, u32[]{:S(2)}) %collective-permute-start.10) | collective-permute-done | bytes 589856 | tf_op jit(solution)/shard_map/ppermute | solution.py:295
  97.7 4.3 %shard_map.105 = bf16[64,72,128]{2,1,0:T(8,128)(2,1)} custom-call(bf16[64,72,128]{2,1,0:T(8,128)(2,1)} %collective-permute-done.7.refs_0_, bf16[64,72,128]{2,1,0:T(8,128)(2,1)} %collective-permute-done.8.refs_1_, bf16[32,72,128]{2,1,0:T(8,128)(2,1)S(1)} %collective-permute-done.10.refs_2_, bf16[32,72,128]{2,1,0:T(8,128)(2,1)S(1)} %collective-permute-done.11.refs_3_, ...), custom_call_target="tpu_custom_call" | custom-call | flops 4718592 | bytes 5898240 | tf_op jit(solution)/shard_map/pallas_call | solution.py:232
  102.0 22.6 %all-to-all-start.1 = ((bf16[64,72,128]{2,1,0:T(8,128)(2,1)}), bf16[64,72,128]{2,1,0:T(8,128)(2,1)S(1)}, u32[]{:S(2)}, u32[]{:S(2)}) async-start(bf16[64,72,128]{2,1,0:T(8,128)(2,1)} %shard_map.105), calls=%async_computation.1 | async-start | bytes 2359296 | tf_op jit(solution)/shard_map/all_to_all | solution.py:370
  124.6 2.4 %collective-permute-start.12 = (s32[4,8]{1,0:T(4,128)S(1)}, s32[4,8]{1,0:T(4,128)S(1)}, u32[]{:S(2)}, u32[]{:S(2)}) collective-permute-start(s32[4,8]{1,0:T(4,128)S(1)} %get-tuple-element.42), channel_id=1, source_target_pairs={{0,8},{8,0},{1,9},{9,1},{2,10},{10,2},{3,11},{11,3},{4,12},{12,4},... | collective-permute-start | bytes 392 | tf_op jit(solution)/shard_map/ppermute | solution.py:318
  128.9 1.1 copy.14.value_ref
  130.0 1.2 fusion.2
  131.5 9.9 %all-to-all-done.1.x_ref = bf16[64,72,128]{2,1,0:T(8,128)(2,1)S(1)} async-done(((bf16[64,72,128]{2,1,0:T(8,128)(2,1)}), bf16[64,72,128]{2,1,0:T(8,128)(2,1)S(1)}, u32[]{:S(2)}, u32[]{:S(2)}) %all-to-all-start.1) | async-done | bytes 1179680 | tf_op jit(solution)/shard_map/all_to_all | solution.py:370
  142.0 3.9 %collective-permute-start.13 = (bf16[4,4,8,128]{3,2,1,0:T(8,128)(2,1)S(1)}, bf16[4,4,8,128]{3,2,1,0:T(8,128)(2,1)S(1)}, u32[]{:S(2)}, u32[]{:S(2)}) collective-permute-start(bf16[4,4,8,128]{3,2,1,0:T(8,128)(2,1)S(1)} %get-tuple-element.46), channel_id=1, source_target_pairs={{0,8},{8,0},{1,9},{9,1},{2,10},{10,2},{3,11},{11,3},{4,12},{12,4},... | collective-permute-start | bytes 98312 | tf_op jit(solution)/shard_map/ppermute | solution.py:389
  (48 shorter events, 9.9 us)
Async XLA Ops:
  0.0 127.9 %copy-start = (bf16[1024,1024]{1,0:T(8,128)(2,1)S(1)}, bf16[1024,1024]{1,0:T(8,128)(2,1)}, u32[]{:S(2)}) copy-start(bf16[1024,1024]{1,0:T(8,128)(2,1)} %param.14) | copy-start | bytes 6291460
  1.7 4.4 %copy-start.3 = (pred[64]{0:T(512)(128)(4,1)S(1)}, pred[64]{0:T(512)(128)(4,1)}, u32[]{:S(2)}) copy-start(pred[64]{0:T(512)(128)(4,1)} %constant.60) | copy-start | bytes 196
  1.7 4.5 %copy-start.4 = (pred[64]{0:T(512)(128)(4,1)S(1)}, pred[64]{0:T(512)(128)(4,1)}, u32[]{:S(2)}) copy-start(pred[64]{0:T(512)(128)(4,1)} %constant.61) | copy-start | bytes 196
  1.7 4.5 %copy-start.5 = (pred[64]{0:T(512)(128)(4,1)S(1)}, pred[64]{0:T(512)(128)(4,1)}, u32[]{:S(2)}) copy-start(pred[64]{0:T(512)(128)(4,1)} %constant.62) | copy-start | bytes 196
  1.7 4.4 %collective-permute-start = (bf16[4,4,8,128]{3,2,1,0:T(8,128)(2,1)S(1)}, bf16[4,4,8,128]{3,2,1,0:T(8,128)(2,1)S(1)}, u32[]{:S(2)}, u32[]{:S(2)}) collective-permute-start(bf16[4,4,8,128]{3,2,1,0:T(8,128)(2,1)S(1)} %get-tuple-element.24), channel_id=1, source_target_pairs={{0,8},{8,0},{1,9},{9,1},{2,10},{10,2},{3,11},{11,3},{4,12},{12,4},... | collective-permute-start | bytes 98312 | tf_op jit(solution)/shard_map/ppermute | solution.py:317
  3.2 4.6 %copy-start.1 = (bf16[8,512,1024]{2,1,0:T(8,128)(2,1)S(1)}, bf16[8,512,1024]{2,1,0:T(8,128)(2,1)}, u32[]{:S(2)}) copy-start(bf16[8,512,1024]{2,1,0:T(8,128)(2,1)} %refs_3_.5) | copy-start | bytes 25165828
  6.0 30.1 %collective-permute-start.1 = (bf16[4,512,1024]{2,1,0:T(8,128)(2,1)S(1)}, bf16[4,512,1024]{2,1,0:T(8,128)(2,1)}, u32[]{:S(2)}, u32[]{:S(2)}) collective-permute-start(bf16[4,512,1024]{2,1,0:T(8,128)(2,1)S(1)} %constant_dynamic-slice_fusion.2), channel_id=1, source_target_pairs={{0,8},{8,0},{1,9},{9,1},{2,10},{10,2},{3,11},{11,3},{4,12},{12,4},... | collective-permute-start | bytes 12582920 | tf_op jit(solution)/shard_map/ppermute | solution.py:337
  8.3 27.9 %collective-permute-start.2 = (bf16[4,512,1024]{2,1,0:T(8,128)(2,1)S(1)}, bf16[4,512,1024]{2,1,0:T(8,128)(2,1)}, u32[]{:S(2)}, u32[]{:S(2)}) collective-permute-start(bf16[4,512,1024]{2,1,0:T(8,128)(2,1)S(1)} %constant_dynamic-slice_fusion.1), channel_id=1, source_target_pairs={{0,8},{8,0},{1,9},{9,1},{2,10},{10,2},{3,11},{11,3},{4,12},{12,4},... | collective-permute-start | bytes 12582920 | tf_op jit(solution)/shard_map/ppermute | solution.py:338
  36.2 8.4 %copy-start.2 = (bf16[64,64,128]{2,1,0:T(8,128)(2,1)}, bf16[64,64,128]{2,1,0:T(8,128)(2,1)S(1)}, u32[]{:S(2)}) copy-start(bf16[64,64,128]{2,1,0:T(8,128)(2,1)S(1)} %all_to_all.10) | copy-start | bytes 3145732
  37.4 13.8 %collective-permute-start.3 = (bf16[4,8,64,128]{3,2,1,0:T(8,128)(2,1)}, bf16[4,8,64,128]{3,2,1,0:T(8,128)(2,1)}, u32[]{:S(2)}, u32[]{:S(2)}) collective-permute-start(bf16[4,8,64,128]{3,2,1,0:T(8,128)(2,1)} %get-tuple-element.44), channel_id=1, source_target_pairs={{0,2},{2,4},{4,6},{6,0},{1,3},{3,5},{5,7},{7,1},{8,10},{10,12},{12... | collective-permute-start | bytes 1572872 | tf_op jit(solution)/shard_map/ppermute | solution.py:295
  38.3 12.9 %collective-permute-start.4 = (bf16[4,8,64,128]{3,2,1,0:T(8,128)(2,1)}, bf16[4,8,64,128]{3,2,1,0:T(8,128)(2,1)}, u32[]{:S(2)}, u32[]{:S(2)}) collective-permute-start(bf16[4,8,64,128]{3,2,1,0:T(8,128)(2,1)} %get-tuple-element.43), channel_id=1, source_target_pairs={{0,16},{16,32},{32,48},{48,0},{1,17},{17,33},{33,49},{49,1},{2,18}... | collective-permute-start | bytes 1572872 | tf_op jit(solution)/shard_map/ppermute | solution.py:295
  38.9 12.3 %collective-permute-start.5 = (bf16[4,8,64,128]{3,2,1,0:T(8,128)(2,1)}, bf16[4,8,64,128]{3,2,1,0:T(8,128)(2,1)}, u32[]{:S(2)}, u32[]{:S(2)}) collective-permute-start(bf16[4,8,64,128]{3,2,1,0:T(8,128)(2,1)} %get-tuple-element.44), channel_id=1, source_target_pairs={{0,6},{2,0},{4,2},{6,4},{1,7},{3,1},{5,3},{7,5},{8,14},{10,8},{12,... | collective-permute-start | bytes 1572872 | tf_op jit(solution)/shard_map/ppermute | solution.py:295
  41.0 10.8 %collective-permute-start.6 = (bf16[4,8,64,128]{3,2,1,0:T(8,128)(2,1)}, bf16[4,8,64,128]{3,2,1,0:T(8,128)(2,1)}, u32[]{:S(2)}, u32[]{:S(2)}) collective-permute-start(bf16[4,8,64,128]{3,2,1,0:T(8,128)(2,1)} %get-tuple-element.43), channel_id=1, source_target_pairs={{0,48},{16,0},{32,16},{48,32},{1,49},{17,1},{33,17},{49,33},{2,50}... | collective-permute-start | bytes 1572872 | tf_op jit(solution)/shard_map/ppermute | solution.py:295
  42.8 31.5 %collective-permute-start.9 = (bf16[8,8,64,128]{3,2,1,0:T(8,128)(2,1)S(1)}, bf16[8,8,64,128]{3,2,1,0:T(8,128)(2,1)}, u32[]{:S(2)}, u32[]{:S(2)}) collective-permute-start(bf16[8,8,64,128]{3,2,1,0:T(8,128)(2,1)S(1)} %bitcast.34), channel_id=1, source_target_pairs={{0,1},{64,65},{1,0},{65,64},{2,3},{66,67},{3,2},{67,66},{4,5},{68,... | collective-permute-start | bytes 3145736 | tf_op jit(solution)/shard_map/ppermute | solution.py:293
  71.6 25.2 %collective-permute-start.8 = (bf16[64,72,128]{2,1,0:T(8,128)(2,1)}, bf16[64,72,128]{2,1,0:T(8,128)(2,1)}, u32[]{:S(2)}, u32[]{:S(2)}) collective-permute-start(bf16[64,72,128]{2,1,0:T(8,128)(2,1)} %bitcast.39), channel_id=1, source_target_pairs={{0,16},{16,32},{32,48},{48,0},{1,17},{17,33},{33,49},{49,1},{2,18}... | collective-permute-start | bytes 3538952 | tf_op jit(solution)/shard_map/ppermute | solution.py:295
  72.8 24.8 %collective-permute-start.7 = (bf16[64,72,128]{2,1,0:T(8,128)(2,1)}, bf16[64,72,128]{2,1,0:T(8,128)(2,1)}, u32[]{:S(2)}, u32[]{:S(2)}) collective-permute-start(bf16[64,72,128]{2,1,0:T(8,128)(2,1)} %bitcast.38), channel_id=1, source_target_pairs={{0,6},{2,0},{4,2},{6,4},{1,7},{3,1},{5,3},{7,5},{8,14},{10,8},{12,... | collective-permute-start | bytes 3538952 | tf_op jit(solution)/shard_map/ppermute | solution.py:295
  84.2 12.7 %collective-permute-start.10 = (bf16[32,72,128]{2,1,0:T(8,128)(2,1)}, bf16[32,72,128]{2,1,0:T(8,128)(2,1)S(1)}, u32[]{:S(2)}, u32[]{:S(2)}) collective-permute-start(bf16[32,72,128]{2,1,0:T(8,128)(2,1)} %bitcast.48), channel_id=1, source_target_pairs={{0,4},{2,6},{4,0},{6,2},{1,5},{3,7},{5,1},{7,3},{8,12},{10,14},{12... | collective-permute-start | bytes 1769480 | tf_op jit(solution)/shard_map/ppermute | solution.py:295
  84.2 12.7 %collective-permute-start.11 = (bf16[32,72,128]{2,1,0:T(8,128)(2,1)}, bf16[32,72,128]{2,1,0:T(8,128)(2,1)S(1)}, u32[]{:S(2)}, u32[]{:S(2)}) collective-permute-start(bf16[32,72,128]{2,1,0:T(8,128)(2,1)} %bitcast.47), channel_id=1, source_target_pairs={{0,1},{64,65},{1,0},{65,64},{2,3},{66,67},{3,2},{67,66},{4,5},{68,... | collective-permute-start | bytes 1769480 | tf_op jit(solution)/shard_map/ppermute | solution.py:293
  102.0 39.5 %all-to-all-start.1 = ((bf16[64,72,128]{2,1,0:T(8,128)(2,1)}), bf16[64,72,128]{2,1,0:T(8,128)(2,1)S(1)}, u32[]{:S(2)}, u32[]{:S(2)}) async-start(bf16[64,72,128]{2,1,0:T(8,128)(2,1)} %shard_map.105), calls=%async_computation.1 | async-start | bytes 2359296 | tf_op jit(solution)/shard_map/all_to_all | solution.py:370
  124.6 3.2 %collective-permute-start.12 = (s32[4,8]{1,0:T(4,128)S(1)}, s32[4,8]{1,0:T(4,128)S(1)}, u32[]{:S(2)}, u32[]{:S(2)}) collective-permute-start(s32[4,8]{1,0:T(4,128)S(1)} %get-tuple-element.42), channel_id=1, source_target_pairs={{0,8},{8,0},{1,9},{9,1},{2,10},{10,2},{3,11},{11,3},{4,12},{12,4},... | collective-permute-start | bytes 392 | tf_op jit(solution)/shard_map/ppermute | solution.py:318
  142.0 4.7 %collective-permute-start.13 = (bf16[4,4,8,128]{3,2,1,0:T(8,128)(2,1)S(1)}, bf16[4,4,8,128]{3,2,1,0:T(8,128)(2,1)S(1)}, u32[]{:S(2)}, u32[]{:S(2)}) collective-permute-start(bf16[4,4,8,128]{3,2,1,0:T(8,128)(2,1)S(1)} %get-tuple-element.46), channel_id=1, source_target_pairs={{0,8},{8,0},{1,9},{9,1},{2,10},{10,2},{3,11},{11,3},{4,12},{12,4},... | collective-permute-start | bytes 98312 | tf_op jit(solution)/shard_map/ppermute | solution.py:389
